TPU v7x, 256 devices: a whole 4x4x8 slice. The times are simulated.
256 devices in a mesh: section: 4 (over z_lo), tensor: 8 (over x, z_hi), dp: 8 (over y, core).
Axes of the slice: x: 4, y: 4, z: 8 (z_hi: 2, z_lo: 4; z = z_hi * 4 + z_lo), core: 2. Of those that a mesh axis runs over, the one named last changes fastest.
Arguments:
- hidden_in: bfloat16 [16, 64, 4096], P('dp', None, 'tensor'), may hold values from -6 to 6
- lengths: int32 [16], P('dp'), may hold values from 16 to 64
- gains: bfloat16 [4, 4096], P('section', 'tensor'), may hold values from 0.25 to 1.75
- w_query: bfloat16 [4, 4096, 4096], P('section', None, 'tensor'), may hold values from -0.09375 to 0.09375
- w_keyval: bfloat16 [4, 4096, 8, 256], P('section', None, 'tensor'), may hold values from -0.09375 to 0.09375
- w_out: bfloat16 [4, 4096, 4096], P('section', 'tensor'), may hold values from -0.09375 to 0.09375
- grad_out: bfloat16 [16, 64, 4096], P('dp', None, 'tensor'), may hold values from -6 to 6
Outputs:
- grad_query: float32 [4, 4096, 4096], P('section', 'dp', 'tensor')
- grad_keyval: float32 [4, 4096, 8, 256], P('section', 'dp', 'tensor')
- grad_outproj: float32 [4, 4096, 4096], P('section', 'tensor', 'dp')
- grad_gain: float32 [4, 4096], P('section', ('tensor', 'dp'))
Inputs may be any that keep to these rules, and one draw needn't show every extreme that they name: `lengths`: A row's keys at positions at or beyond its length are padding.
All inputs are finite; a program needn't handle non-finite values.
Results may differ from a plain program's by a relative error of at most 0.035.
Values may be sent and summed in bfloat16 or wider, within the bound.
No kernel may reach another device: no remote copies, remote signals or barrier semaphores. Data moves between devices by JAX's collectives and lax.ppermute only.
A program may use at most 128 MiB of HBM per device.

v0:
```python
import jax
import jax.numpy as jnp
from jax import lax
from jax.sharding import PartitionSpec as P

HEAD_DIM = 128


EPS = 1e-05
NEG = -1e30


def shifted(block, axis, distance):
    devices = range(lax.axis_size(axis))
    route = [(i - distance, i) for i in devices if i - distance in devices]
    return lax.ppermute(block, axis, route)


def features(operand):
    return lax.all_gather(operand, "tensor", axis=1, tiled=True)


def row_sum(operand):
    return lax.psum(operand, "tensor")


def head_total(operand):
    return lax.psum_scatter(operand, "tensor", scatter_dimension=1, tiled=True)


def neighbour(operand, offset):
    return shifted(operand, "section", offset)


def inner(former, latter):
    return lax.dot_general(
        former, latter, (((0,), (0,)), ((), ())), preferred_element_type=jnp.float32
    )


def outer_side(former, latter):
    return lax.dot_general(
        former, latter, (((1,), (1,)), ((), ())), preferred_element_type=jnp.float32
    )


def select_step(stacked, position):
    return lax.dynamic_index_in_dim(stacked, position, 0, keepdims=False)


def attend(queries, keyval, length):
    row_count = queries.shape[0]
    pair_count = keyval.shape[1] // (2 * HEAD_DIM)
    group_size = queries.shape[1] // (HEAD_DIM * pair_count)
    query_heads = queries.reshape(row_count, pair_count, group_size, HEAD_DIM)
    pairs = keyval.reshape(row_count, pair_count, 2, HEAD_DIM)
    scores = jnp.einsum(
        "ighd,jgd->ghij", query_heads, pairs[:, :, 0], preferred_element_type=jnp.float32
    ) * HEAD_DIM ** (-0.5)
    position = jnp.arange(row_count)
    allowed = (position[None, :] <= position[:, None]) & (position[None, :] < length)
    scores = jnp.where(allowed, scores, NEG)
    highest = jnp.max(scores, -1, keepdims=True)
    raised = jnp.exp(scores - highest)
    attn_weights = raised / jnp.sum(raised, -1, keepdims=True)
    head_mix = jnp.einsum(
        "ghij,jgd->ighd",
        attn_weights.astype(jnp.bfloat16),
        pairs[:, :, 1],
        preferred_element_type=jnp.float32,
    )
    return (head_mix.reshape(row_count, -1).astype(jnp.bfloat16), attn_weights)


def attend_back(queries, keyval, attn_weights, mix_grad):
    row_count = queries.shape[0]
    pair_count = keyval.shape[1] // (2 * HEAD_DIM)
    group_size = queries.shape[1] // (HEAD_DIM * pair_count)
    query_heads = queries.reshape(row_count, pair_count, group_size, HEAD_DIM)
    pairs = keyval.reshape(row_count, pair_count, 2, HEAD_DIM)
    grad_heads = mix_grad.reshape(row_count, pair_count, group_size, HEAD_DIM)
    value_grad = jnp.einsum(
        "ghij,ighd->jgd",
        attn_weights.astype(jnp.bfloat16),
        grad_heads,
        preferred_element_type=jnp.float32,
    ).astype(jnp.bfloat16)
    weight_grad = jnp.einsum(
        "ighd,jgd->ghij", grad_heads, pairs[:, :, 1], preferred_element_type=jnp.float32
    )
    score_grad = (
        attn_weights
        * (weight_grad - jnp.sum(weight_grad * attn_weights, -1, keepdims=True))
        * HEAD_DIM ** (-0.5)
    )
    score_grad = score_grad.astype(jnp.bfloat16)
    query_grad = (
        jnp.einsum("ghij,jgd->ighd", score_grad, pairs[:, :, 0], preferred_element_type=jnp.float32)
        .reshape(row_count, -1)
        .astype(jnp.bfloat16)
    )
    key_grad = jnp.einsum(
        "ghij,ighd->jgd", score_grad, query_heads, preferred_element_type=jnp.float32
    ).astype(jnp.bfloat16)
    return (query_grad, jnp.stack([key_grad, value_grad], 2).reshape(row_count, -1))


def window_rows(collected_items, first_step, micro_count):
    stacked = jnp.stack(collected_items)
    picked = lax.dynamic_slice_in_dim(stacked, first_step, micro_count, 0)
    return picked.reshape(micro_count * picked.shape[1], picked.shape[2])


def shards(hidden_in, lengths, gains, w_query, w_keyval, w_out, grad_out):
    sections = lax.axis_size("section")
    station = lax.axis_index("section")
    micro_count = hidden_in.shape[0]
    step_count = micro_count + sections - 1
    gain_row = gains[0]
    query_weight = w_query[0]
    model_width = query_weight.shape[0]
    pair_count = w_keyval.shape[2]
    pair_weight = w_keyval[0].reshape(model_width, -1)
    out_weight = w_out[0]
    incoming = jnp.zeros_like(hidden_in[0])
    kept_items = []
    for moment in range(step_count):
        slot_index = jnp.clip(moment - station, 0, micro_count - 1)
        own_rows = lax.dynamic_index_in_dim(hidden_in, slot_index, 0, keepdims=False)
        current = jnp.where(station == 0, own_rows, incoming)
        length = lax.dynamic_index_in_dim(lengths, slot_index, 0, keepdims=False)
        current_wide = current.astype(jnp.float32)
        scale_row = lax.rsqrt(row_sum(jnp.sum(current_wide * current_wide, -1)) / model_width + EPS)
        normed = features((current_wide * scale_row[:, None] * gain_row).astype(jnp.bfloat16))
        queries = jnp.dot(normed, query_weight, preferred_element_type=jnp.float32).astype(
            jnp.bfloat16
        )
        keyval = jnp.dot(normed, pair_weight, preferred_element_type=jnp.float32).astype(
            jnp.bfloat16
        )
        head_mix, attn_weights = attend(queries, keyval, length)
        branch = head_total(jnp.dot(head_mix, out_weight, preferred_element_type=jnp.float32))
        result = (current_wide + branch).astype(jnp.bfloat16)
        kept_items.append((current, scale_row, normed, queries, keyval, head_mix, attn_weights))
        if moment + 1 < step_count:
            incoming = neighbour(result, 1)
    past_input, past_scale, past_normed, past_queries, past_keyval, past_mix, past_weights = [
        jnp.stack(list(member_items)) for member_items in zip(*kept_items)
    ]
    incoming_grad = jnp.zeros_like(grad_out[0])
    gain_grad = jnp.zeros(gain_row.shape, jnp.float32)
    collected = []
    for moment in range(step_count):
        batch_offset = moment - (sections - 1 - station)
        is_valid = (batch_offset >= 0) & (batch_offset < micro_count)
        slot_index = jnp.clip(batch_offset, 0, micro_count - 1)
        forward_step = jnp.clip(batch_offset + station, 0, step_count - 1)
        own_grad = lax.dynamic_index_in_dim(grad_out, slot_index, 0, keepdims=False)
        current_grad = jnp.where(station == sections - 1, own_grad, incoming_grad)
        current = select_step(past_input, forward_step)
        scale_row = select_step(past_scale, forward_step)
        normed = select_step(past_normed, forward_step)
        queries = select_step(past_queries, forward_step)
        keyval = select_step(past_keyval, forward_step)
        head_mix = select_step(past_mix, forward_step)
        attn_weights = select_step(past_weights, forward_step)
        full_grad = features(current_grad)
        mix_grad = outer_side(full_grad, out_weight).astype(jnp.bfloat16)
        query_grad, pair_grad = attend_back(queries, keyval, attn_weights, mix_grad)
        normed_grad = head_total(
            outer_side(query_grad, query_weight) + outer_side(pair_grad, pair_weight)
        )
        current_wide = current.astype(jnp.float32)
        correction = row_sum(jnp.sum(normed_grad * gain_row * current_wide, -1))
        gain_step = jnp.sum(normed_grad * current_wide * scale_row[:, None], 0)
        gain_grad = gain_grad + jnp.where(is_valid, gain_step, 0.0)
        input_grad = (
            current_grad.astype(jnp.float32)
            + scale_row[:, None] * gain_row * normed_grad
            - current_wide * (scale_row**3 / model_width)[:, None] * correction[:, None]
        ).astype(jnp.bfloat16)
        collected.append((normed, query_grad, pair_grad, head_mix, full_grad))
        if moment + 1 < step_count:
            incoming_grad = neighbour(input_grad, -1)
    first_step = sections - 1 - station
    normed_rows, qgrad_rows, pgrad_rows, mixed_rows, outgrad_rows = [
        window_rows(list(member_items), first_step, micro_count) for member_items in zip(*collected)
    ]
    grad_terms = (
        inner(normed_rows, qgrad_rows),
        inner(normed_rows, pgrad_rows),
        inner(mixed_rows, outgrad_rows),
        gain_grad,
    )
    query_total, pair_total, output_total, gain_total = (
        lax.psum_scatter(grad_terms[0], "dp", scatter_dimension=0, tiled=True),
        lax.psum_scatter(grad_terms[1], "dp", scatter_dimension=0, tiled=True),
        lax.psum_scatter(grad_terms[2], "dp", scatter_dimension=1, tiled=True),
        lax.psum_scatter(grad_terms[3], "dp", scatter_dimension=0, tiled=True),
    )
    grad_query = query_total[None]
    grad_keyval = pair_total.reshape(1, pair_total.shape[0], pair_count, 2 * HEAD_DIM)
    grad_outproj = output_total[None]
    grad_gain = gain_total[None]
    return (grad_query, grad_keyval, grad_outproj, grad_gain)


def solution(mesh):
    in_specs = (
        P("dp", None, "tensor"),
        P("dp"),
        P("section", "tensor"),
        P("section", None, "tensor"),
        P("section", None, "tensor", None),
        P("section", "tensor", None),
        P("dp", None, "tensor"),
    )
    out_specs = (
        P("section", "dp", "tensor"),
        P("section", "dp", "tensor", None),
        P("section", "tensor", "dp"),
        P("section", ("tensor", "dp")),
    )
    return jax.shard_map(shards, mesh=mesh, in_specs=in_specs, out_specs=out_specs, check_vma=False)
```

profile of v0, /device:TPU:1, one launch (start us, length us, event | category | flops | bytes accessed | tf_op | source)
XLA Modules:
  0.0 1765.9 jit_solution(11593985656011356482)
XLA Ops:
  8.3 30.3 %psum.63 = f32[64]{0:T(128)S(1)} all-reduce(f32[64]{0:T(128)S(1)} %fusion.172), channel_id=1, replica_groups=mesh['section'=4,'tensor'=8,'dp'=8] {'tensor'}, use_global_device_ids=true, to_apply=%region_1.2 | all-reduce | flops 64 | bytes 512 | tf_op jit(solution)/shard_map/psum | solution.py:24
  40.8 40.0 %all_gather.30 = bf16[64,4096]{1,0:T(8,128)(2,1)S(1)} all-gather(bf16[64,512]{1,0:T(8,128)(2,1)S(1)} %fusion.174), channel_id=1, replica_groups=mesh['section'=4,'tensor'=8,'dp'=8] {'tensor'}, dimensions={1}, use_global_device_ids=true | all-gather | bytes 589824 | tf_op jit(solution)/shard_map/all_gather | solution.py:20
  81.9 3.7 constant_dynamic-update-slice_fusion.9
  87.5 4.1 fusion.16
  92.3 90.2 %reduce-scatter.13.cloned.1.call-done = f32[64,512]{1,0:T(8,128)} async-done(((f32[64,4096]{1,0:T(8,128)}), f32[64,512]{1,0:T(8,128)}) %reduce-scatter.13.cloned.1.call-update) | async-done | bytes 131088 | tf_op jit(solution)/shard_map/reduce_scatter | solution.py:28
  186.4 22.4 %psum.64 = f32[64]{0:T(128)S(1)} all-reduce(f32[64]{0:T(128)S(1)} %fusion.160), channel_id=1, replica_groups=mesh['section'=4,'tensor'=8,'dp'=8] {'tensor'}, use_global_device_ids=true, to_apply=%region_6.7 | all-reduce | flops 64 | bytes 512 | tf_op jit(solution)/shard_map/psum | solution.py:24
  209.3 41.1 %all_gather.31 = bf16[64,4096]{1,0:T(8,128)(2,1)S(1)} all-gather(bf16[64,512]{1,0:T(8,128)(2,1)S(1)} %fusion.162), channel_id=1, replica_groups=mesh['section'=4,'tensor'=8,'dp'=8] {'tensor'}, dimensions={1}, use_global_device_ids=true | all-gather | bytes 589824 | tf_op jit(solution)/shard_map/all_gather | solution.py:20
  250.4 3.7 constant_dynamic-update-slice_fusion.8
  257.5 4.0 fusion.14
  262.7 94.9 %reduce-scatter.15.cloned.1.call-done = f32[64,512]{1,0:T(8,128)} async-done(((f32[64,4096]{1,0:T(8,128)}), f32[64,512]{1,0:T(8,128)}) %reduce-scatter.15.cloned.1.call-update) | async-done | bytes 131088 | tf_op jit(solution)/shard_map/reduce_scatter | solution.py:28
  362.1 22.3 %psum.65 = f32[64]{0:T(128)S(1)} all-reduce(f32[64]{0:T(128)S(1)} %fusion.164), channel_id=1, replica_groups=mesh['section'=4,'tensor'=8,'dp'=8] {'tensor'}, use_global_device_ids=true, to_apply=%region_11.12 | all-reduce | flops 64 | bytes 512 | tf_op jit(solution)/shard_map/psum | solution.py:24
  385.0 41.1 %all_gather.32 = bf16[64,4096]{1,0:T(8,128)(2,1)S(1)} all-gather(bf16[64,512]{1,0:T(8,128)(2,1)S(1)} %fusion.166), channel_id=1, replica_groups=mesh['section'=4,'tensor'=8,'dp'=8] {'tensor'}, dimensions={1}, use_global_device_ids=true | all-gather | bytes 589824 | tf_op jit(solution)/shard_map/all_gather | solution.py:20
  426.2 3.9 constant_dynamic-update-slice_fusion.7
  433.5 4.0 fusion.12
  438.7 94.4 %reduce-scatter.17.cloned.1.call-done = f32[64,512]{1,0:T(8,128)} async-done(((f32[64,4096]{1,0:T(8,128)}), f32[64,512]{1,0:T(8,128)}) %reduce-scatter.17.cloned.1.call-update) | async-done | bytes 131088 | tf_op jit(solution)/shard_map/reduce_scatter | solution.py:28
  537.6 22.3 %psum.66 = f32[64]{0:T(128)S(1)} all-reduce(f32[64]{0:T(128)S(1)} %fusion.168), channel_id=1, replica_groups=mesh['section'=4,'tensor'=8,'dp'=8] {'tensor'}, use_global_device_ids=true, to_apply=%region_16.17 | all-reduce | flops 64 | bytes 512 | tf_op jit(solution)/shard_map/psum | solution.py:24
  560.6 41.2 %all_gather.33 = bf16[64,4096]{1,0:T(8,128)(2,1)S(1)} all-gather(bf16[64,512]{1,0:T(8,128)(2,1)S(1)} %fusion.170), channel_id=1, replica_groups=mesh['section'=4,'tensor'=8,'dp'=8] {'tensor'}, dimensions={1}, use_global_device_ids=true | all-gather | bytes 589824 | tf_op jit(solution)/shard_map/all_gather | solution.py:20
  601.8 3.9 constant_dynamic-update-slice_fusion.6
  609.1 4.0 fusion.10
  614.0 39.4 %all-gather = bf16[1,64,4096]{2,1,0:T(8,128)(2,1)S(1)} all-gather(bf16[1,64,512]{2,1,0:T(8,128)(2,1)S(1)} %dynamic-slice_select_fusion), channel_id=2, replica_groups=mesh['section'=4,'tensor'=8,'dp'=8] {'tensor'}, dimensions={2}, use_global_device_ids=true | all-gather | bytes 589824 | tf_op jit(solution)/shard_map/all_gather | solution.py:20
  655.0 4.3 fusion.115
  660.7 50.7 %reduce-scatter.19.cloned.1.call-done = f32[64,512]{1,0:T(8,128)} async-done(((f32[64,4096]{1,0:T(8,128)}), f32[64,512]{1,0:T(8,128)}) %reduce-scatter.19.cloned.1.call-update) | async-done | bytes 131088 | tf_op jit(solution)/shard_map/reduce_scatter | solution.py:28
  716.0 22.3 %psum.67 = f32[64]{0:T(128)S(1)} all-reduce(f32[64]{0:T(128)S(1)} %fusion.157), channel_id=1, replica_groups=mesh['section'=4,'tensor'=8,'dp'=8] {'tensor'}, use_global_device_ids=true, to_apply=%region_21.22 | all-reduce | flops 64 | bytes 512 | tf_op jit(solution)/shard_map/psum | solution.py:24
  738.9 41.2 %all_gather.34 = bf16[64,4096]{1,0:T(8,128)(2,1)S(1)} all-gather(bf16[64,512]{1,0:T(8,128)(2,1)S(1)} %fusion.159), channel_id=1, replica_groups=mesh['section'=4,'tensor'=8,'dp'=8] {'tensor'}, dimensions={1}, use_global_device_ids=true | all-gather | bytes 589824 | tf_op jit(solution)/shard_map/all_gather | solution.py:20
  780.1 3.8 constant_dynamic-update-slice_fusion.5
  791.1 1.8 constant_dynamic-slice_fusion
  794.4 3.6 fusion.26
  798.0 1.7 convolution_add_fusion.4
  801.1 94.6 %reduce-scatter.21.cloned.1.call-done = f32[64,512]{1,0:T(8,128)} async-done(((f32[64,4096]{1,0:T(8,128)}), f32[64,512]{1,0:T(8,128)}) %reduce-scatter.21.cloned.1.call-update) | async-done | bytes 131088 | tf_op jit(solution)/shard_map/reduce_scatter | solution.py:28
  897.3 21.2 %psum.68 = f32[64]{0:T(128)S(1)} all-reduce(f32[64]{0:T(128)S(1)} %get-tuple-element.17), channel_id=1, replica_groups=mesh['section'=4,'tensor'=8,'dp'=8] {'tensor'}, use_global_device_ids=true, to_apply=%region_27.28 | all-reduce | flops 64 | bytes 512 | tf_op jit(solution)/shard_map/psum | solution.py:24
  923.6 1.9 collective-permute-done.4
  926.3 42.4 %all_gather.36 = bf16[64,4096]{1,0:T(8,128)(2,1)S(1)} all-gather(bf16[64,512]{1,0:T(8,128)(2,1)S(1)} %bitcast_select_fusion.3), channel_id=1, replica_groups=mesh['section'=4,'tensor'=8,'dp'=8] {'tensor'}, dimensions={1}, use_global_device_ids=true | all-gather | bytes 589824 | tf_op jit(solution)/shard_map/all_gather | solution.py:20
  968.7 3.8 fusion.112
  980.9 92.8 %reduce-scatter.23.cloned.1.call-done = f32[64,512]{1,0:T(8,128)} async-done(((f32[64,4096]{1,0:T(8,128)}), f32[64,512]{1,0:T(8,128)}) %reduce-scatter.23.cloned.1.call-update) | async-done | bytes 131088 | tf_op jit(solution)/shard_map/reduce_scatter | solution.py:28
  1075.3 21.9 %psum.69 = f32[64]{0:T(128)} all-reduce(f32[64]{0:T(128)} %get-tuple-element.19), channel_id=1, replica_groups=mesh['section'=4,'tensor'=8,'dp'=8] {'tensor'}, use_global_device_ids=true, to_apply=%region_31.32 | all-reduce | flops 64 | bytes 512 | tf_op jit(solution)/shard_map/psum | solution.py:24
  1105.0 41.4 %all_gather.37 = bf16[64,4096]{1,0:T(8,128)(2,1)S(1)} all-gather(bf16[64,512]{1,0:T(8,128)(2,1)S(1)} %bitcast_select_fusion.2), channel_id=1, replica_groups=mesh['section'=4,'tensor'=8,'dp'=8] {'tensor'}, dimensions={1}, use_global_device_ids=true | all-gather | bytes 589824 | tf_op jit(solution)/shard_map/all_gather | solution.py:20
  1146.4 3.8 fusion.109
  1155.4 1.7 convolution_add_fusion.2
  1158.9 1.9 bitcast_dynamic-update-slice_fusion.6
  1161.5 91.1 %reduce-scatter.25.cloned.1.call-done = f32[64,512]{1,0:T(8,128)} async-done(((f32[64,4096]{1,0:T(8,128)}), f32[64,512]{1,0:T(8,128)}) %reduce-scatter.25.cloned.1.call-update) | async-done | bytes 131088 | tf_op jit(solution)/shard_map/reduce_scatter | solution.py:28
  1254.2 21.1 %psum.70 = f32[64]{0:T(128)S(1)} all-reduce(f32[64]{0:T(128)S(1)} %get-tuple-element.21), channel_id=1, replica_groups=mesh['section'=4,'tensor'=8,'dp'=8] {'tensor'}, use_global_device_ids=true, to_apply=%region_35.36 | all-reduce | flops 64 | bytes 512 | tf_op jit(solution)/shard_map/psum | solution.py:24
  1277.7 3.6 collective-permute-done.6
  1281.3 43.0 %all_gather.38 = bf16[64,4096]{1,0:T(8,128)(2,1)S(1)} all-gather(bf16[64,512]{1,0:T(8,128)(2,1)S(1)} %bitcast_select_fusion.1), channel_id=1, replica_groups=mesh['section'=4,'tensor'=8,'dp'=8] {'tensor'}, dimensions={1}, use_global_device_ids=true | all-gather | bytes 589824 | tf_op jit(solution)/shard_map/all_gather | solution.py:20
  1324.3 3.8 fusion.106
  1337.6 1.9 dynamic-slice_dynamic-update-slice_fusion.4
  1339.5 88.9 %reduce-scatter.27.cloned.1.call-done = f32[64,512]{1,0:T(8,128)} async-done(((f32[64,4096]{1,0:T(8,128)}), f32[64,512]{1,0:T(8,128)}) %reduce-scatter.27.cloned.1.call-update) | async-done | bytes 131088 | tf_op jit(solution)/shard_map/reduce_scatter | solution.py:28
  1429.9 21.2 %psum.71 = f32[64]{0:T(128)S(1)} all-reduce(f32[64]{0:T(128)S(1)} %get-tuple-element.23), channel_id=1, replica_groups=mesh['section'=4,'tensor'=8,'dp'=8] {'tensor'}, use_global_device_ids=true, to_apply=%region_39.40 | all-reduce | flops 64 | bytes 512 | tf_op jit(solution)/shard_map/psum | solution.py:24
  1453.6 3.6 collective-permute-done.7
  1457.2 42.3 %all_gather.39 = bf16[64,4096]{1,0:T(8,128)(2,1)S(1)} all-gather(bf16[64,512]{1,0:T(8,128)(2,1)S(1)} %bitcast_select_fusion), channel_id=1, replica_groups=mesh['section'=4,'tensor'=8,'dp'=8] {'tensor'}, dimensions={1}, use_global_device_ids=true | all-gather | bytes 589824 | tf_op jit(solution)/shard_map/all_gather | solution.py:20
  1499.5 3.8 fusion.103
  1508.4 1.7 convolution_add_fusion
  1510.2 1.9 dynamic-slice_dynamic-update-slice_fusion.3
  1512.2 1.9 dynamic-slice_dynamic-update-slice_fusion.2
  1514.0 1.9 dynamic-slice_dynamic-update-slice_fusion.1
  1515.9 1.9 dynamic-slice_dynamic-update-slice_fusion
  1518.0 3.9 convolution_bitcast_fusion.2
  1541.4 5.8 convolution_bitcast_fusion
  1548.3 5.7 convolution_bitcast_fusion.1
  1555.9 48.2 %reduce-scatter.35.cloned.1.call-done = f32[64,512]{1,0:T(8,128)} async-done(((f32[64,4096]{1,0:T(8,128)}), f32[64,512]{1,0:T(8,128)}) %reduce-scatter.35.cloned.1.call-update) | async-done | bytes 131088 | tf_op jit(solution)/shard_map/reduce_scatter | solution.py:28
  1605.1 13.9 all-reduce
  1619.7 22.0 %reduce-scatter.31.cloned.1.call-done = f32[512,256]{1,0:T(8,128)} async-done(((f32[4096,256]{1,0:T(8,128)}), f32[512,256]{1,0:T(8,128)}) %reduce-scatter.31.cloned.1.call-update) | async-done | bytes 524304 | tf_op jit(solution)/shard_map/reduce_scatter | solution.py:197
  1641.7 2.4 copy.206
  1644.0 57.3 %reduce-scatter.33.cloned.1.call-done = f32[512,512]{1,0:T(8,128)} async-done(((f32[512,4096]{1,0:T(8,128)}), f32[512,512]{1,0:T(8,128)}) %reduce-scatter.33.cloned.1.call-update) | async-done | bytes 1048592 | tf_op jit(solution)/shard_map/reduce_scatter | solution.py:198
  1701.3 57.8 %reduce-scatter.29.cloned.1.call-done = f32[512,512]{1,0:T(8,128)} async-done(((f32[4096,512]{1,0:T(8,128)}), f32[512,512]{1,0:T(8,128)}) %reduce-scatter.29.cloned.1.call-update) | async-done | bytes 1048592 | tf_op jit(solution)/shard_map/reduce_scatter | solution.py:196
  (411 shorter events, 131.6 us)
Async XLA Ops:
  7.2 73.6 %copy-start = (bf16[1,4096,1,256]{3,1,2,0:T(8,128)(2,1)S(1)}, bf16[1,4096,1,256]{3,1,2,0:T(8,128)(2,1)}, u32[]{:S(2)}) copy-start(bf16[1,4096,1,256]{3,1,2,0:T(8,128)(2,1)} %param.11) | copy-start | bytes 6291460
  7.2 175.3 %reduce-scatter.13.cloned.1.call-start = ((), (), s32[]{:S(2)}) async-start(), calls=%async_computation.12 | async-start | bytes 1179648 | tf_op jit(solution)/shard_map/reduce_scatter | solution.py:28
  87.5 95.0 %copy-start.20 = (bf16[2,64,512]{2,1,0:T(8,128)(2,1)S(1)}, bf16[2,64,512]{2,1,0:T(8,128)(2,1)}, u32[]{:S(2)}) copy-start(bf16[2,64,512]{2,1,0:T(8,128)(2,1)} %param.7) | copy-start | bytes 393220
  91.5 266.0 %reduce-scatter.15.cloned.1.call-start = ((), (), s32[]{:S(2)}) async-start(), calls=%async_computation.13 | async-start | bytes 1179648 | tf_op jit(solution)/shard_map/reduce_scatter | solution.py:28
  183.4 2.8 collective-permute-start
  186.2 23.0 %copy-start.21 = (bf16[5,64,512]{2,1,0:T(8,128)(2,1)}, bf16[5,64,512]{2,1,0:T(8,128)(2,1)S(1)}, u32[]{:S(2)}) copy-start(bf16[5,64,512]{2,1,0:T(8,128)(2,1)S(1)} %get-tuple-element.38) | copy-start | bytes 983044
  186.2 67.9 %copy-start.34 = (bf16[64,512]{1,0:T(8,128)(2,1)}, bf16[64,512]{1,0:T(8,128)(2,1)S(1)}, u32[]{:S(2)}) copy-start(bf16[64,512]{1,0:T(8,128)(2,1)S(1)} %get-tuple-element.39) | copy-start | bytes 196612
  261.5 271.6 %reduce-scatter.17.cloned.1.call-start = ((), (), s32[]{:S(2)}) async-start(), calls=%async_computation.14 | async-start | bytes 1179648 | tf_op jit(solution)/shard_map/reduce_scatter | solution.py:28
  358.5 2.8 collective-permute-start.1
  361.9 68.1 %copy-start.35 = (bf16[64,512]{1,0:T(8,128)(2,1)}, bf16[64,512]{1,0:T(8,128)(2,1)S(1)}, u32[]{:S(2)}) copy-start(bf16[64,512]{1,0:T(8,128)(2,1)S(1)} %get-tuple-element.37) | copy-start | bytes 196612
  437.5 273.9 %reduce-scatter.19.cloned.1.call-start = ((), (), s32[]{:S(2)}) async-start(), calls=%async_computation.15 | async-start | bytes 1179648 | tf_op jit(solution)/shard_map/reduce_scatter | solution.py:28
  534.1 2.8 collective-permute-start.2
  537.5 68.1 %copy-start.33 = (bf16[64,512]{1,0:T(8,128)(2,1)}, bf16[64,512]{1,0:T(8,128)(2,1)S(1)}, u32[]{:S(2)}) copy-start(bf16[64,512]{1,0:T(8,128)(2,1)S(1)} %get-tuple-element.35) | copy-start | bytes 196612
  613.2 282.5 %reduce-scatter.21.cloned.1.call-start = ((), (), s32[]{:S(2)}) async-start(), calls=%async_computation.16 | async-start | bytes 1179648 | tf_op jit(solution)/shard_map/reduce_scatter | solution.py:28
  653.3 6.6 copy-start.10
  653.3 5.9 copy-start.69
  653.3 5.9 copy-start.77
  653.3 6.6 copy-start.30
  653.4 6.6 copy-start.71
  653.4 6.6 copy-start.79
  655.0 58.8 %copy-start.32 = (f32[1,4,64,64]{2,3,1,0:T(8,128)S(1)}, f32[1,4,64,64]{2,3,1,0:T(8,128)}, u32[]{:S(2)}) copy-start(f32[1,4,64,64]{2,3,1,0:T(8,128)} %copy-done.31) | copy-start | bytes 196612
  655.0 58.8 %copy-start.73 = (f32[4,64]{1,0:T(4,128)S(1)}, f32[4,64]{1,0:T(4,128)}, u32[]{:S(2)}) copy-start(f32[4,64]{1,0:T(4,128)} %copy-done.72) | copy-start | bytes 3076
  712.3 2.9 collective-permute-start.3
  798.0 97.7 %copy-start.22 = (bf16[5,64,512]{2,1,0:T(8,128)(2,1)S(1)}, bf16[5,64,512]{2,1,0:T(8,128)(2,1)}, u32[]{:S(2)}) copy-start(bf16[5,64,512]{2,1,0:T(8,128)(2,1)} %get-tuple-element.32) | copy-start | bytes 983044
  799.8 273.9 %reduce-scatter.23.cloned.1.call-start = ((), (), s32[]{:S(2)}) async-start(), calls=%async_computation.17 | async-start | bytes 1179648 | tf_op jit(solution)/shard_map/reduce_scatter | solution.py:28
  920.1 5.3 collective-permute-start.4
  926.3 47.4 %copy-start.66 = (bf16[64,1,1,128]{3,2,0,1:T(2,128)(2,1)S(1)}, bf16[64,1,1,128]{3,2,0,1:T(2,128)(2,1)}, u32[]{:S(2)}) copy-start(bf16[64,1,1,128]{3,2,0,1:T(2,128)(2,1)} %get-tuple-element.59) | copy-start | bytes 49156
  968.7 6.1 copy-start.12
  968.7 7.0 copy-start.62
  968.7 7.3 copy-start.64
  968.7 7.6 copy-start.1
  979.5 273.2 %reduce-scatter.25.cloned.1.call-start = ((), (), s32[]{:S(2)}) async-start(), calls=%async_computation.18 | async-start | bytes 1179648 | tf_op jit(solution)/shard_map/reduce_scatter | solution.py:28
  1098.8 5.3 collective-permute-start.5
  1105.0 46.3 %copy-start.67 = (bf16[64,1,1,128]{3,2,0,1:T(2,128)(2,1)S(1)}, bf16[64,1,1,128]{3,2,0,1:T(2,128)(2,1)}, u32[]{:S(2)}) copy-start(bf16[64,1,1,128]{3,2,0,1:T(2,128)(2,1)} %get-tuple-element.57) | copy-start | bytes 49156
  1146.4 6.1 copy-start.14
  1146.4 7.0 copy-start.63
  1146.4 7.3 copy-start.65
  1146.4 7.6 copy-start.2
  1157.2 271.2 %reduce-scatter.27.cloned.1.call-start = ((), (), s32[]{:S(2)}) async-start(), calls=%async_computation.19 | async-start | bytes 1179648 | tf_op jit(solution)/shard_map/reduce_scatter | solution.py:28
  1158.1 119.6 %copy-start.61 = (bf16[1,64,512]{2,1,0:T(8,128)(2,1)S(1)}, bf16[1,64,512]{2,1,0:T(8,128)(2,1)}, u32[]{:S(2)}) copy-start(bf16[1,64,512]{2,1,0:T(8,128)(2,1)} %get-tuple-element.41) | copy-start | bytes 196612
  1158.1 123.2 %copy-start.24 = (bf16[2,64,512]{2,1,0:T(8,128)(2,1)S(1)}, bf16[2,64,512]{2,1,0:T(8,128)(2,1)}, u32[]{:S(2)}) copy-start(bf16[2,64,512]{2,1,0:T(8,128)(2,1)} %param.13) | copy-start | bytes 393220
  1276.3 5.0 collective-permute-start.6
  1324.3 6.0 copy-start.16
  1324.3 7.5 copy-start.3
  1335.0 269.0 %reduce-scatter.35.cloned.1.call-start = ((), (), s32[]{:S(2)}) async-start(), calls=%async_computation.23 | async-start | bytes 1179648 | tf_op jit(solution)/shard_map/reduce_scatter | solution.py:28
  1335.9 117.6 %copy-start.60 = (bf16[1,64,512]{2,1,0:T(8,128)(2,1)S(1)}, bf16[1,64,512]{2,1,0:T(8,128)(2,1)}, u32[]{:S(2)}) copy-start(bf16[1,64,512]{2,1,0:T(8,128)(2,1)} %get-tuple-element.40) | copy-start | bytes 196612
  1335.9 121.3 %copy-start.25 = (bf16[2,64,512]{2,1,0:T(8,128)(2,1)S(1)}, bf16[2,64,512]{2,1,0:T(8,128)(2,1)}, u32[]{:S(2)}) copy-start(bf16[2,64,512]{2,1,0:T(8,128)(2,1)} %param.13) | copy-start | bytes 393220
  1452.2 5.0 collective-permute-start.7
  1499.5 6.1 copy-start.18
  1499.5 7.5 copy-start.4
  1510.1 7.7 copy-start.55
  1510.1 7.7 copy-start.57
  1510.2 7.8 copy-start.59
  1510.2 131.5 %reduce-scatter.31.cloned.1.call-start = ((), (), s32[]{:S(2)}) async-start(), calls=%async_computation.21 | async-start | bytes 4718592 | tf_op jit(solution)/shard_map/reduce_scatter | solution.py:197
  1522.0 16.0 copy-start.13
  1522.0 179.3 %reduce-scatter.33.cloned.1.call-start = ((), (), s32[]{:S(2)}) async-start(), calls=%async_computation.22 | async-start | bytes 9437184 | tf_op jit(solution)/shard_map/reduce_scatter | solution.py:198
  1525.8 13.0 copy-start.15
  1533.1 6.6 copy-start.17
  1533.1 7.4 copy-start.19
  1547.2 211.9 %reduce-scatter.29.cloned.1.call-start = ((), (), s32[]{:S(2)}) async-start(), calls=%async_computation.20 | async-start | bytes 9437184 | tf_op jit(solution)/shard_map/reduce_scatter | solution.py:196
  1554.0 51.1 %copy-start.81 = (f32[512]{0:T(512)S(1)}, f32[512]{0:T(512)}, u32[]{:S(2)}) copy-start(f32[512]{0:T(512)} %get-tuple-element.16) | copy-start | bytes 6148
  1554.0 51.1 %copy-start.82 = (f32[512]{0:T(512)S(1)}, f32[512]{0:T(512)}, u32[]{:S(2)}) copy-start(f32[512]{0:T(512)} %get-tuple-element.18) | copy-start | bytes 6148
  1554.0 51.1 %copy-start.83 = (f32[512]{0:T(512)S(1)}, f32[512]{0:T(512)}, u32[]{:S(2)}) copy-start(f32[512]{0:T(512)} %get-tuple-element.20) | copy-start | bytes 6148
  1554.0 51.1 %copy-start.84 = (f32[512]{0:T(512)S(1)}, f32[512]{0:T(512)}, u32[]{:S(2)}) copy-start(f32[512]{0:T(512)} %get-tuple-element.22) | copy-start | bytes 6148
  (42 other events, 110.1 us)
Sparse Core Ops, SparseCore 0:
  91.7 90.7 reduce-scatter.12
  261.7 95.8 reduce-scatter.14
  437.6 95.4 reduce-scatter.16
  613.3 97.9 reduce-scatter.18
  799.9 95.7 reduce-scatter.20
  979.6 94.0 reduce-scatter.22
  1157.3 95.3 reduce-scatter.24
  1335.2 93.1 reduce-scatter.26
  1510.3 93.7 reduce-scatter.34
  1606.6 34.9 reduce-scatter.30
  1645.0 56.2 reduce-scatter.32
  1704.4 54.5 reduce-scatter.28
where the time goes:
time: 1770 us
  waiting for transfers between devices  895 us (51%)
  blocking collectives  632 us (36%)
  matrix products  112 us (6%)
  local copies, waits for them, and re-layouts  56.3 us (3%)
  other arithmetic  42.7 us (2%)
    reduce_scatter x9, waiting for transfers between devices, head_total(): return lax.psum_scatter(operand, 'tensor', scatter_dimension=1, tiled=True)  746 us
    all_gather x10, blocking collectives, features(): return lax.all_gather(operand, 'tensor', axis=1, tiled=True)  413 us
    psum x9, blocking collectives, row_sum(): return lax.psum(operand, 'tensor')  205 us
    reduce_scatter x1, waiting for transfers between devices, shards(): lax.psum_scatter(grad_terms[0], 'dp', scatter_dimension=0, tiled=True)  57.8 us
    reduce_scatter x1, waiting for transfers between devices, shards(): lax.psum_scatter(grad_terms[2], 'dp', scatter_dimension=1, tiled=True)  57.3 us
    dot_general x15, matrix products, outer_side(): lax.dot_general(former, latter, (((1,), (1,)), ((), ())), preferred_eleme...  37.3 us
  transfers between devices with their start and end apart: 20, of which 19 were waited for; matrix products, arithmetic and copies ran while one was open for 4% of the time, Pallas kernels for 0%

commit v1 on v0

v1 whole, which is shorter than its diff:
```python
import jax
import jax.numpy as jnp
from jax import lax
from jax.sharding import Mesh, PartitionSpec as P

HEAD_DIM = 128
EPS = 1e-05
NEG = -1e30
F32 = jnp.float32
BF16 = jnp.bfloat16
SECTIONS, XS, HALVES = 4, 4, 2


def dot(former, latter, dims):
    return lax.dot_general(former, latter, (dims, ((), ())), preferred_element_type=F32)


def place(section, x, half):
    return (section * XS + x) * HALVES + half


def gather_x(block):
    spread = jnp.broadcast_to(block[None], (XS,) + block.shape)
    parts = lax.all_to_all(spread, "x", 0, 0)
    return jnp.concatenate([parts[j] for j in range(XS)], axis=-1)


def scatter_x(wide):
    width = wide.shape[1] // XS
    parts = jnp.stack([wide[:, j * width : (j + 1) * width] for j in range(XS)])
    return jnp.sum(lax.all_to_all(parts, "x", 0, 0).astype(F32), 0)


def hop(block, source, target):
    total = None
    for cross in range(HALVES):
        route = [
            (place(source, x, half), place(target, x, half ^ cross))
            for x in range(XS)
            for half in range(HALVES)
        ]
        got = lax.ppermute(block, ("s", "x", "zh"), route).astype(F32)
        total = got if total is None else total + got
    return total.astype(BF16)


def pair_up(block):
    route = [
        (place(s, x, half), place(s, x, 1 - half))
        for s in range(SECTIONS)
        for x in range(XS)
        for half in range(HALVES)
    ]
    other = lax.ppermute(block, ("s", "x", "zh"), route)
    first = lax.axis_index("zh") == 0
    return jnp.concatenate([jnp.where(first, block, other), jnp.where(first, other, block)], -1)


def pick(items, station):
    chosen = items[0]
    for s in range(1, SECTIONS):
        chosen = jnp.where(station == s, items[s], chosen)
    return chosen


def attend(queries, keyval, lengths, rows, length):
    group = queries.shape[1] // HEAD_DIM
    q = queries.reshape(rows, length, group, HEAD_DIM)
    keys = keyval[:, :HEAD_DIM].reshape(rows, length, HEAD_DIM)
    values = keyval[:, HEAD_DIM:].reshape(rows, length, HEAD_DIM)
    scores = jnp.einsum("rigd,rjd->rgij", q, keys, preferred_element_type=F32) * HEAD_DIM ** (-0.5)
    position = jnp.arange(length)
    allowed = (position[None, None, :] <= position[None, :, None]) & (
        position[None, None, :] < lengths[:, None, None]
    )
    scores = jnp.where(allowed[:, None], scores, NEG)
    raised = jnp.exp(scores - jnp.max(scores, -1, keepdims=True))
    weights = raised / jnp.sum(raised, -1, keepdims=True)
    mix = jnp.einsum("rgij,rjd->rigd", weights.astype(BF16), values, preferred_element_type=F32)
    return mix.reshape(rows * length, -1).astype(BF16), weights


def attend_back(queries, keyval, weights, mix_grad, rows, length):
    group = queries.shape[1] // HEAD_DIM
    q = queries.reshape(rows, length, group, HEAD_DIM)
    keys = keyval[:, :HEAD_DIM].reshape(rows, length, HEAD_DIM)
    values = keyval[:, HEAD_DIM:].reshape(rows, length, HEAD_DIM)
    grads = mix_grad.reshape(rows, length, group, HEAD_DIM)
    value_grad = jnp.einsum("rgij,rigd->rjd", weights.astype(BF16), grads, preferred_element_type=F32)
    weight_grad = jnp.einsum("rigd,rjd->rgij", grads, values, preferred_element_type=F32)
    score_grad = (
        weights * (weight_grad - jnp.sum(weight_grad * weights, -1, keepdims=True)) * HEAD_DIM ** (-0.5)
    ).astype(BF16)
    query_grad = jnp.einsum("rgij,rjd->rigd", score_grad, keys, preferred_element_type=F32)
    key_grad = jnp.einsum("rgij,rigd->rjd", score_grad, q, preferred_element_type=F32)
    pair_grad = jnp.concatenate([key_grad, value_grad], -1).reshape(rows * length, -1)
    return query_grad.reshape(rows * length, -1).astype(BF16), pair_grad.astype(BF16)


def shards(hidden_in, lengths, gains, w_query, w_keyval, w_out, grad_out):
    station = lax.axis_index("s")
    x = lax.axis_index("x")
    rows, length, shard = hidden_in.shape
    tokens = rows * length
    query_weight = w_query[0]
    width = query_weight.shape[0]
    pair_weight = w_keyval[0].reshape(width, -1)
    out_weight = w_out[0]
    block_width = width // XS

    start = jnp.where(
        station == 0, hidden_in.reshape(tokens, shard), grad_out.reshape(tokens, shard)
    )
    start = jnp.concatenate([start, jnp.broadcast_to(gains, (16, shard))], 0)
    start_block = pair_up(start)
    start_full = gather_x(start_block)
    gain_row = start_full[tokens].astype(F32)
    block = start_block[:tokens]
    full = start_full[:tokens]

    def own(wide):
        return lax.dynamic_slice_in_dim(wide, x * block_width, block_width, 1)

    kept = []
    for step in range(SECTIONS):
        if step:
            full = gather_x(block)
        wide = full.astype(F32)
        scale = lax.rsqrt(jnp.sum(wide * wide, -1, keepdims=True) / width + EPS)
        normed = (wide * scale * gain_row).astype(BF16)
        queries = dot(normed, query_weight, ((1,), (0,))).astype(BF16)
        keyval = dot(normed, pair_weight, ((1,), (0,))).astype(BF16)
        mix, weights = attend(queries, keyval, lengths, rows, length)
        kept.append((full, scale, normed, queries, keyval, mix, weights))
        if step + 1 < SECTIONS:
            branch = scatter_x(dot(mix, out_weight, ((1,), (0,))).astype(BF16))
            block = hop((0.5 * block.astype(F32) + branch).astype(BF16), step, step + 1)

    block = start_block[:tokens]
    full_grad = start_full[:tokens]
    found = [None] * SECTIONS
    for step in reversed(range(SECTIONS)):
        if step + 1 < SECTIONS:
            full_grad = gather_x(block)
        full, scale, normed, queries, keyval, mix, weights = kept[step]
        wide = full.astype(F32)
        mix_grad = dot(full_grad, out_weight, ((1,), (1,))).astype(BF16)
        query_grad, pair_grad = attend_back(queries, keyval, weights, mix_grad, rows, length)
        normed_grad = dot(query_grad, query_weight, ((1,), (1,))) + dot(
            pair_grad, pair_weight, ((1,), (1,))
        )
        gain_part = jnp.sum(normed_grad * wide * scale, 0)
        found[step] = (normed, full_grad, query_grad, pair_grad, mix, gain_part)
        if step:
            correction = jnp.sum(normed_grad * gain_row * wide, -1, keepdims=True)
            change = scale * gain_row * normed_grad - wide * (scale**3 / width) * correction
            branch = scatter_x(change.astype(BF16))
            block = hop((0.5 * block.astype(F32) + branch).astype(BF16), step, step - 1)

    normed, full_grad, query_grad, pair_grad, mix, gain_part = [
        pick(items, station) for items in zip(*found)
    ]
    dp = 8
    small = width // dp
    cut = lambda wide: wide.reshape(tokens, dp, small).transpose(1, 0, 2)
    spread = lambda narrow: jnp.broadcast_to(narrow[None], (dp,) + narrow.shape)
    send = jnp.concatenate(
        [cut(normed), cut(full_grad), spread(query_grad), spread(pair_grad), spread(mix)], -1
    )
    got = lax.all_to_all(send, ("y", "core"), 0, 0).reshape(dp * tokens, -1)
    edges = [0]
    for piece in (small, small, query_grad.shape[1], pair_grad.shape[1], mix.shape[1]):
        edges.append(edges[-1] + piece)
    normed, full_grad, query_grad, pair_grad, mix = [
        got[:, a:b] for a, b in zip(edges[:-1], edges[1:])
    ]
    grad_query = dot(normed, query_grad, ((0,), (0,)))
    grad_pair = dot(normed, pair_grad, ((0,), (0,)))
    grad_out_weight = dot(mix, full_grad, ((0,), (0,)))

    pieces = gain_part.reshape(8, dp, -1)
    pieces = lax.all_to_all(pieces.transpose(1, 0, 2), ("y", "core"), 0, 0)
    pieces = jnp.sum(pieces, 0)
    pieces = lax.all_to_all(pieces, ("x", "zh"), 0, 0)
    gain_grad = jnp.sum(pieces, 0)
    return (
        grad_query[None],
        grad_pair.reshape(1, small, 1, -1),
        grad_out_weight[None],
        gain_grad[None],
    )


def solution(mesh):
    grid = Mesh(mesh.devices.reshape(SECTIONS, XS, HALVES, 4, 2), ("s", "x", "zh", "y", "core"))
    section, tensor, dp = "s", ("x", "zh"), ("y", "core")
    in_specs = (
        P(dp, None, tensor),
        P(dp),
        P(section, tensor),
        P(section, None, tensor),
        P(section, None, tensor, None),
        P(section, tensor, None),
        P(dp, None, tensor),
    )
    out_specs = (
        P(section, dp, tensor),
        P(section, dp, tensor, None),
        P(section, tensor, dp),
        P(section, tensor + dp),
    )
    return jax.shard_map(shards, mesh=grid, in_specs=in_specs, out_specs=out_specs, check_vma=False)
```

time: 1770 us -> 517 us (0.29)
  waiting for transfers between devices: 895 us -> 114 us
  blocking collectives: 632 us -> 143 us
  starting transfers between devices: 11.6 us -> 80.4 us
  other arithmetic: 42.7 us -> 17.4 us
    reduce_scatter x12 -> x0, waiting for transfers between devices: 883 us -> none  [the longest x9 746 us: head_total(): return lax.psum_scatter(operand, 'tensor', scatter_dimension=1, tiled=True)]
    all_gather x10 -> x0, blocking collectives: 413 us -> none  [features(): return lax.all_gather(operand, 'tensor', axis=1, tiled=True)]
    psum x9 -> x0, blocking collectives: 205 us -> none  [row_sum(): return lax.psum(operand, 'tensor')]
    all_to_all x0 -> x10, blocking collectives: none -> 143 us  [the longest x6 86.6 us: scatter_x(): return jnp.sum(lax.all_to_all(parts, 'x', 0, 0).astype(F32), 0)]
    all_to_all x0 -> x6, waiting for transfers between devices: none -> 86.5 us  [the longest x1 54 us: shards(): got = lax.all_to_all(send, ('y', 'core'), 0, 0).reshape(dp * tokens, -1)]
    all_to_all x0 -> x6, starting transfers between devices: none -> 54 us  [the longest x1 30.3 us: shards(): pieces = lax.all_to_all(pieces.transpose(1, 0, 2), ('y', 'core'), 0, 0)]
    dot_general x62 -> x46, matrix products: 112 us -> 95.4 us  [the longest x26 55.7 us: dot(): lax.dot_general(former, latter, (dims, ((), ())), preferred_element_type=...]
  transfers between devices with their start and end apart: 20 -> 19, of which waited for: 19 -> 11; matrix products, arithmetic and copies ran while one was open for 4% -> 4% of each run, Pallas kernels for 0% -> 0%
where the time goes in v1:
time: 517 us; the launch traced here: 511 us
  blocking collectives  143 us (28%)
  waiting for transfers between devices  114 us (22%)
  matrix products  105 us (20%)
  starting transfers between devices  80.4 us (16%)
  local copies, waits for them, and re-layouts  48.8 us (9%)
  other arithmetic  17.4 us (3%)
    all_to_all x6, blocking collectives, scatter_x(): return jnp.sum(lax.all_to_all(parts, 'x', 0, 0).astype(F32), 0)  86.6 us
    all_to_all x4, blocking collectives, gather_x(): parts = lax.all_to_all(spread, 'x', 0, 0)  56.5 us
    dot_general x26, matrix products, dot(): lax.dot_general(former, latter, (dims, ((), ())), preferred_element_type=...  55.7 us
    all_to_all x1, waiting for transfers between devices, shards(): got = lax.all_to_all(send, ('y', 'core'), 0, 0).reshape(dp * tokens, -1)  54 us
    all_to_all x1, starting transfers between devices, shards(): pieces = lax.all_to_all(pieces.transpose(1, 0, 2), ('y', 'core'), 0, 0)  30.3 us
    ppermute x12, waiting for transfers between devices, hop(): got = lax.ppermute(block, ('s', 'x', 'zh'), route).astype(F32)  24.7 us
    all_to_all x3, waiting for transfers between devices, gather_x(): parts = lax.all_to_all(spread, 'x', 0, 0)  24.5 us
    ppermute x12, starting transfers between devices, hop(): got = lax.ppermute(block, ('s', 'x', 'zh'), route).astype(F32)  18.6 us
  transfers between devices with their start and end apart: 19, of which 11 were waited for; matrix products, arithmetic and copies ran while one was open for 4% of the time, Pallas kernels for 0%

profile of v1, /device:TPU:1, one launch (start us, length us, event | category | flops | bytes accessed | tf_op | source)
XLA Modules:
  0.0 511.4 jit_solution(9062520839798025737)
XLA Ops:
  2.5 7.8 %collective-permute-start = (bf16[144,512]{1,0:T(8,128)(2,1)S(1)}, bf16[144,512]{1,0:T(8,128)(2,1)S(1)}, u32[]{:S(2)}, u32[]{:S(2)}) collective-permute-start(bf16[144,512]{1,0:T(8,128)(2,1)S(1)} %pad_maximum_fusion.17), channel_id=1, source_target_pairs={{0,8},{8,0},{16,24},{24,16},{32,40},{40,32},{48,56},{56,48},{64,72... | collective-permute-start | bytes 442376 | tf_op jit(solution)/shard_map/ppermute | solution.py:54
  10.3 3.0 collective-permute-done
  14.6 4.6 all-to-all-start
  19.4 14.7 %all-to-all-done = bf16[4,144,1024]{2,1,0:T(8,128)(2,1)S(1)} async-done(((bf16[4,144,1024]{2,1,0:T(8,128)(2,1)}), bf16[4,144,1024]{2,1,0:T(8,128)(2,1)S(1)}, u32[]{:S(2)}, u32[]{:S(2)}) %all-to-all-start) | async-done | bytes 1179680 | tf_op jit(solution)/shard_map/all_to_all | solution.py:24
  39.9 1.9 fusion.343
  41.8 2.0 convolution_convert_fusion.10
  44.8 2.9 convolution_convert_fusion.2
  48.0 15.2 %all_to_all.84 = bf16[4,128,1024]{2,1,0:T(8,128)(2,1)S(1)} all-to-all(bf16[4,128,1024]{2,1,0:T(8,128)(2,1)S(1)} %pad_maximum_fusion.1), channel_id=1, replica_groups=mesh['s'=4,'x'=4,'zh'=2,'y'=4,'core'=2] {'x'}, dimensions={0} | all-to-all | bytes 2097152 | tf_op jit(solution)/shard_map/all_to_all | solution.py:31
  63.4 9.0 %collective-permute-start.2 = (bf16[128,1024]{1,0:T(8,128)(2,1)S(1)}, bf16[128,1024]{1,0:T(8,128)(2,1)S(1)}, u32[]{:S(2)}, u32[]{:S(2)}) collective-permute-start(bf16[128,1024]{1,0:T(8,128)(2,1)S(1)} %add_convert_fusion.11), channel_id=1, source_target_pairs={{0,72},{8,64},{16,88},{24,80},{32,104},{40,96},{48,120},{56,112},{... | collective-permute-start | bytes 786440 | tf_op jit(solution)/shard_map/ppermute | solution.py:42
  73.8 2.0 collective-permute-done.2
  77.2 12.5 %all_to_all.85 = bf16[4,128,1024]{2,1,0:T(8,128)(2,1)S(1)} all-to-all(bf16[4,128,1024]{2,1,0:T(8,128)(2,1)S(1)} %broadcast_in_dim.59), channel_id=1, replica_groups=mesh['s'=4,'x'=4,'zh'=2,'y'=4,'core'=2] {'x'}, dimensions={0} | all-to-all | bytes 2097152 | tf_op jit(solution)/shard_map/all_to_all | solution.py:24
  96.5 2.5 fusion.346
  99.0 2.1 convolution_convert_fusion.9
  102.1 2.9 convolution_convert_fusion.1
  105.3 12.3 %all_to_all.86 = bf16[4,128,1024]{2,1,0:T(8,128)(2,1)S(1)} all-to-all(bf16[4,128,1024]{2,1,0:T(8,128)(2,1)S(1)} %pad_maximum_fusion.3), channel_id=1, replica_groups=mesh['s'=4,'x'=4,'zh'=2,'y'=4,'core'=2] {'x'}, dimensions={0} | all-to-all | bytes 2097152 | tf_op jit(solution)/shard_map/all_to_all | solution.py:31
  119.4 12.2 %all_to_all.87 = bf16[4,128,1024]{2,1,0:T(8,128)(2,1)S(1)} all-to-all(bf16[4,128,1024]{2,1,0:T(8,128)(2,1)S(1)} %broadcast_in_dim.60), channel_id=1, replica_groups=mesh['s'=4,'x'=4,'zh'=2,'y'=4,'core'=2] {'x'}, dimensions={0} | all-to-all | bytes 2097152 | tf_op jit(solution)/shard_map/all_to_all | solution.py:24
  133.2 1.6 copy-done.6
  138.4 2.5 fusion.349
  140.9 2.1 convolution_convert_fusion.8
  144.0 2.9 convolution_convert_fusion
  147.2 12.3 %all_to_all.88 = bf16[4,128,1024]{2,1,0:T(8,128)(2,1)S(1)} all-to-all(bf16[4,128,1024]{2,1,0:T(8,128)(2,1)S(1)} %pad_maximum_fusion.5), channel_id=1, replica_groups=mesh['s'=4,'x'=4,'zh'=2,'y'=4,'core'=2] {'x'}, dimensions={0} | all-to-all | bytes 2097152 | tf_op jit(solution)/shard_map/all_to_all | solution.py:31
  162.6 4.3 all-to-all-start.6
  166.8 4.4 fusion.126
  172.8 3.9 all-to-all-done.6
  184.6 1.9 convolution_bitcast_fusion.6
  186.5 2.5 fusion.352
  189.0 2.1 fusion.154
  191.0 2.1 fusion.153
  193.1 2.1 fusion.138
  196.3 3.7 fusion.27
  202.7 12.3 %all_to_all.89 = bf16[4,128,1024]{2,1,0:T(8,128)(2,1)S(1)} all-to-all(bf16[4,128,1024]{2,1,0:T(8,128)(2,1)S(1)} %pad_maximum_fusion.7), channel_id=1, replica_groups=mesh['s'=4,'x'=4,'zh'=2,'y'=4,'core'=2] {'x'}, dimensions={0} | all-to-all | bytes 2097152 | tf_op jit(solution)/shard_map/all_to_all | solution.py:31
  216.9 14.8 %all_to_all.90 = bf16[4,128,1024]{2,1,0:T(8,128)(2,1)S(1)} all-to-all(bf16[4,128,1024]{2,1,0:T(8,128)(2,1)S(1)} %broadcast_in_dim.62), channel_id=1, replica_groups=mesh['s'=4,'x'=4,'zh'=2,'y'=4,'core'=2] {'x'}, dimensions={0} | all-to-all | bytes 2097152 | tf_op jit(solution)/shard_map/all_to_all | solution.py:24
  232.7 2.2 fusion.129
  236.5 2.1 fusion.156
  238.6 1.9 convolution_bitcast_fusion.5
  240.5 2.1 fusion.155
  242.5 2.2 convolution_convert_fusion.6
  245.8 3.7 fusion.25
  252.2 22.3 %all_to_all.91 = bf16[4,128,1024]{2,1,0:T(8,128)(2,1)S(1)} all-to-all(bf16[4,128,1024]{2,1,0:T(8,128)(2,1)S(1)} %pad_maximum_fusion.9), channel_id=1, replica_groups=mesh['s'=4,'x'=4,'zh'=2,'y'=4,'core'=2] {'x'}, dimensions={0} | all-to-all | bytes 2097152 | tf_op jit(solution)/shard_map/all_to_all | solution.py:31
  276.3 17.1 %all_to_all.92 = bf16[4,128,1024]{2,1,0:T(8,128)(2,1)S(1)} all-to-all(bf16[4,128,1024]{2,1,0:T(8,128)(2,1)S(1)} %broadcast_in_dim.63), channel_id=1, replica_groups=mesh['s'=4,'x'=4,'zh'=2,'y'=4,'core'=2] {'x'}, dimensions={0} | all-to-all | bytes 2097152 | tf_op jit(solution)/shard_map/all_to_all | solution.py:24
  294.5 2.2 fusion.132
  298.2 2.1 fusion.158
  300.3 1.9 convolution_bitcast_fusion.4
  302.2 2.1 fusion.157
  304.3 2.2 convolution_convert_fusion.5
  307.5 3.7 fusion.23
  313.9 12.3 %all_to_all.93 = bf16[4,128,1024]{2,1,0:T(8,128)(2,1)S(1)} all-to-all(bf16[4,128,1024]{2,1,0:T(8,128)(2,1)S(1)} %pad_maximum_fusion.11), channel_id=1, replica_groups=mesh['s'=4,'x'=4,'zh'=2,'y'=4,'core'=2] {'x'}, dimensions={0} | all-to-all | bytes 2097152 | tf_op jit(solution)/shard_map/all_to_all | solution.py:31
  329.7 2.2 fusion.140
  333.6 21.0 %collective-permute-done.12 = bf16[128,1024]{1,0:T(8,128)(2,1)} collective-permute-done((bf16[128,1024]{1,0:T(8,128)(2,1)}, bf16[128,1024]{1,0:T(8,128)(2,1)}, u32[]{:S(2)}, u32[]{:S(2)}) %collective-permute-start.12) | collective-permute-done | bytes 262176 | tf_op jit(solution)/shard_map/ppermute | solution.py:42
  357.2 4.3 all-to-all-start.12
  361.5 2.8 select_select_fusion.1
  365.3 5.9 %all-to-all-done.12 = bf16[4,128,1024]{2,1,0:T(8,128)(2,1)} async-done(((bf16[4,128,1024]{2,1,0:T(8,128)(2,1)}), bf16[4,128,1024]{2,1,0:T(8,128)(2,1)}, u32[]{:S(2)}, u32[]{:S(2)}) %all-to-all-start.12) | async-done | bytes 1048608 | tf_op jit(solution)/shard_map/all_to_all | solution.py:24
  378.5 1.7 convolution_bitcast_fusion.3
  380.2 2.2 bitcast_select_fusion
  385.1 3.7 fusion.21
  390.7 30.3 %all-to-all-start.14 = ((f32[8,1,512]{2,1,0:T(1,128)}), f32[8,1,512]{2,1,0:T(1,128)S(1)}, u32[]{:S(2)}, u32[]{:S(2)}) async-start(f32[8,1,512]{2,1,0:T(1,128)} %reshape.388), calls=%async_computation.14 | async-start | bytes 32768 | tf_op jit(solution)/shard_map/all_to_all | solution.py:182
  421.0 2.3 fusion.161
  427.5 4.1 all-to-all-start.15
  432.7 7.7 %all-to-all-done.15 = f32[8,1,64]{2,1,0:T(1,128)S(1)} async-done(((f32[8,1,64]{2,1,0:T(1,128)}), f32[8,1,64]{2,1,0:T(1,128)S(1)}, u32[]{:S(2)}, u32[]{:S(2)}) %all-to-all-start.15) | async-done | bytes 2080 | tf_op jit(solution)/shard_map/all_to_all | solution.py:184
  440.4 6.6 %all-to-all-start.13 = ((bf16[8,128,2304]{2,1,0:T(8,128)(2,1)}), bf16[8,128,2304]{2,1,0:T(8,128)(2,1)}, u32[]{:S(2)}, u32[]{:S(2)}) async-start(bf16[8,128,2304]{2,1,0:T(8,128)(2,1)} %broadcast_dynamic-update-slice_fusion), calls=%async_computation.13 | async-start | bytes 9437184 | tf_op jit(solution)/shard_map/all_to_all | solution.py:170
  447.6 54.0 %all-to-all-done.13 = bf16[8,128,2304]{2,1,0:T(8,128)(2,1)} async-done(((bf16[8,128,2304]{2,1,0:T(8,128)(2,1)}), bf16[8,128,2304]{2,1,0:T(8,128)(2,1)}, u32[]{:S(2)}, u32[]{:S(2)}) %all-to-all-start.13) | async-done | bytes 4718624 | tf_op jit(solution)/shard_map/all_to_all | solution.py:170
  501.6 1.8 convolution_bitcast_fusion.2
  503.4 3.3 convolution_bitcast_fusion
  506.7 3.3 convolution_bitcast_fusion.1
  (325 shorter events, 88.9 us)
Async XLA Ops:
  0.6 34.0 %copy-start = (bf16[1,4096,1,256]{3,1,2,0:T(8,128)(2,1)S(1)}, bf16[1,4096,1,256]{3,1,2,0:T(8,128)(2,1)}, u32[]{:S(2)}) copy-start(bf16[1,4096,1,256]{3,1,2,0:T(8,128)(2,1)} %param.11) | copy-start | bytes 6291460
  2.5 10.9 %collective-permute-start = (bf16[144,512]{1,0:T(8,128)(2,1)S(1)}, bf16[144,512]{1,0:T(8,128)(2,1)S(1)}, u32[]{:S(2)}, u32[]{:S(2)}) collective-permute-start(bf16[144,512]{1,0:T(8,128)(2,1)S(1)} %pad_maximum_fusion.17), channel_id=1, source_target_pairs={{0,8},{8,0},{16,24},{24,16},{32,40},{40,32},{48,56},{56,48},{64,72... | collective-permute-start | bytes 442376 | tf_op jit(solution)/shard_map/ppermute | solution.py:54
  13.4 50.0 %copy-start.38 = (bf16[144,512]{1,0:T(8,128)(2,1)}, bf16[144,512]{1,0:T(8,128)(2,1)S(1)}, u32[]{:S(2)}) copy-start(bf16[144,512]{1,0:T(8,128)(2,1)S(1)} %get-tuple-element.78) | copy-start | bytes 442372
  13.4 5.8 %copy-start.89 = (s32[2]{0:T(128)S(1)}, s32[2]{0:T(128)}, u32[]{:S(2)}) copy-start(s32[2]{0:T(128)} %param.8) | copy-start | bytes 28
  14.6 19.5 %all-to-all-start = ((bf16[4,144,1024]{2,1,0:T(8,128)(2,1)}), bf16[4,144,1024]{2,1,0:T(8,128)(2,1)S(1)}, u32[]{:S(2)}, u32[]{:S(2)}) async-start(bf16[4,144,1024]{2,1,0:T(8,128)(2,1)} %broadcast_in_dim.56), calls=%async_computation | async-start | bytes 2359296 | tf_op jit(solution)/shard_map/all_to_all | solution.py:24
  19.4 22.4 %copy-start.74 = (pred[2,64,64]{1,2,0:T(8,128)(4,1)}, pred[2,64,64]{1,2,0:T(8,128)(4,1)S(1)}, u32[]{:S(2)}) copy-start(pred[2,64,64]{1,2,0:T(8,128)(4,1)S(1)} %broadcast_and_fusion) | copy-start | bytes 24580
  36.8 5.0 copy-start.60
  41.8 6.0 %copy-start.90 = (f32[2,4,64]{2,1,0:T(4,128)}, f32[2,4,64]{2,1,0:T(4,128)S(1)}, u32[]{:S(2)}) copy-start(f32[2,4,64]{2,1,0:T(4,128)S(1)} %get-tuple-element.94) | copy-start | bytes 6148
  48.0 15.4 %copy-start.41 = (bf16[144,512]{1,0:T(8,128)(2,1)S(1)}, bf16[144,512]{1,0:T(8,128)(2,1)}, u32[]{:S(2)}) copy-start(bf16[144,512]{1,0:T(8,128)(2,1)} %copy-done.40) | copy-start | bytes 442372
  63.4 12.3 %collective-permute-start.2 = (bf16[128,1024]{1,0:T(8,128)(2,1)S(1)}, bf16[128,1024]{1,0:T(8,128)(2,1)S(1)}, u32[]{:S(2)}, u32[]{:S(2)}) collective-permute-start(bf16[128,1024]{1,0:T(8,128)(2,1)S(1)} %add_convert_fusion.11), channel_id=1, source_target_pairs={{0,72},{8,64},{16,88},{24,80},{32,104},{40,96},{48,120},{56,112},{... | collective-permute-start | bytes 786440 | tf_op jit(solution)/shard_map/ppermute | solution.py:42
  72.4 4.6 collective-permute-start.1
  77.1 12.7 %copy-start.34 = (bf16[128,1024]{1,0:T(8,128)(2,1)}, bf16[128,1024]{1,0:T(8,128)(2,1)S(1)}, u32[]{:S(2)}) copy-start(bf16[128,1024]{1,0:T(8,128)(2,1)S(1)} %add_convert_fusion.10) | copy-start | bytes 786436
  105.2 12.5 %copy-start.35 = (bf16[128,1024]{1,0:T(8,128)(2,1)S(1)}, bf16[128,1024]{1,0:T(8,128)(2,1)}, u32[]{:S(2)}) copy-start(bf16[128,1024]{1,0:T(8,128)(2,1)} %copy-done.34) | copy-start | bytes 786436
  117.8 1.4 collective-permute-start.4
  118.5 0.7 collective-permute-start.3
  119.3 12.4 %copy-start.36 = (bf16[128,1024]{1,0:T(8,128)(2,1)}, bf16[128,1024]{1,0:T(8,128)(2,1)S(1)}, u32[]{:S(2)}) copy-start(bf16[128,1024]{1,0:T(8,128)(2,1)S(1)} %add_convert_fusion.8) | copy-start | bytes 786436
  147.2 12.5 %copy-start.37 = (bf16[128,1024]{1,0:T(8,128)(2,1)S(1)}, bf16[128,1024]{1,0:T(8,128)(2,1)}, u32[]{:S(2)}) copy-start(bf16[128,1024]{1,0:T(8,128)(2,1)} %copy-done.36) | copy-start | bytes 786436
  159.7 1.6 collective-permute-start.6
  160.4 1.0 collective-permute-start.5
  162.6 14.1 %all-to-all-start.6 = ((bf16[4,128,1024]{2,1,0:T(8,128)(2,1)}), bf16[4,128,1024]{2,1,0:T(8,128)(2,1)}, u32[]{:S(2)}, u32[]{:S(2)}) async-start(bf16[4,128,1024]{2,1,0:T(8,128)(2,1)} %broadcast_in_dim.61), calls=%async_computation.6 | async-start | bytes 2097152 | tf_op jit(solution)/shard_map/all_to_all | solution.py:24
  196.3 3.8 copy-start.23
  196.3 3.8 copy-start.25
  196.3 3.8 copy-start.27
  196.3 3.8 copy-start.29
  196.3 3.8 copy-start.61
  196.3 3.8 copy-start.63
  196.3 3.8 copy-start.85
  202.7 12.5 %copy-start.39 = (bf16[144,512]{1,0:T(8,128)(2,1)S(1)}, bf16[144,512]{1,0:T(8,128)(2,1)}, u32[]{:S(2)}) copy-start(bf16[144,512]{1,0:T(8,128)(2,1)} %copy-done.38) | copy-start | bytes 442372
  202.7 12.5 %copy-start.42 = (bf16[144,512]{1,0:T(8,128)(2,1)S(1)}, bf16[144,512]{1,0:T(8,128)(2,1)}, u32[]{:S(2)}) copy-start(bf16[144,512]{1,0:T(8,128)(2,1)} %copy-done.40) | copy-start | bytes 442372
  215.3 1.4 collective-permute-start.8
  215.9 0.7 collective-permute-start.7
  216.7 15.0 %copy-start.30 = (bf16[128,1024]{1,0:T(8,128)(2,1)}, bf16[128,1024]{1,0:T(8,128)(2,1)S(1)}, u32[]{:S(2)}) copy-start(bf16[128,1024]{1,0:T(8,128)(2,1)S(1)} %add_convert_fusion.4) | copy-start | bytes 786436
  216.9 15.9 %copy-start.1 = (bf16[1,512,4096]{2,1,0:T(8,128)(2,1)S(1)}, bf16[1,512,4096]{2,1,0:T(8,128)(2,1)}, u32[]{:S(2)}) copy-start(bf16[1,512,4096]{2,1,0:T(8,128)(2,1)} %param.12) | copy-start | bytes 12582916
  245.7 3.8 copy-start.15
  245.7 3.8 copy-start.17
  245.7 3.8 copy-start.19
  245.8 3.8 copy-start.21
  245.8 3.8 copy-start.65
  245.8 3.8 copy-start.67
  245.8 3.8 copy-start.83
  252.1 22.5 %copy-start.31 = (bf16[128,1024]{1,0:T(8,128)(2,1)S(1)}, bf16[128,1024]{1,0:T(8,128)(2,1)}, u32[]{:S(2)}) copy-start(bf16[128,1024]{1,0:T(8,128)(2,1)} %copy-done.30) | copy-start | bytes 786436
  274.7 1.4 collective-permute-start.10
  275.4 0.7 collective-permute-start.9
  276.2 17.3 %copy-start.32 = (bf16[128,1024]{1,0:T(8,128)(2,1)}, bf16[128,1024]{1,0:T(8,128)(2,1)S(1)}, u32[]{:S(2)}) copy-start(bf16[128,1024]{1,0:T(8,128)(2,1)S(1)} %add_convert_fusion.2) | copy-start | bytes 786436
  276.3 18.2 %copy-start.2 = (bf16[1,512,4096]{2,1,0:T(8,128)(2,1)S(1)}, bf16[1,512,4096]{2,1,0:T(8,128)(2,1)}, u32[]{:S(2)}) copy-start(bf16[1,512,4096]{2,1,0:T(8,128)(2,1)} %param.12) | copy-start | bytes 12582916
  307.5 3.8 copy-start.9
  307.5 3.8 copy-start.11
  307.5 3.8 copy-start.13
  307.5 3.8 copy-start.69
  307.5 3.8 copy-start.71
  307.5 3.8 copy-start.81
  313.9 12.5 %copy-start.33 = (bf16[128,1024]{1,0:T(8,128)(2,1)S(1)}, bf16[128,1024]{1,0:T(8,128)(2,1)}, u32[]{:S(2)}) copy-start(bf16[128,1024]{1,0:T(8,128)(2,1)} %copy-done.32) | copy-start | bytes 786436
  327.1 27.5 %collective-permute-start.12 = (bf16[128,1024]{1,0:T(8,128)(2,1)}, bf16[128,1024]{1,0:T(8,128)(2,1)}, u32[]{:S(2)}, u32[]{:S(2)}) collective-permute-start(bf16[128,1024]{1,0:T(8,128)(2,1)} %add_convert_fusion.1), channel_id=1, source_target_pairs={{64,8},{72,0},{80,24},{88,16},{96,40},{104,32},{112,56},{120,48},{... | collective-permute-start | bytes 786440 | tf_op jit(solution)/shard_map/ppermute | solution.py:42
  328.4 26.6 %collective-permute-start.11 = (bf16[128,1024]{1,0:T(8,128)(2,1)}, bf16[128,1024]{1,0:T(8,128)(2,1)}, u32[]{:S(2)}, u32[]{:S(2)}) collective-permute-start(bf16[128,1024]{1,0:T(8,128)(2,1)} %add_convert_fusion.1), channel_id=1, source_target_pairs={{64,0},{72,8},{80,16},{88,24},{96,32},{104,40},{112,48},{120,56},{... | collective-permute-start | bytes 786440 | tf_op jit(solution)/shard_map/ppermute | solution.py:42
  357.2 14.1 %all-to-all-start.12 = ((bf16[4,128,1024]{2,1,0:T(8,128)(2,1)}), bf16[4,128,1024]{2,1,0:T(8,128)(2,1)}, u32[]{:S(2)}, u32[]{:S(2)}) async-start(bf16[4,128,1024]{2,1,0:T(8,128)(2,1)} %broadcast_in_dim.64), calls=%async_computation.12 | async-start | bytes 2097152 | tf_op jit(solution)/shard_map/all_to_all | solution.py:24
  364.2 8.5 %copy-start.44 = (bf16[128,1024]{1,0:T(8,128)(2,1)S(1)}, bf16[128,1024]{1,0:T(8,128)(2,1)}, u32[]{:S(2)}) copy-start(bf16[128,1024]{1,0:T(8,128)(2,1)} %copy-done.43) | copy-start | bytes 786436
  385.0 3.8 copy-start.62
  385.0 3.8 copy-start.64
  385.0 3.8 copy-start.66
  385.1 3.8 copy-start.79
  389.9 41.7 %copy-start.59 = (bf16[16,8,4,128]{3,1,2,0:T(8,128)(2,1)S(1)}, bf16[16,8,4,128]{3,1,2,0:T(8,128)(2,1)}, u32[]{:S(2)}) copy-start(bf16[16,8,4,128]{3,1,2,0:T(8,128)(2,1)} %copy.300) | copy-start | bytes 393220
  390.7 34.9 %all-to-all-start.14 = ((f32[8,1,512]{2,1,0:T(1,128)}), f32[8,1,512]{2,1,0:T(1,128)S(1)}, u32[]{:S(2)}, u32[]{:S(2)}) async-start(f32[8,1,512]{2,1,0:T(1,128)} %reshape.388), calls=%async_computation.14 | async-start | bytes 32768 | tf_op jit(solution)/shard_map/all_to_all | solution.py:182
  427.5 12.9 %all-to-all-start.15 = ((f32[8,1,64]{2,1,0:T(1,128)}), f32[8,1,64]{2,1,0:T(1,128)S(1)}, u32[]{:S(2)}, u32[]{:S(2)}) async-start(f32[8,1,64]{2,1,0:T(1,128)} %bitcast.146), calls=%async_computation.15 | async-start | bytes 8192 | tf_op jit(solution)/shard_map/all_to_all | solution.py:184
  440.4 61.2 %all-to-all-start.13 = ((bf16[8,128,2304]{2,1,0:T(8,128)(2,1)}), bf16[8,128,2304]{2,1,0:T(8,128)(2,1)}, u32[]{:S(2)}, u32[]{:S(2)}) async-start(bf16[8,128,2304]{2,1,0:T(8,128)(2,1)} %broadcast_dynamic-update-slice_fusion), calls=%async_computation.13 | async-start | bytes 9437184 | tf_op jit(solution)/shard_map/all_to_all | solution.py:170
  (47 other events, 71.8 us)

commit v2 on v1

v2 whole, which is shorter than its diff:
```python
import functools

import jax
import jax.numpy as jnp
from jax import lax
from jax.experimental import pallas as pl
from jax.experimental.pallas import tpu as pltpu
from jax.sharding import Mesh, PartitionSpec as P

HEAD_DIM = 128
EPS = 1e-05
NEG = -1e30
F32 = jnp.float32
BF16 = jnp.bfloat16
SECTIONS, XS, HALVES, DP = 4, 4, 2, 8
VMEM = pl.BlockSpec(memory_space=pltpu.VMEM)
SMEM = pl.BlockSpec(memory_space=pltpu.SMEM)
HBM = pl.BlockSpec(memory_space=pl.ANY)


def dot(former, latter, dims=((1,), (0,))):
    return lax.dot_general(former, latter, (dims, ((), ())), preferred_element_type=F32)


def copies(pairs, sems):
    return [pltpu.make_async_copy(a, b, sems.at[i]) for i, (a, b) in enumerate(pairs)]


def heads_down(wide, row, length):
    part = wide[row * length : (row + 1) * length, :]
    return jnp.concatenate(
        [part[:, a : a + HEAD_DIM] for a in range(0, part.shape[1], HEAD_DIM)], axis=0
    )


def heads_across(tall, length):
    return jnp.concatenate(
        [tall[a : a + length] for a in range(0, tall.shape[0], length)], axis=1
    )


def forward_kernel(
    rows, length, project, lens, parts, gain, wq, wkv, wo, *rest
):
    if project:
        send, scale_out, q_out, kv_out, mix_out, attn_out, wq_v, wkv_v, wo_v, sems = rest
    else:
        scale_out, q_out, kv_out, mix_out, attn_out, wq_v, wkv_v, sems = rest
    block = parts.shape[2]
    width = XS * block
    pairs = []
    for j in range(XS):
        span = pl.ds(j * block, block)
        pairs.append((wq.at[span], wq_v.at[span]))
        pairs.append((wkv.at[span], wkv_v.at[span]))
    if project:
        for j in range(XS):
            span = pl.ds(j * block, block)
            pairs.append((wo.at[:, span], wo_v.at[:, span]))
    moves = copies(pairs, sems)
    for move in moves:
        move.start()
    total = jnp.zeros((parts.shape[1], 1), F32)
    for j in range(XS):
        h = parts[j].astype(F32)
        total = total + jnp.sum(h * h, -1, keepdims=True)
    scale = lax.rsqrt(total / width + EPS)
    scale_out[...] = scale
    q = jnp.zeros(q_out.shape, F32)
    kv = jnp.zeros(kv_out.shape, F32)
    for j in range(XS):
        span = slice(j * block, (j + 1) * block)
        normed = (parts[j].astype(F32) * scale * gain[:, span].astype(F32)).astype(BF16)
        moves[2 * j].wait()
        q = q + dot(normed, wq_v[span, :])
        moves[2 * j + 1].wait()
        kv = kv + dot(normed, wkv_v[span, :])
    q = q.astype(BF16)
    kv = kv.astype(BF16)
    q_out[...] = q
    kv_out[...] = kv
    tall = q.shape[1] // HEAD_DIM * length
    at = lax.broadcasted_iota(jnp.int32, (tall, length), 0) % length
    key_at = lax.broadcasted_iota(jnp.int32, (tall, length), 1)
    mixes = []
    for row in range(rows):
        here = slice(row * length, (row + 1) * length)
        keys, values = kv[here, :HEAD_DIM], kv[here, HEAD_DIM:]
        scores = dot(heads_down(q, row, length), keys, ((1,), (1,))) * HEAD_DIM ** (-0.5)
        scores = jnp.where((key_at <= at) & (key_at < lens[row]), scores, NEG)
        raised = jnp.exp(scores - jnp.max(scores, -1, keepdims=True))
        attn = raised / jnp.sum(raised, -1, keepdims=True)
        attn_out[row] = attn
        mixes.append(heads_across(dot(attn.astype(BF16), values).astype(BF16), length))
    mix = jnp.concatenate(mixes, axis=0)
    mix_out[...] = mix
    if project:
        for j in range(XS):
            moves[2 * XS + j].wait()
            send[j] = dot(mix, wo_v[:, j * block : (j + 1) * block]).astype(BF16)


def backward_kernel(
    rows, length, onward, grads, parts, gain, scale_in, q_in, kv_in, attn_in, wq, wkv, wo, *rest
):
    if onward:
        send, qg_out, pg_out, gain_out, wq_v, wkv_v, wo_v, sems = rest
    else:
        qg_out, pg_out, gain_out, wq_v, wkv_v, wo_v, sems = rest
    block = parts.shape[2]
    width = XS * block
    pairs = []
    for j in range(XS):
        span = pl.ds(j * block, block)
        pairs.append((wo.at[:, span], wo_v.at[:, span]))
    for j in range(XS):
        span = pl.ds(j * block, block)
        pairs.append((wq.at[span], wq_v.at[span]))
        pairs.append((wkv.at[span], wkv_v.at[span]))
    moves = copies(pairs, sems)
    for move in moves:
        move.start()
    mix_grad = jnp.zeros(q_in.shape, F32)
    for j in range(XS):
        moves[j].wait()
        mix_grad = mix_grad + dot(grads[j], wo_v[:, j * block : (j + 1) * block], ((1,), (1,)))
    mix_grad = mix_grad.astype(BF16)
    q = q_in[...]
    kv = kv_in[...]
    query_grads, pair_grads = [], []
    for row in range(rows):
        here = slice(row * length, (row + 1) * length)
        keys, values = kv[here, :HEAD_DIM], kv[here, HEAD_DIM:]
        attn = attn_in[row]
        mixed = heads_down(mix_grad, row, length)
        value_grad = dot(attn.astype(BF16), mixed, ((0,), (0,)))
        weight_grad = dot(mixed, values, ((1,), (1,)))
        score_grad = attn * (weight_grad - jnp.sum(weight_grad * attn, -1, keepdims=True))
        score_grad = (score_grad * HEAD_DIM ** (-0.5)).astype(BF16)
        query_grads.append(heads_across(dot(score_grad, keys).astype(BF16), length))
        key_grad = dot(score_grad, heads_down(q, row, length), ((0,), (0,)))
        pair_grads.append(jnp.concatenate([key_grad, value_grad], axis=1).astype(BF16))
    query_grad = jnp.concatenate(query_grads, axis=0)
    pair_grad = jnp.concatenate(pair_grads, axis=0)
    qg_out[...] = query_grad
    pg_out[...] = pair_grad
    scale = scale_in[...]
    if onward:
        correction = jnp.sum(query_grad.astype(F32) * q.astype(F32), -1, keepdims=True)
        correction += jnp.sum(pair_grad.astype(F32) * kv.astype(F32), -1, keepdims=True)
        pull = scale * scale / width * correction
    for j in range(XS):
        span = slice(j * block, (j + 1) * block)
        moves[XS + 2 * j].wait()
        moves[XS + 2 * j + 1].wait()
        normed_grad = dot(query_grad, wq_v[span, :], ((1,), (1,))) + dot(
            pair_grad, wkv_v[span, :], ((1,), (1,))
        )
        h = parts[j].astype(F32)
        scaled = normed_grad * scale
        gain_out[:, span] = jnp.sum(scaled * h, 0, keepdims=True)
        if onward:
            send[j] = (scaled * gain[:, span].astype(F32) - h * pull).astype(BF16)


def call(kernel, outs, scratch, sems, flops, args):
    specs = [SMEM if a.dtype == jnp.int32 else HBM if a.size > 2**20 - 1 else VMEM for a in args]
    return pl.pallas_call(
        kernel,
        out_shape=outs,
        in_specs=specs,
        out_specs=[VMEM] * len(outs),
        scratch_shapes=scratch + [pltpu.SemaphoreType.DMA((sems,))],
        compiler_params=pltpu.CompilerParams(vmem_limit_bytes=32 * 2**20),
        cost_estimate=pl.CostEstimate(flops=flops, bytes_accessed=12 * 2**20, transcendentals=2**16),
    )(*args)


def place(section, x, half):
    return (section * XS + x) * HALVES + half


def gather_x(spread):
    return lax.all_to_all(spread, "x", 0, 0)


def scatter_x(parts):
    return jnp.sum(lax.all_to_all(parts, "x", 0, 0).astype(F32), 0)


def hop(block, source, target):
    total = None
    for cross in range(HALVES):
        route = [
            (place(source, x, half), place(target, x, half ^ cross))
            for x in range(XS)
            for half in range(HALVES)
        ]
        got = lax.ppermute(block, ("s", "x", "zh"), route).astype(F32)
        total = got if total is None else total + got
    return jnp.broadcast_to(total.astype(BF16)[None], (XS,) + block.shape)


def pair_up(block, sections):
    route = [
        (place(s, x, half), place(s, x, 1 - half))
        for s in sections
        for x in range(XS)
        for half in range(HALVES)
    ]
    other = lax.ppermute(block, ("s", "x", "zh"), route)
    first = lax.axis_index("zh") == 0
    return jnp.concatenate([jnp.where(first, block, other), jnp.where(first, other, block)], -1)


def pick(items, station):
    chosen = items[0]
    for s in range(1, SECTIONS):
        chosen = jnp.where(station == s, items[s], chosen)
    return chosen


def shards(hidden_in, lengths, gains, w_query, w_keyval, w_out, grad_out):
    station = lax.axis_index("s")
    rows, length, shard = hidden_in.shape
    tokens = rows * length
    wq = w_query[0]
    width = wq.shape[0]
    wkv = w_keyval[0].reshape(width, -1)
    wo = w_out[0]
    block_width = width // XS
    qs, kvs = wq.shape[1], wkv.shape[1]
    flops = 2 * tokens * width * (2 * qs + kvs)
    tall = qs // HEAD_DIM * length

    start = jnp.where(
        station == 0, hidden_in.reshape(tokens, shard), grad_out.reshape(tokens, shard)
    )
    start = jnp.concatenate([start, jnp.broadcast_to(gains, (16, shard))], 0)
    start_block = pair_up(start, range(SECTIONS))
    start_full = gather_x(jnp.broadcast_to(start_block[None], (XS,) + start_block.shape))
    gain = start_full[:, tokens, :].reshape(1, width)
    first = start_full[:, :tokens]
    first_block = start_block[:tokens]

    shape = jax.ShapeDtypeStruct
    sent = shape((XS, tokens, block_width), BF16)
    saved = [
        shape((tokens, 1), F32),
        shape((tokens, qs), BF16),
        shape((tokens, kvs), BF16),
        shape((tokens, qs), BF16),
        shape((rows, tall, length), F32),
    ]
    held = [pltpu.VMEM((width, qs), BF16), pltpu.VMEM((width, kvs), BF16)]
    held_out = [pltpu.VMEM((qs, width), BF16)]

    kept = []
    parts, block = first, first_block
    for step in range(SECTIONS):
        if step:
            parts = gather_x(spread)
            block = spread[0]
        project = step + 1 < SECTIONS
        got = call(
            functools.partial(forward_kernel, rows, length, project),
            [sent] * project + saved,
            held + held_out * project,
            3 * XS,
            flops,
            (lengths, parts, gain, wq, wkv, wo),
        )
        kept.append((parts,) + tuple(got[project:]))
        if project:
            block = (0.5 * block.astype(F32) + scatter_x(got[0])).astype(BF16)
            spread = hop(block, step, step + 1)

    cut = lambda wide: wide.reshape(tokens, DP, width // DP).transpose(1, 0, 2)
    to_all = lambda narrow: jnp.broadcast_to(narrow[None], (DP,) + narrow.shape)
    half = width // DP
    over_dp = lambda v: lax.all_to_all(v, ("y", "core"), 0, 0)

    def early(items):
        picked, scale, mix = items
        gains_cut = gain.reshape(XS, 1, block_width).astype(F32)
        normed = (picked.astype(F32) * scale * gains_cut).astype(BF16)
        normed = normed.reshape(XS, tokens, 2, half).transpose(0, 2, 1, 3).reshape(DP, tokens, half)
        return over_dp(jnp.concatenate([normed, to_all(mix)], -1))

    def items_at(step):
        return kept[step][0], kept[step][1], kept[step][4]

    chosen = [
        jnp.where(station == 0, a, jnp.where(station == 1, b, c))
        for a, b, c in zip(items_at(0), items_at(1), items_at(2))
    ]
    factors = lax.cond(
        station < SECTIONS - 1,
        early,
        lambda items: jnp.zeros((DP, tokens, half + qs), BF16),
        chosen,
    )

    parts_grad, block = first, first_block
    last = None
    for step in reversed(range(SECTIONS)):
        if step + 1 < SECTIONS:
            parts_grad = gather_x(spread)
            block = spread[0]
        parts, scale, q, kv, mix, attn = kept[step]
        onward = step > 0
        got = call(
            functools.partial(backward_kernel, rows, length, onward),
            [sent] * onward
            + [shape((tokens, qs), BF16), shape((tokens, kvs), BF16), shape((1, width), F32)],
            held + held_out,
            3 * XS,
            flops,
            (parts_grad, parts, gain, scale, q, kv, attn, wq, wkv, wo),
        )
        found = (parts_grad,) + tuple(got[onward:])
        last = found if last is None else [jnp.where(station == step, a, b) for a, b in zip(found, last)]
        if onward:
            block = (0.5 * block.astype(F32) + scatter_x(got[0])).astype(BF16)
            spread = hop(block, step, step - 1)
        if step == SECTIONS - 1:
            factors = lax.cond(
                station == SECTIONS - 1, lambda items, kept_factors: early(items),
                lambda items, kept_factors: kept_factors, items_at(step), factors,
            )

    parts_grad, query_grad, pair_grad, gain_part = last
    send_g = parts_grad.reshape(XS, tokens, 2, half).transpose(0, 2, 1, 3).reshape(DP, tokens, half)
    full_grad = over_dp(send_g).reshape(DP * tokens, half)
    piece = width // (DP * XS * HALVES)
    pieces = gain_part.reshape(XS * HALVES, DP, piece).transpose(1, 0, 2).reshape(DP, 1, half)
    high = pieces.astype(BF16)
    low = (pieces - high.astype(F32)).astype(BF16)
    extra = jnp.concatenate([high, low, jnp.zeros((DP, 14, half), BF16)], 1)
    extra = jnp.concatenate([extra, jnp.zeros((DP, 16, qs + kvs - half), BF16)], -1)
    pair = jnp.concatenate([to_all(query_grad), to_all(pair_grad)], -1)
    got = over_dp(jnp.concatenate([pair, extra], 1))
    pieces = jnp.sum(got[:, tokens : tokens + 2, :half].astype(F32), (0, 1)).reshape(XS * HALVES, 1, piece)
    gain_grad = jnp.sum(lax.all_to_all(pieces, ("x", "zh"), 0, 0), 0)
    pair = got[:, :tokens].reshape(DP * tokens, -1)
    normed = factors[:, :, :half].reshape(DP * tokens, half)
    mix = factors[:, :, half:].reshape(DP * tokens, qs)
    grad_out_weight = dot(mix, full_grad, ((0,), (0,)))
    grad_query = dot(normed, pair[:, :qs], ((0,), (0,)))
    grad_pair = dot(normed, pair[:, qs:], ((0,), (0,)))
    return (
        grad_query[None],
        grad_pair.reshape(1, half, 1, -1),
        grad_out_weight[None],
        gain_grad[None][:, 0],
    )


def solution(mesh):
    grid = Mesh(mesh.devices.reshape(SECTIONS, XS, HALVES, 4, 2), ("s", "x", "zh", "y", "core"))
    section, tensor, dp = "s", ("x", "zh"), ("y", "core")
    in_specs = (
        P(dp, None, tensor),
        P(dp),
        P(section, tensor),
        P(section, None, tensor),
        P(section, None, tensor, None),
        P(section, tensor, None),
        P(dp, None, tensor),
    )
    out_specs = (
        P(section, dp, tensor),
        P(section, dp, tensor, None),
        P(section, tensor, dp),
        P(section, tensor + dp),
    )
    return jax.shard_map(shards, mesh=grid, in_specs=in_specs, out_specs=out_specs, check_vma=False)
```

time: 517 us -> 443 us (0.86)
  the two profiles are of different devices: /device:TPU:1 before, /device:TPU:32 now
where the time goes in v2:
time: 443 us; the launch traced here: 435 us
  blocking collectives  210 us (47%)
  waiting for transfers between devices  80.5 us (18%)
  Pallas kernels  50.8 us (11%)
  starting transfers between devices  38.7 us (9%)
  local copies, waits for them, and re-layouts  30 us (7%)
  other arithmetic  15.2 us (3%)
  matrix products  7.85 us (2%)
    all_to_all x6, blocking collectives, gather_x(): return lax.all_to_all(spread, 'x', 0, 0)  91.4 us
    all_to_all x6, blocking collectives, scatter_x(): return jnp.sum(lax.all_to_all(parts, 'x', 0, 0).astype(F32), 0)  86.3 us
    pallas_call x8, Pallas kernels, call(): pl.pallas_call(kernel, out_shape=outs, in_specs=specs, out_specs=[VMEM] *...  50.8 us
    ppermute x12, waiting for transfers between devices, hop(): got = lax.ppermute(block, ('s', 'x', 'zh'), route).astype(F32)  37.2 us
    all_to_all x1, blocking collectives, shards(): over_dp = lambda v: lax.all_to_all(v, ('y', 'core'), 0, 0)  31.9 us
    all_to_all x2, waiting for transfers between devices, shards(): over_dp = lambda v: lax.all_to_all(v, ('y', 'core'), 0, 0)  19.4 us
    ppermute x12, starting transfers between devices, hop(): got = lax.ppermute(block, ('s', 'x', 'zh'), route).astype(F32)  14.5 us
    all_to_all x1, waiting for transfers between devices, gather_x(): return lax.all_to_all(spread, 'x', 0, 0)  14.4 us
  transfers between devices with their start and end apart: 17, of which 10 were waited for; matrix products, arithmetic and copies ran while one was open for 7% of the time, Pallas kernels for 2%

profile of v2, /device:TPU:32, one launch (start us, length us, event | category | flops | bytes accessed | tf_op | source)
XLA Modules:
  0.0 434.8 jit_solution(12909141976092078035)
XLA Ops:
  2.3 6.4 %collective-permute-start = (bf16[144,512]{1,0:T(8,128)(2,1)S(1)}, bf16[144,512]{1,0:T(8,128)(2,1)S(1)}, u32[]{:S(2)}, u32[]{:S(2)}) collective-permute-start(bf16[144,512]{1,0:T(8,128)(2,1)S(1)} %pad_maximum_fusion.7), channel_id=1, source_target_pairs={{0,8},{8,0},{16,24},{24,16},{32,40},{40,32},{48,56},{56,48},{64,72... | collective-permute-start | bytes 442376 | tf_op jit(solution)/shard_map/ppermute | solution.py:211
  8.7 7.1 %collective-permute-done = bf16[144,512]{1,0:T(8,128)(2,1)S(1)} collective-permute-done((bf16[144,512]{1,0:T(8,128)(2,1)S(1)}, bf16[144,512]{1,0:T(8,128)(2,1)S(1)}, u32[]{:S(2)}, u32[]{:S(2)}) %collective-permute-start) | collective-permute-done | bytes 147488 | tf_op jit(solution)/shard_map/ppermute | solution.py:211
  16.0 20.2 %all_to_all.90 = bf16[4,144,1024]{2,1,0:T(8,128)(2,1)S(1)} all-to-all(bf16[4,144,1024]{2,1,0:T(8,128)(2,1)S(1)} %broadcast_in_dim.39), channel_id=1, replica_groups=mesh['s'=4,'x'=4,'zh'=2,'y'=4,'core'=2] {'x'}, dimensions={0} | all-to-all | bytes 2359296 | tf_op jit(solution)/shard_map/all_to_all | solution.py:184
  36.4 2.9 copy-done.2
  39.2 6.4 %shard_map.102 = (bf16[4,128,1024]{2,1,0:T(8,128)(2,1)S(1)}, f32[128,1]{1,0:T(8,128)}, bf16[128,512]{1,0:T(8,128)(2,1)S(1)}, bf16[128,256]{1,0:T(8,128)(2,1)S(1)...) custom-call(s32[2]{0:T(128)S(1)} %copy-done.25, bf16[4,128,1024]{2,1,0:T(8,128)(2,1)S(1)} %slice.72.parts.grads, ...), custom_call_target="tpu_custom_call" | custom-call | flops 1342177280 | bytes 12582912 | tf_op jit(solution)/shard_map/pallas_call | solution.py:168
  45.6 16.0 %all_to_all.91 = bf16[4,128,1024]{2,1,0:T(8,128)(2,1)S(1)} all-to-all(bf16[4,128,1024]{2,1,0:T(8,128)(2,1)S(1)} %get-tuple-element.84), channel_id=1, replica_groups=mesh['s'=4,'x'=4,'zh'=2,'y'=4,'core'=2] {'x'}, dimensions={0} | all-to-all | bytes 2097152 | tf_op jit(solution)/shard_map/all_to_all | solution.py:188
  61.9 1.3 collective-permute-start.2
  63.1 1.3 collective-permute-start.1
  64.5 8.7 %collective-permute-done.2 = bf16[128,1024]{1,0:T(8,128)(2,1)S(1)} collective-permute-done((bf16[128,1024]{1,0:T(8,128)(2,1)S(1)}, bf16[128,1024]{1,0:T(8,128)(2,1)S(1)}, u32[]{:S(2)}, u32[]{:S(2)}) %collective-permute-start.2) | collective-permute-done | bytes 262176 | tf_op jit(solution)/shard_map/ppermute | solution.py:199
  73.1 2.0 collective-permute-done.1
  75.3 13.7 %all_to_all.92.parts = bf16[4,128,1024]{2,1,0:T(8,128)(2,1)S(1)} all-to-all(bf16[4,128,1024]{2,1,0:T(8,128)(2,1)S(1)} %broadcast_in_dim.45), channel_id=1, replica_groups=mesh['s'=4,'x'=4,'zh'=2,'y'=4,'core'=2] {'x'}, dimensions={0} | all-to-all | bytes 2097152 | tf_op jit(solution)/shard_map/all_to_all | solution.py:184
  89.0 6.3 %shard_map.103 = (bf16[4,128,1024]{2,1,0:T(8,128)(2,1)S(1)}, f32[128,1]{1,0:T(8,128)S(1)}, bf16[128,512]{1,0:T(8,128)(2,1)S(1)}, bf16[128,256]{1,0:T(8,128)(2,1)...) custom-call(s32[2]{0:T(128)S(1)} %copy-done.25, bf16[4,128,1024]{2,1,0:T(8,128)(2,1)S(1)} %all_to_all.92.parts, ...), custom_call_target="tpu_custom_call" | custom-call | flops 1342177280 | bytes 12582912 | tf_op jit(solution)/shard_map/pallas_call | solution.py:168
  95.4 13.3 %all_to_all.93 = bf16[4,128,1024]{2,1,0:T(8,128)(2,1)S(1)} all-to-all(bf16[4,128,1024]{2,1,0:T(8,128)(2,1)S(1)} %get-tuple-element.85), channel_id=1, replica_groups=mesh['s'=4,'x'=4,'zh'=2,'y'=4,'core'=2] {'x'}, dimensions={0} | all-to-all | bytes 2097152 | tf_op jit(solution)/shard_map/all_to_all | solution.py:188
  108.9 1.3 collective-permute-start.4
  110.2 1.3 collective-permute-start.3
  111.6 2.5 collective-permute-done.4
  114.1 1.3 collective-permute-done.3
  115.6 13.5 %all_to_all.94.parts = bf16[4,128,1024]{2,1,0:T(8,128)(2,1)S(1)} all-to-all(bf16[4,128,1024]{2,1,0:T(8,128)(2,1)S(1)} %broadcast_in_dim.46), channel_id=1, replica_groups=mesh['s'=4,'x'=4,'zh'=2,'y'=4,'core'=2] {'x'}, dimensions={0} | all-to-all | bytes 2097152 | tf_op jit(solution)/shard_map/all_to_all | solution.py:184
  129.1 6.3 %shard_map.104 = (bf16[4,128,1024]{2,1,0:T(8,128)(2,1)S(1)}, f32[128,1]{1,0:T(8,128)S(1)}, bf16[128,512]{1,0:T(8,128)(2,1)S(1)}, bf16[128,256]{1,0:T(8,128)(2,1)...) custom-call(s32[2]{0:T(128)S(1)} %copy-done.25, bf16[4,128,1024]{2,1,0:T(8,128)(2,1)S(1)} %all_to_all.94.parts, ...), custom_call_target="tpu_custom_call" | custom-call | flops 1342177280 | bytes 12582912 | tf_op jit(solution)/shard_map/pallas_call | solution.py:168
  135.4 14.2 %all_to_all.95 = bf16[4,128,1024]{2,1,0:T(8,128)(2,1)S(1)} all-to-all(bf16[4,128,1024]{2,1,0:T(8,128)(2,1)S(1)} %get-tuple-element.92), channel_id=1, replica_groups=mesh['s'=4,'x'=4,'zh'=2,'y'=4,'core'=2] {'x'}, dimensions={0} | all-to-all | bytes 2097152 | tf_op jit(solution)/shard_map/all_to_all | solution.py:188
  151.5 13.3 %all_to_all.96.parts = bf16[4,128,1024]{2,1,0:T(8,128)(2,1)S(1)} all-to-all(bf16[4,128,1024]{2,1,0:T(8,128)(2,1)S(1)} %broadcast_in_dim.47), channel_id=1, replica_groups=mesh['s'=4,'x'=4,'zh'=2,'y'=4,'core'=2] {'x'}, dimensions={0} | all-to-all | bytes 2097152 | tf_op jit(solution)/shard_map/all_to_all | solution.py:184
  164.8 4.8 %shard_map.105 = (f32[128,1]{1,0:T(8,128)S(1)}, bf16[128,512]{1,0:T(8,128)(2,1)S(1)}, bf16[128,256]{1,0:T(8,128)(2,1)S(1)}, bf16[128,512]{1,0:T(8,128)(2,1)}, f32[2,256,64]{2,1,0:T(8,128)S(1)}) custom-call(s32[2]{0:T(128)S(1)} %copy-done.25, bf16[4,128,1024]{2,1,0:T(8,128)(2,1)S(1)} %all_to_all.96.parts, bf16[1,4096]{1,0:T(2,128)(2,1)S(1)} %bitcast.65, ...), custom_call_target="tpu_custom_call" | custom-call | flops 1342177280 | bytes 12582912 | tf_op jit(solution)/shard_map/pallas_call | solution.py:168
  169.7 6.3 %shard_map.106 = (bf16[4,128,1024]{2,1,0:T(8,128)(2,1)S(1)}, bf16[128,512]{1,0:T(8,128)(2,1)S(1)}, bf16[128,256]{1,0:T(8,128)(2,1)S(1)}, f32[1,4096]{1,0:T(1,128)S(1)}) custom-call(bf16[4,128,1024]{2,1,0:T(8,128)(2,1)S(1)} %slice.72.parts.grads, bf16[4,128,1024]{2,1,0:T(8,128)(2,1)S(1)} %all_to_all.96.parts, bf16[1,4096]{1,0:T(2,128)(2,1)S(1)} %bitcast.66, ...), custom_call_target="tpu_custom_call" | custom-call | flops 1342177280 | bytes 12582912 | tf_op jit(solution)/shard_map/pallas_call | solution.py:168
  176.0 16.2 %all_to_all.97 = bf16[4,128,1024]{2,1,0:T(8,128)(2,1)S(1)} all-to-all(bf16[4,128,1024]{2,1,0:T(8,128)(2,1)S(1)} %get-tuple-element.99), channel_id=1, replica_groups=mesh['s'=4,'x'=4,'zh'=2,'y'=4,'core'=2] {'x'}, dimensions={0} | all-to-all | bytes 2097152 | tf_op jit(solution)/shard_map/all_to_all | solution.py:188
  194.1 13.5 %all_to_all.98.grads = bf16[4,128,1024]{2,1,0:T(8,128)(2,1)S(1)} all-to-all(bf16[4,128,1024]{2,1,0:T(8,128)(2,1)S(1)} %broadcast_in_dim.48), channel_id=1, replica_groups=mesh['s'=4,'x'=4,'zh'=2,'y'=4,'core'=2] {'x'}, dimensions={0} | all-to-all | bytes 2097152 | tf_op jit(solution)/shard_map/all_to_all | solution.py:184
  207.6 6.3 %shard_map.107 = (bf16[4,128,1024]{2,1,0:T(8,128)(2,1)S(1)}, bf16[128,512]{1,0:T(8,128)(2,1)S(1)}, bf16[128,256]{1,0:T(8,128)(2,1)S(1)}, f32[1,4096]{1,0:T(1,128)S(1)}) custom-call(bf16[4,128,1024]{2,1,0:T(8,128)(2,1)S(1)} %all_to_all.98.grads, bf16[4,128,1024]{2,1,0:T(8,128)(2,1)S(1)} %all_to_all.94.parts, bf16[1,4096]{1,0:T(2,128)(2,1)S(1)} %bitcast.67, ...), custom_call_target="tpu_custom_call" | custom-call | flops 1342177280 | bytes 12582912 | tf_op jit(solution)/shard_map/pallas_call | solution.py:168
  213.9 13.3 %all_to_all.99 = bf16[4,128,1024]{2,1,0:T(8,128)(2,1)S(1)} all-to-all(bf16[4,128,1024]{2,1,0:T(8,128)(2,1)S(1)} %get-tuple-element.103), channel_id=1, replica_groups=mesh['s'=4,'x'=4,'zh'=2,'y'=4,'core'=2] {'x'}, dimensions={0} | all-to-all | bytes 2097152 | tf_op jit(solution)/shard_map/all_to_all | solution.py:188
  227.5 1.3 collective-permute-start.10
  228.8 1.3 collective-permute-start.9
  230.1 22.6 %collective-permute-done.10 = bf16[128,1024]{1,0:T(8,128)(2,1)S(1)} collective-permute-done((bf16[128,1024]{1,0:T(8,128)(2,1)S(1)}, bf16[128,1024]{1,0:T(8,128)(2,1)S(1)}, u32[]{:S(2)}, u32[]{:S(2)}) %collective-permute-start.10) | collective-permute-done | bytes 262176 | tf_op jit(solution)/shard_map/ppermute | solution.py:199
  253.0 17.2 %all_to_all.100.grads = bf16[4,128,1024]{2,1,0:T(8,128)(2,1)S(1)} all-to-all(bf16[4,128,1024]{2,1,0:T(8,128)(2,1)S(1)} %broadcast_in_dim.49), channel_id=1, replica_groups=mesh['s'=4,'x'=4,'zh'=2,'y'=4,'core'=2] {'x'}, dimensions={0} | all-to-all | bytes 2097152 | tf_op jit(solution)/shard_map/all_to_all | solution.py:184
  270.2 6.3 %shard_map.108 = (bf16[4,128,1024]{2,1,0:T(8,128)(2,1)S(1)}, bf16[128,512]{1,0:T(8,128)(2,1)S(1)}, bf16[128,256]{1,0:T(8,128)(2,1)S(1)}, f32[1,4096]{1,0:T(1,128)S(1)}) custom-call(bf16[4,128,1024]{2,1,0:T(8,128)(2,1)S(1)} %all_to_all.100.grads, bf16[4,128,1024]{2,1,0:T(8,128)(2,1)S(1)} %all_to_all.92.parts, bf16[1,4096]{1,0:T(2,128)(2,1)S(1)} %bitcast.68, ...), custom_call_target="tpu_custom_call" | custom-call | flops 1342177280 | bytes 12582912 | tf_op jit(solution)/shard_map/pallas_call | solution.py:168
  276.5 13.3 %all_to_all.101 = bf16[4,128,1024]{2,1,0:T(8,128)(2,1)S(1)} all-to-all(bf16[4,128,1024]{2,1,0:T(8,128)(2,1)S(1)} %get-tuple-element.107), channel_id=1, replica_groups=mesh['s'=4,'x'=4,'zh'=2,'y'=4,'core'=2] {'x'}, dimensions={0} | all-to-all | bytes 2097152 | tf_op jit(solution)/shard_map/all_to_all | solution.py:188
  290.8 2.0 collective-permute-start.12
  292.8 2.0 collective-permute-start.11
  298.0 42.2 %conditional.2 = (bf16[8,128,1024]{2,1,0:T(8,128)(2,1)}) conditional(s32[]{:T(128)} %convert_element_type.167, () %tuple.32, (pred[4,128,1024]{2,1,0:T(8,128)(4,1)}, pred[]{:T(512)}, bf16[4,1,1024]{2,1,0:T(2,128)(2,1)}, pred[128,512]{1,0:T(8,128)(4,1)}, bf16[4,128,1024]{2,1,0:T(8,128)(2,1)}, /*index=5*/pred[4,128,1024]{2,1,0:T(8,128)(4,1)}, ...), branch_computations={%region_2.3_spmd, %region_3.4_spmd} | conditional | flops 9572608 | bytes 21804694 | solution.py:297
  298.0 1.4 copy.78
  299.4 1.5 copy.77
  300.9 1.4 copy.76
  303.7 3.0 multiply_convert_fusion
  308.3 31.9 %all_to_all.88 = bf16[8,128,1024]{2,1,0:T(8,128)(2,1)} all-to-all(bf16[8,128,1024]{2,1,0:T(8,128)(2,1)S(1)} %pad_maximum_fusion), channel_id=1, replica_groups=mesh['s'=4,'x'=4,'zh'=2,'y'=4,'core'=2] {'y','core'}, dimensions={0} | all-to-all | bytes 4194304 | tf_op jit(solution)/shard_map/cond/branch_1_fun/all_to_all | solution.py:281
  340.2 4.5 %conditional.3 = (bf16[8,128,1024]{2,1,0:T(8,128)(2,1)}, bf16[8,128,512]{2,1,0:T(8,128)(2,1)}, bf16[1024,512]{1,0:T(8,128)(2,1)}) conditional(s32[]{:T(128)} %convert_element_type.166, bf16[8,128,1024]{2,1,0:T(8,128)(2,1)} %get-tuple-element.341, (bf16[4,128,1024]{2,1,0:T(8,128)(2,1)}, f32[128,1]{1,0:T(8,128)}, bf16[4,1,1024]{2,1,0:T(2,128)(2,1)}, ...), branch_computations={%region_5.6_spmd, %region_6.7_spmd} | conditional | flops 8392704 | bytes 29009488 | solution.py:327
  340.2 2.3 slice.42
  342.4 2.3 copy.104
  345.8 1.1 broadcast_in_dim.50
  346.9 4.5 %all-to-all-start.14 = ((bf16[4,128,1024]{2,1,0:T(8,128)(2,1)}), bf16[4,128,1024]{2,1,0:T(8,128)(2,1)}, u32[]{:S(2)}, u32[]{:S(2)}) async-start(bf16[4,128,1024]{2,1,0:T(8,128)(2,1)} %broadcast_in_dim.50), calls=%async_computation.14 | async-start | bytes 2097152 | tf_op jit(solution)/shard_map/all_to_all | solution.py:184
  352.0 14.4 %all-to-all-done.14.grads = bf16[4,128,1024]{2,1,0:T(8,128)(2,1)} async-done(((bf16[4,128,1024]{2,1,0:T(8,128)(2,1)}), bf16[4,128,1024]{2,1,0:T(8,128)(2,1)}, u32[]{:S(2)}, u32[]{:S(2)}) %all-to-all-start.14) | async-done | bytes 1048608 | tf_op jit(solution)/shard_map/all_to_all | solution.py:184
  366.5 1.7 select_select_fusion.2
  369.4 4.3 all-to-all-start.16
  373.7 2.2 copy-done.1
  375.8 2.2 copy-done.4
  378.1 8.1 %shard_map.109 = (bf16[128,512]{1,0:T(8,128)(2,1)S(1)}, bf16[128,256]{1,0:T(8,128)(2,1)S(1)}, f32[1,4096]{1,0:T(1,128)S(1)}) custom-call(bf16[4,128,1024]{2,1,0:T(8,128)(2,1)} %all-to-all-done.14.grads, bf16[4,128,1024]{2,1,0:T(8,128)(2,1)} %copy-done.26, bf16[1,4096]{1,0:T(2,128)(2,1)S(1)} %bitcast.69, f32[128,1]{1,0:T(8,128)S(1)} %copy-done.35, ...), custom_call_target="tpu_custom_call" | custom-call | flops 1342177280 | bytes 12582912 | tf_op jit(solution)/shard_map/pallas_call | solution.py:168
  386.8 1.4 fusion.2
  388.2 1.4 all-to-all-done.16
  389.6 4.3 all-to-all-start.15
  393.9 2.4 copy.84
  396.4 3.2 convolution_bitcast_fusion
  399.6 18.0 %all-to-all-done.15 = bf16[8,144,768]{2,1,0:T(8,128)(2,1)} async-done(((bf16[8,144,768]{2,1,0:T(8,128)(2,1)}), bf16[8,144,768]{2,1,0:T(8,128)(2,1)}, u32[]{:S(2)}, u32[]{:S(2)}) %all-to-all-start.15) | async-done | bytes 1769504 | tf_op jit(solution)/shard_map/all_to_all | solution.py:281
  419.2 4.7 %all-to-all-start.17 = ((f32[8,1,64]{2,1,0:T(1,128)}), f32[8,1,64]{2,1,0:T(1,128)S(1)}, u32[]{:S(2)}, u32[]{:S(2)}) async-start(f32[8,1,64]{2,1,0:T(1,128)} %reshape.106), calls=%async_computation.17 | async-start | bytes 8192 | tf_op jit(solution)/shard_map/all_to_all | solution.py:344
  423.9 1.5 slice.75
  425.4 2.9 convolution_bitcast_fusion.1
  428.3 1.7 convolution_bitcast_fusion.2
  430.1 1.3 copy.87
  431.4 2.4 all-to-all-done.17
  (158 shorter events, 19.3 us)
Async XLA Ops:
  2.3 13.4 %collective-permute-start = (bf16[144,512]{1,0:T(8,128)(2,1)S(1)}, bf16[144,512]{1,0:T(8,128)(2,1)S(1)}, u32[]{:S(2)}, u32[]{:S(2)}) collective-permute-start(bf16[144,512]{1,0:T(8,128)(2,1)S(1)} %pad_maximum_fusion.7), channel_id=1, source_target_pairs={{0,8},{8,0},{16,24},{24,16},{32,40},{40,32},{48,56},{56,48},{64,72... | collective-permute-start | bytes 442376 | tf_op jit(solution)/shard_map/ppermute | solution.py:211
  15.8 20.6 %copy-start.5 = (bf16[1,4096,1,256]{3,1,2,0:T(8,128)(2,1)S(1)}, bf16[1,4096,1,256]{3,1,2,0:T(8,128)(2,1)}, u32[]{:S(2)}) copy-start(bf16[1,4096,1,256]{3,1,2,0:T(8,128)(2,1)} %param.15) | copy-start | bytes 6291460
  16.0 20.4 %copy-start = (bf16[1,4096,512]{2,1,0:T(8,128)(2,1)S(1)}, bf16[1,4096,512]{2,1,0:T(8,128)(2,1)}, u32[]{:S(2)}) copy-start(bf16[1,4096,512]{2,1,0:T(8,128)(2,1)} %param.14) | copy-start | bytes 12582916
  16.0 20.4 %copy-start.25 = (s32[2]{0:T(128)S(1)}, s32[2]{0:T(128)}, u32[]{:S(2)}) copy-start(s32[2]{0:T(128)} %lens.7) | copy-start | bytes 28
  36.2 9.4 %copy-start.32 = (bf16[4,144,1024]{2,1,0:T(8,128)(2,1)}, bf16[4,144,1024]{2,1,0:T(8,128)(2,1)S(1)}, u32[]{:S(2)}) copy-start(bf16[4,144,1024]{2,1,0:T(8,128)(2,1)S(1)} %all_to_all.90) | copy-start | bytes 3538948
  36.2 233.9 %copy-start.33 = (bf16[4,1,1024]{2,1,0:T(2,128)(2,1)}, bf16[4,1,1024]{2,1,0:T(2,128)(2,1)S(1)}, u32[]{:S(2)}) copy-start(bf16[4,1,1024]{2,1,0:T(2,128)(2,1)S(1)} %slice.71) | copy-start | bytes 24580
  36.3 133.4 %copy-start.26 = (bf16[4,128,1024]{2,1,0:T(8,128)(2,1)}, bf16[4,128,1024]{2,1,0:T(8,128)(2,1)S(1)}, u32[]{:S(2)}) copy-start(bf16[4,128,1024]{2,1,0:T(8,128)(2,1)S(1)} %slice.72.parts.grads) | copy-start | bytes 3145732
  36.4 2.9 copy-start.2
  45.6 16.2 %copy-start.13 = (bf16[128,256]{1,0:T(8,128)(2,1)}, bf16[128,256]{1,0:T(8,128)(2,1)S(1)}, u32[]{:S(2)}) copy-start(bf16[128,256]{1,0:T(8,128)(2,1)S(1)} %get-tuple-element.109.kv_in) | copy-start | bytes 196612
  61.9 11.3 %collective-permute-start.2 = (bf16[128,1024]{1,0:T(8,128)(2,1)S(1)}, bf16[128,1024]{1,0:T(8,128)(2,1)S(1)}, u32[]{:S(2)}, u32[]{:S(2)}) collective-permute-start(bf16[128,1024]{1,0:T(8,128)(2,1)S(1)} %add_convert_fusion.11), channel_id=1, source_target_pairs={{0,72},{8,64},{16,88},{24,80},{32,104},{40,96},{48,120},{56,112},{... | collective-permute-start | bytes 786440 | tf_op jit(solution)/shard_map/ppermute | solution.py:199
  63.1 12.0 %collective-permute-start.1 = (bf16[128,1024]{1,0:T(8,128)(2,1)S(1)}, bf16[128,1024]{1,0:T(8,128)(2,1)S(1)}, u32[]{:S(2)}, u32[]{:S(2)}) collective-permute-start(bf16[128,1024]{1,0:T(8,128)(2,1)S(1)} %add_convert_fusion.11), channel_id=1, source_target_pairs={{0,64},{8,72},{16,80},{24,88},{32,96},{40,104},{48,112},{56,120},{... | collective-permute-start | bytes 786440 | tf_op jit(solution)/shard_map/ppermute | solution.py:199
  89.0 181.1 %copy-start.30 = (bf16[4,128,1024]{2,1,0:T(8,128)(2,1)}, bf16[4,128,1024]{2,1,0:T(8,128)(2,1)S(1)}, u32[]{:S(2)}) copy-start(bf16[4,128,1024]{2,1,0:T(8,128)(2,1)S(1)} %all_to_all.92.parts) | copy-start | bytes 3145732
  95.3 174.8 %copy-start.36 = (f32[128,1]{1,0:T(8,128)}, f32[128,1]{1,0:T(8,128)S(1)}, u32[]{:S(2)}) copy-start(f32[128,1]{1,0:T(8,128)S(1)} %get-tuple-element.87.scale_in) | copy-start | bytes 1540
  108.9 5.2 %collective-permute-start.4 = (bf16[128,1024]{1,0:T(8,128)(2,1)S(1)}, bf16[128,1024]{1,0:T(8,128)(2,1)S(1)}, u32[]{:S(2)}, u32[]{:S(2)}) collective-permute-start(bf16[128,1024]{1,0:T(8,128)(2,1)S(1)} %add_convert_fusion.9), channel_id=1, source_target_pairs={{64,136},{72,128},{80,152},{88,144},{96,168},{104,160},{112,184},{... | collective-permute-start | bytes 786440 | tf_op jit(solution)/shard_map/ppermute | solution.py:199
  110.2 5.2 %collective-permute-start.3 = (bf16[128,1024]{1,0:T(8,128)(2,1)S(1)}, bf16[128,1024]{1,0:T(8,128)(2,1)S(1)}, u32[]{:S(2)}, u32[]{:S(2)}) collective-permute-start(bf16[128,1024]{1,0:T(8,128)(2,1)S(1)} %add_convert_fusion.9), channel_id=1, source_target_pairs={{64,128},{72,136},{80,144},{88,152},{96,160},{104,168},{112,176},{... | collective-permute-start | bytes 786440 | tf_op jit(solution)/shard_map/ppermute | solution.py:199
  129.1 78.5 %copy-start.31 = (bf16[4,128,1024]{2,1,0:T(8,128)(2,1)}, bf16[4,128,1024]{2,1,0:T(8,128)(2,1)S(1)}, u32[]{:S(2)}) copy-start(bf16[4,128,1024]{2,1,0:T(8,128)(2,1)S(1)} %all_to_all.94.parts) | copy-start | bytes 3145732
  135.4 72.2 %copy-start.38 = (f32[128,1]{1,0:T(8,128)}, f32[128,1]{1,0:T(8,128)S(1)}, u32[]{:S(2)}) copy-start(f32[128,1]{1,0:T(8,128)S(1)} %get-tuple-element.88.scale_in) | copy-start | bytes 1540
  149.9 1.4 collective-permute-start.6
  150.6 0.7 collective-permute-start.5
  164.8 11.2 %copy-start.29 = (bf16[4,128,1024]{2,1,0:T(8,128)(2,1)}, bf16[4,128,1024]{2,1,0:T(8,128)(2,1)S(1)}, u32[]{:S(2)}) copy-start(bf16[4,128,1024]{2,1,0:T(8,128)(2,1)S(1)} %all_to_all.96.parts) | copy-start | bytes 3145732
  164.8 4.9 %copy-start.3 = (bf16[1,512,4096]{2,1,0:T(8,128)(2,1)S(1)}, bf16[1,512,4096]{2,1,0:T(8,128)(2,1)}, u32[]{:S(2)}) copy-start(bf16[1,512,4096]{2,1,0:T(8,128)(2,1)} %param.16) | copy-start | bytes 12582916
  169.7 6.3 %copy-start.37 = (f32[128,1]{1,0:T(8,128)}, f32[128,1]{1,0:T(8,128)S(1)}, u32[]{:S(2)}) copy-start(f32[128,1]{1,0:T(8,128)S(1)} %get-tuple-element.93.scale_in) | copy-start | bytes 1540
  176.0 16.5 %copy-start.7 = (bf16[128,512]{1,0:T(8,128)(2,1)}, bf16[128,512]{1,0:T(8,128)(2,1)S(1)}, u32[]{:S(2)}) copy-start(bf16[128,512]{1,0:T(8,128)(2,1)S(1)} %get-tuple-element.114) | copy-start | bytes 393220
  176.0 16.5 %copy-start.15 = (bf16[128,256]{1,0:T(8,128)(2,1)}, bf16[128,256]{1,0:T(8,128)(2,1)S(1)}, u32[]{:S(2)}) copy-start(bf16[128,256]{1,0:T(8,128)(2,1)S(1)} %get-tuple-element.118) | copy-start | bytes 196612
  192.5 1.4 collective-permute-start.8
  193.2 0.7 collective-permute-start.7
  213.9 13.6 %copy-start.9 = (bf16[128,512]{1,0:T(8,128)(2,1)}, bf16[128,512]{1,0:T(8,128)(2,1)S(1)}, u32[]{:S(2)}) copy-start(bf16[128,512]{1,0:T(8,128)(2,1)S(1)} %get-tuple-element.113) | copy-start | bytes 393220
  213.9 13.6 %copy-start.17 = (bf16[128,256]{1,0:T(8,128)(2,1)}, bf16[128,256]{1,0:T(8,128)(2,1)S(1)}, u32[]{:S(2)}) copy-start(bf16[128,256]{1,0:T(8,128)(2,1)S(1)} %get-tuple-element.117) | copy-start | bytes 196612
  213.9 13.6 %copy-start.21 = (f32[1,4096]{1,0:T(1,128)}, f32[1,4096]{1,0:T(1,128)S(1)}, u32[]{:S(2)}) copy-start(f32[1,4096]{1,0:T(1,128)S(1)} %get-tuple-element.121) | copy-start | bytes 49156
  227.5 25.2 %collective-permute-start.10 = (bf16[128,1024]{1,0:T(8,128)(2,1)S(1)}, bf16[128,1024]{1,0:T(8,128)(2,1)S(1)}, u32[]{:S(2)}, u32[]{:S(2)}) collective-permute-start(bf16[128,1024]{1,0:T(8,128)(2,1)S(1)} %add_convert_fusion.3), channel_id=1, source_target_pairs={{128,72},{136,64},{144,88},{152,80},{160,104},{168,96},{176,120},{... | collective-permute-start | bytes 786440 | tf_op jit(solution)/shard_map/ppermute | solution.py:199
  228.8 23.9 %collective-permute-start.9 = (bf16[128,1024]{1,0:T(8,128)(2,1)S(1)}, bf16[128,1024]{1,0:T(8,128)(2,1)S(1)}, u32[]{:S(2)}, u32[]{:S(2)}) collective-permute-start(bf16[128,1024]{1,0:T(8,128)(2,1)S(1)} %add_convert_fusion.3), channel_id=1, source_target_pairs={{128,64},{136,72},{144,80},{152,88},{160,96},{168,104},{176,112},{... | collective-permute-start | bytes 786440 | tf_op jit(solution)/shard_map/ppermute | solution.py:199
  270.1 6.3 %copy-start.6 = (bf16[4,128,1024]{2,1,0:T(8,128)(2,1)}, bf16[4,128,1024]{2,1,0:T(8,128)(2,1)S(1)}, u32[]{:S(2)}) copy-start(bf16[4,128,1024]{2,1,0:T(8,128)(2,1)S(1)} %all_to_all.100.grads) | copy-start | bytes 3145732
  276.4 14.3 %copy-start.11 = (bf16[128,512]{1,0:T(8,128)(2,1)}, bf16[128,512]{1,0:T(8,128)(2,1)S(1)}, u32[]{:S(2)}) copy-start(bf16[128,512]{1,0:T(8,128)(2,1)S(1)} %get-tuple-element.112) | copy-start | bytes 393220
  276.4 14.3 %copy-start.19 = (bf16[128,256]{1,0:T(8,128)(2,1)}, bf16[128,256]{1,0:T(8,128)(2,1)S(1)}, u32[]{:S(2)}) copy-start(bf16[128,256]{1,0:T(8,128)(2,1)S(1)} %get-tuple-element.116) | copy-start | bytes 196612
  276.5 14.3 %copy-start.23 = (f32[1,4096]{1,0:T(1,128)}, f32[1,4096]{1,0:T(1,128)S(1)}, u32[]{:S(2)}) copy-start(f32[1,4096]{1,0:T(1,128)S(1)} %get-tuple-element.120) | copy-start | bytes 49156
  290.8 53.9 %collective-permute-start.12 = (bf16[128,1024]{1,0:T(8,128)(2,1)}, bf16[128,1024]{1,0:T(8,128)(2,1)}, u32[]{:S(2)}, u32[]{:S(2)}) collective-permute-start(bf16[128,1024]{1,0:T(8,128)(2,1)} %add_convert_fusion.1), channel_id=1, source_target_pairs={{64,8},{72,0},{80,24},{88,16},{96,40},{104,32},{112,56},{120,48},{... | collective-permute-start | bytes 786440 | tf_op jit(solution)/shard_map/ppermute | solution.py:199
  292.8 51.9 %collective-permute-start.11 = (bf16[128,1024]{1,0:T(8,128)(2,1)}, bf16[128,1024]{1,0:T(8,128)(2,1)}, u32[]{:S(2)}, u32[]{:S(2)}) collective-permute-start(bf16[128,1024]{1,0:T(8,128)(2,1)} %add_convert_fusion.1), channel_id=1, source_target_pairs={{64,0},{72,8},{80,16},{88,24},{96,32},{104,40},{112,48},{120,56},{... | collective-permute-start | bytes 786440 | tf_op jit(solution)/shard_map/ppermute | solution.py:199
  306.8 0.8 copy-start.39
  306.8 0.9 copy-start.40
  306.8 1.0 copy-start.41
  306.8 1.0 copy-start.42
  306.8 1.1 copy-start.44
  346.9 19.6 %all-to-all-start.14 = ((bf16[4,128,1024]{2,1,0:T(8,128)(2,1)}), bf16[4,128,1024]{2,1,0:T(8,128)(2,1)}, u32[]{:S(2)}, u32[]{:S(2)}) async-start(bf16[4,128,1024]{2,1,0:T(8,128)(2,1)} %broadcast_in_dim.50), calls=%async_computation.14 | async-start | bytes 2097152 | tf_op jit(solution)/shard_map/all_to_all | solution.py:184
  368.3 5.3 %copy-start.14 = (bf16[128,256]{1,0:T(8,128)(2,1)S(1)}, bf16[128,256]{1,0:T(8,128)(2,1)}, u32[]{:S(2)}) copy-start(bf16[128,256]{1,0:T(8,128)(2,1)} %copy-done.13) | copy-start | bytes 196612
  368.3 5.3 %copy-start.34 = (bf16[4,1,1024]{2,1,0:T(2,128)(2,1)S(1)}, bf16[4,1,1024]{2,1,0:T(2,128)(2,1)}, u32[]{:S(2)}) copy-start(bf16[4,1,1024]{2,1,0:T(2,128)(2,1)} %copy-done.33) | copy-start | bytes 24580
  368.3 5.3 %copy-start.35 = (f32[128,1]{1,0:T(8,128)S(1)}, f32[128,1]{1,0:T(8,128)}, u32[]{:S(2)}) copy-start(f32[128,1]{1,0:T(8,128)} %get-tuple-element.86.scale_in) | copy-start | bytes 1540
  369.4 20.2 %all-to-all-start.16 = ((bf16[8,128,512]{2,1,0:T(8,128)(2,1)}), bf16[8,128,512]{2,1,0:T(8,128)(2,1)}, u32[]{:S(2)}, u32[]{:S(2)}) async-start(bf16[8,128,512]{2,1,0:T(8,128)(2,1)} %bitcast.59), calls=%async_computation.16 | async-start | bytes 2097152 | tf_op jit(solution)/shard_map/all_to_all | solution.py:281
  373.6 2.2 copy-start.1
  375.8 2.2 copy-start.4
  378.0 8.2 %copy-start.22 = (f32[1,4096]{1,0:T(1,128)S(1)}, f32[1,4096]{1,0:T(1,128)}, u32[]{:S(2)}) copy-start(f32[1,4096]{1,0:T(1,128)} %copy-done.21) | copy-start | bytes 49156
  378.0 8.2 %copy-start.24 = (f32[1,4096]{1,0:T(1,128)S(1)}, f32[1,4096]{1,0:T(1,128)}, u32[]{:S(2)}) copy-start(f32[1,4096]{1,0:T(1,128)} %copy-done.23) | copy-start | bytes 49156
  378.0 8.5 %copy-start.16 = (bf16[128,256]{1,0:T(8,128)(2,1)S(1)}, bf16[128,256]{1,0:T(8,128)(2,1)}, u32[]{:S(2)}) copy-start(bf16[128,256]{1,0:T(8,128)(2,1)} %copy-done.15) | copy-start | bytes 196612
  378.0 8.5 %copy-start.18 = (bf16[128,256]{1,0:T(8,128)(2,1)S(1)}, bf16[128,256]{1,0:T(8,128)(2,1)}, u32[]{:S(2)}) copy-start(bf16[128,256]{1,0:T(8,128)(2,1)} %copy-done.17) | copy-start | bytes 196612
  378.0 8.5 %copy-start.20 = (bf16[128,256]{1,0:T(8,128)(2,1)S(1)}, bf16[128,256]{1,0:T(8,128)(2,1)}, u32[]{:S(2)}) copy-start(bf16[128,256]{1,0:T(8,128)(2,1)} %copy-done.19) | copy-start | bytes 196612
  378.0 8.5 %copy-start.8 = (bf16[128,512]{1,0:T(8,128)(2,1)S(1)}, bf16[128,512]{1,0:T(8,128)(2,1)}, u32[]{:S(2)}) copy-start(bf16[128,512]{1,0:T(8,128)(2,1)} %copy-done.7) | copy-start | bytes 393220
  378.1 8.5 %copy-start.10 = (bf16[128,512]{1,0:T(8,128)(2,1)S(1)}, bf16[128,512]{1,0:T(8,128)(2,1)}, u32[]{:S(2)}) copy-start(bf16[128,512]{1,0:T(8,128)(2,1)} %copy-done.9) | copy-start | bytes 393220
  378.1 8.5 %copy-start.12 = (bf16[128,512]{1,0:T(8,128)(2,1)S(1)}, bf16[128,512]{1,0:T(8,128)(2,1)}, u32[]{:S(2)}) copy-start(bf16[128,512]{1,0:T(8,128)(2,1)} %copy-done.11) | copy-start | bytes 393220
  378.1 8.6 %copy-start.45 = (bf16[16]{0:T(256)(128)(2,1)S(1)}, bf16[16]{0:T(256)(128)(2,1)}, u32[]{:S(2)}) copy-start(bf16[16]{0:T(256)(128)(2,1)} %pad.16.clone) | copy-start | bytes 100
  388.2 5.7 %copy-start.28 = (bf16[8,128,1024]{2,1,0:T(8,128)(2,1)S(1)}, bf16[8,128,1024]{2,1,0:T(8,128)(2,1)}, u32[]{:S(2)}) copy-start(bf16[8,128,1024]{2,1,0:T(8,128)(2,1)} %get-tuple-element.123) | copy-start | bytes 6291460
  389.6 28.0 %all-to-all-start.15 = ((bf16[8,144,768]{2,1,0:T(8,128)(2,1)}), bf16[8,144,768]{2,1,0:T(8,128)(2,1)}, u32[]{:S(2)}, u32[]{:S(2)}) async-start(bf16[8,144,768]{2,1,0:T(8,128)(2,1)} %fusion.2), calls=%async_computation.15 | async-start | bytes 3538944 | tf_op jit(solution)/shard_map/all_to_all | solution.py:281
  419.2 14.6 %all-to-all-start.17 = ((f32[8,1,64]{2,1,0:T(1,128)}), f32[8,1,64]{2,1,0:T(1,128)S(1)}, u32[]{:S(2)}, u32[]{:S(2)}) async-start(f32[8,1,64]{2,1,0:T(1,128)} %reshape.106), calls=%async_computation.17 | async-start | bytes 8192 | tf_op jit(solution)/shard_map/all_to_all | solution.py:344

commit v3 on v2

v3 whole, which is shorter than its diff:
```python
import functools

import jax
import jax.numpy as jnp
from jax import lax
from jax.experimental import pallas as pl
from jax.experimental.pallas import tpu as pltpu
from jax.sharding import Mesh, PartitionSpec as P

HEAD_DIM = 128
EPS = 1e-05
NEG = -1e30
F32 = jnp.float32
BF16 = jnp.bfloat16
SECTIONS, XS, HALVES, DP = 4, 4, 2, 8
VMEM = pl.BlockSpec(memory_space=pltpu.VMEM)
SMEM = pl.BlockSpec(memory_space=pltpu.SMEM)
HBM = pl.BlockSpec(memory_space=pltpu.HBM)


def dot(former, latter, dims=((1,), (0,))):
    return lax.dot_general(former, latter, (dims, ((), ())), preferred_element_type=F32)


def copies(pairs, sems):
    at = (lambda i: sems[i]) if isinstance(sems, list) else (lambda i: sems.at[i])
    return [pltpu.make_async_copy(a, b, at(i)) for i, (a, b) in enumerate(pairs)]


def heads_down(wide, row, length):
    part = wide[row * length : (row + 1) * length, :]
    return jnp.concatenate(
        [part[:, a : a + HEAD_DIM] for a in range(0, part.shape[1], HEAD_DIM)], axis=0
    )


def heads_across(tall, length):
    return jnp.concatenate(
        [tall[a : a + length] for a in range(0, tall.shape[0], length)], axis=1
    )


def forward_kernel(rows, length, project, lens, parts, gain, wq, wkv, wo, *rest):
    if project:
        send, rest = rest[0], rest[1:]
    pack, scale_out, q_out, kv_out, attn_out = rest[:5]
    wq_v, wkv_v, normed_v, mix_v, sems, out_sems = rest[5:11]
    wo_v = rest[11] if project else None
    block = parts.shape[2]
    width = XS * block
    piece = width // DP
    pairs = []
    for j in range(XS):
        span = pl.ds(j * block, block)
        pairs.append((wq.at[span], wq_v.at[span]))
        pairs.append((wkv.at[span], wkv_v.at[span]))
    if project:
        for j in range(XS):
            span = pl.ds(j * block, block)
            pairs.append((wo.at[:, span], wo_v.at[:, span]))
    moves = copies(pairs, sems)
    for move in moves:
        move.start()
    total = jnp.zeros((parts.shape[1], 1), F32)
    for j in range(XS):
        h = parts[j].astype(F32)
        total = total + jnp.sum(h * h, -1, keepdims=True)
    scale = lax.rsqrt(total / width + EPS)
    scale_out[...] = scale
    q = jnp.zeros(q_out.shape, F32)
    kv = jnp.zeros(kv_out.shape, F32)
    for j in range(XS):
        span = slice(j * block, (j + 1) * block)
        normed = (parts[j].astype(F32) * scale * gain[:, span].astype(F32)).astype(BF16)
        normed_v[:, span] = normed
        moves[2 * j].wait()
        q = q + dot(normed, wq_v[span, :])
        moves[2 * j + 1].wait()
        kv = kv + dot(normed, wkv_v[span, :])
    q = q.astype(BF16)
    kv = kv.astype(BF16)
    q_out[...] = q
    kv_out[...] = kv
    tall = q.shape[1] // HEAD_DIM * length
    at = lax.broadcasted_iota(jnp.int32, (tall, length), 0) % length
    key_at = lax.broadcasted_iota(jnp.int32, (tall, length), 1)
    mixes = []
    for row in range(rows):
        here = slice(row * length, (row + 1) * length)
        keys, values = kv[here, :HEAD_DIM], kv[here, HEAD_DIM:]
        scores = dot(heads_down(q, row, length), keys, ((1,), (1,))) * HEAD_DIM ** (-0.5)
        scores = jnp.where((key_at <= at) & (key_at < lens[row]), scores, NEG)
        raised = jnp.exp(scores - jnp.max(scores, -1, keepdims=True))
        attn = raised / jnp.sum(raised, -1, keepdims=True)
        attn_out[row] = attn
        mixes.append(heads_across(dot(attn.astype(BF16), values).astype(BF16), length))
    mix = jnp.concatenate(mixes, axis=0)
    mix_v[...] = mix
    outs = []
    for d in range(DP):
        outs.append((normed_v.at[:, pl.ds(d * piece, piece)], pack.at[d, :, pl.ds(0, piece)]))
        outs.append((mix_v, pack.at[d, :, pl.ds(piece, mix.shape[1])]))
    outs = copies(outs, out_sems)

    for move in outs:
        move.start()

    if project:
        for j in range(XS):
            moves[2 * XS + j].wait()
            send[j] = dot(mix, wo_v[:, j * block : (j + 1) * block]).astype(BF16)

    for move in outs:
        move.wait()


def backward_kernel(
    rows, length, onward, grads, parts, gain, scale_in, q_in, kv_in, attn_in,
    wq, wkv, wo, *rest
):
    if onward:
        send, rest = rest[0], rest[1:]
    pack, wq_v, wkv_v, wo_v, qg_v, pg_v, gain_v, gain_pair_v, sems, out_sems = rest
    tokens, block = parts.shape[1:]
    width = XS * block
    piece = width // DP
    qs, kvs = qg_v.shape[1], pg_v.shape[1]
    pairs = []
    for j in range(XS):
        span = pl.ds(j * block, block)
        pairs.append((wo.at[:, span], wo_v.at[:, span]))
    for j in range(XS):
        span = pl.ds(j * block, block)
        pairs.append((wq.at[span], wq_v.at[span]))
        pairs.append((wkv.at[span], wkv_v.at[span]))
    moves = copies(pairs, sems)
    for move in moves:
        move.start()
    real = pl.ds(0, tokens)
    outs = []
    for d in range(DP):
        outs.append(
            (grads.at[d // 2, :, pl.ds(d % 2 * piece, piece)], pack.at[d, real, pl.ds(0, piece)])
        )
    for d in range(DP):
        outs.append((qg_v, pack.at[d, real, pl.ds(piece, qs)]))
        outs.append((pg_v, pack.at[d, real, pl.ds(piece + qs, kvs)]))
    for d in range(DP):
        outs.append((gain_pair_v, pack.at[d, pl.ds(tokens, 16), pl.ds(0, piece)]))
    outs = copies(outs, out_sems)

    for move in outs[:DP]:
        move.start()

    mix_grad = jnp.zeros(q_in.shape, F32)
    for j in range(XS):
        moves[j].wait()
        mix_grad = mix_grad + dot(grads[j], wo_v[:, j * block : (j + 1) * block], ((1,), (1,)))
    mix_grad = mix_grad.astype(BF16)
    q = q_in[...]
    kv = kv_in[...]
    query_grads, pair_grads = [], []
    for row in range(rows):
        here = slice(row * length, (row + 1) * length)
        keys, values = kv[here, :HEAD_DIM], kv[here, HEAD_DIM:]
        attn = attn_in[row]
        mixed = heads_down(mix_grad, row, length)
        value_grad = dot(attn.astype(BF16), mixed, ((0,), (0,)))
        weight_grad = dot(mixed, values, ((1,), (1,)))
        score_grad = attn * (weight_grad - jnp.sum(weight_grad * attn, -1, keepdims=True))
        score_grad = (score_grad * HEAD_DIM ** (-0.5)).astype(BF16)
        query_grads.append(heads_across(dot(score_grad, keys).astype(BF16), length))
        key_grad = dot(score_grad, heads_down(q, row, length), ((0,), (0,)))
        pair_grads.append(jnp.concatenate([key_grad, value_grad], axis=1).astype(BF16))
    query_grad = jnp.concatenate(query_grads, axis=0)
    pair_grad = jnp.concatenate(pair_grads, axis=0)
    qg_v[...] = query_grad
    pg_v[...] = pair_grad

    for move in outs[DP : 3 * DP]:
        move.start()

    scale = scale_in[...]
    if onward:
        correction = jnp.sum(query_grad.astype(F32) * q.astype(F32), -1, keepdims=True)
        correction += jnp.sum(pair_grad.astype(F32) * kv.astype(F32), -1, keepdims=True)
        pull = scale * scale / width * correction
    for j in range(XS):
        span = slice(j * block, (j + 1) * block)
        moves[XS + 2 * j].wait()
        moves[XS + 2 * j + 1].wait()
        normed_grad = dot(query_grad, wq_v[span, :], ((1,), (1,))) + dot(
            pair_grad, wkv_v[span, :], ((1,), (1,))
        )
        h = parts[j].astype(F32)
        scaled = normed_grad * scale
        part = jnp.sum(scaled * h, 0, keepdims=True)
        gain_v[2 * j : 2 * j + 1, :] = part[:, :piece]
        gain_v[2 * j + 1 : 2 * j + 2, :] = part[:, piece:]
        if onward:
            send[j] = (scaled * gain[:, span].astype(F32) - h * pull).astype(BF16)
    terms = gain_v[...]
    high = terms.astype(BF16)
    low = (terms - high.astype(F32)).astype(BF16)
    gain_pair_v[...] = jnp.concatenate([high, low], axis=0)

    for move in outs[3 * DP :]:
        move.start()
    for move in outs:
        move.wait()


def weights_kernel(
    last, station, early, late, got, grad_query, grad_pair, grad_out, factors, wide_v, out_v, sem, sems
):
    tokens = early.shape[1]
    piece = grad_query.shape[0]
    qs = grad_query.shape[1]
    load = copies([(early, factors), (late, factors)], [sem.at[0], sem.at[0]])

    @pl.when(station[0] != last)
    def _():
        load[0].start()

    @pl.when(station[0] == last)
    def _():
        load[1].start()

    for d in range(DP):
        wide_v[d * tokens : (d + 1) * tokens, :] = got[d, :tokens, :]
    load[0].wait()
    flat = factors[...].reshape(DP * tokens, factors.shape[2])
    wide = wide_v[...]
    kvs = grad_pair.shape[1]
    out_v[:, :qs] = dot(flat[:, piece:], wide[:, :piece], ((0,), (0,)))
    outs = copies(
        [
            (out_v.at[:, pl.ds(0, piece)], grad_out),
            (out_v.at[:, pl.ds(piece, qs)], grad_query),
            (out_v.at[:, pl.ds(piece + qs, kvs)], grad_pair),
        ],
        sems,
    )
    outs[0].start()
    out_v[:, piece:] = dot(flat[:, :piece], wide[:, piece:], ((0,), (0,)))
    outs[1].start()
    outs[2].start()
    for move in outs:
        move.wait()


def combine_kernel(first, second, spread):
    total = (first[...].astype(F32) + second[...].astype(F32)).astype(BF16)
    for j in range(XS):
        spread[j] = total


def call(kernel, ins, outs, scratch, flops, args, aliases={}):
    return pl.pallas_call(
        kernel,
        out_shape=[out for out, _ in outs],
        in_specs=ins,
        out_specs=[spec for _, spec in outs],
        scratch_shapes=scratch,
        input_output_aliases=aliases,
        compiler_params=pltpu.CompilerParams(vmem_limit_bytes=40 * 2**20),
        cost_estimate=pl.CostEstimate(flops=flops, bytes_accessed=12 * 2**20, transcendentals=2**16),
    )(*args)


def place(section, x, half):
    return (section * XS + x) * HALVES + half


def gather_x(spread):
    return lax.all_to_all(spread, "x", 0, 0)


def scatter_x(parts):
    return jnp.sum(lax.all_to_all(parts, "x", 0, 0).astype(F32), 0)


def hop(block, source, target):
    got = []
    for cross in range(HALVES):
        route = [
            (place(source, x, half), place(target, x, half ^ cross))
            for x in range(XS)
            for half in range(HALVES)
        ]
        got.append(lax.ppermute(block, ("s", "x", "zh"), route))
    return got


def combine(first, second):
    spread = jax.ShapeDtypeStruct((XS,) + first.shape, BF16)
    return call(combine_kernel, [VMEM] * 2, [(spread, VMEM)], [], 2**20, (first, second))[0]


def nothing(*outs):
    return pl.pallas_call(
        lambda *refs: None, out_shape=[o for o, _ in outs], out_specs=[HBM for _ in outs]
    )()


def pair_up(block, sections):
    route = [
        (place(s, x, half), place(s, x, 1 - half))
        for s in sections
        for x in range(XS)
        for half in range(HALVES)
    ]
    other = lax.ppermute(block, ("s", "x", "zh"), route)
    first = lax.axis_index("zh") == 0
    return jnp.concatenate([jnp.where(first, block, other), jnp.where(first, other, block)], -1)


def shards(hidden_in, lengths, gains, w_query, w_keyval, w_out, grad_out):
    station = lax.axis_index("s")
    rows, length, shard = hidden_in.shape
    tokens = rows * length
    wq = w_query[0]
    width = wq.shape[0]
    wkv = w_keyval[0].reshape(width, -1)
    wo = w_out[0]
    block_width = width // XS
    qs, kvs = wq.shape[1], wkv.shape[1]
    flops = 2 * tokens * width * (2 * qs + kvs)
    tall = qs // HEAD_DIM * length

    start = jnp.where(
        station == 0, hidden_in.reshape(tokens, shard), grad_out.reshape(tokens, shard)
    )
    start = jnp.concatenate([start, jnp.broadcast_to(gains, (16, shard))], 0)
    start_block = pair_up(start, range(SECTIONS))
    start_full = gather_x(jnp.broadcast_to(start_block[None], (XS,) + start_block.shape))
    gain = start_full[:, tokens, :].reshape(1, width)
    first = start_full[:, :tokens]
    first_block = start_block[:tokens]

    shape = jax.ShapeDtypeStruct
    dma = lambda count: pltpu.SemaphoreType.DMA((count,))
    here = station.reshape(1)
    piece = width // DP
    sent = (shape((XS, tokens, block_width), BF16), VMEM)
    early_pack = (shape((DP, tokens, piece + qs), BF16), HBM)
    late_pack = (shape((DP, tokens + 16, piece + qs + kvs), BF16), HBM)
    saved = [
        (shape((tokens, 1), F32), VMEM),
        (shape((tokens, qs), BF16), VMEM),
        (shape((tokens, kvs), BF16), VMEM),
        (shape((rows, tall, length), F32), VMEM),
    ]
    held = [pltpu.VMEM((width, qs), BF16), pltpu.VMEM((width, kvs), BF16)]
    held_out = [pltpu.VMEM((qs, width), BF16)]
    over_dp = lambda v: lax.all_to_all(v, ("y", "core"), 0, 0)

    last_section = SECTIONS - 1
    block_out = (shape((tokens, block_width), BF16), HBM)
    factors_out = (shape((DP, tokens, piece + qs), BF16), HBM)
    parts_out = (shape((XS, tokens, block_width), BF16), HBM)

    def forward(parts, project):
        return call(
            functools.partial(forward_kernel, rows, length, project),
            [SMEM, VMEM, VMEM, HBM, HBM, HBM],
            [sent] * project + [early_pack] + saved,
            held
            + [pltpu.VMEM((tokens, width), BF16), pltpu.VMEM((tokens, qs), BF16)]
            + [dma(3 * XS), dma(2 * DP)]
            + held_out * project,
            flops,
            (lengths, parts, gain, wq, wkv, wo),
        )

    def backward(parts_grad, kept, onward):
        return call(
            functools.partial(backward_kernel, rows, length, onward),
            [VMEM] * 7 + [HBM] * 3,
            [sent] * onward + [late_pack],
            held
            + held_out
            + [pltpu.VMEM((tokens, qs), BF16), pltpu.VMEM((tokens, kvs), BF16)]
            + [pltpu.VMEM((DP, piece), F32), pltpu.VMEM((2 * DP, piece), BF16)]
            + [dma(3 * XS), dma(4 * DP)],
            flops,
            (parts_grad, kept[0], gain) + tuple(kept[1:]) + (wq, wkv, wo),
        )

    def pass_on(block, sums):
        return (0.5 * block.astype(F32) + scatter_x(sums)).astype(BF16)

    kept = []
    packed = None
    arrived = None
    for step in range(last_section):

        def work(packed, arrived):
            if arrived is None:
                parts, block = first, first_block
            else:
                spread = combine(*arrived)
                parts, block = gather_x(spread), spread[0]
            got = forward(parts, True)
            return pass_on(block, got[0]), got[1], [parts] + list(got[2:])

        def rest(packed, arrived):
            empty = nothing(block_out, early_pack, parts_out, *saved)
            return empty[0], empty[1] if packed is None else packed, list(empty[2:])

        block, packed, saved_here = lax.cond(station == step, work, rest, packed, arrived)
        kept.append(saved_here)
        arrived = hop(block, step, step + 1)

    def turn(packed, arrived):
        spread = combine(*arrived)
        parts = gather_x(spread)
        got = forward(parts, False)
        back = backward(first, [parts] + list(got[1:]), True)
        empty = nothing(factors_out)
        return pass_on(first_block, back[0]), back[1], got[0], empty[0]

    def exchange(packed, arrived):
        empty = nothing(block_out, late_pack, early_pack)
        return tuple(empty) + (over_dp(packed),)

    block, pack, late_factors, early = lax.cond(
        station == last_section, turn, exchange, packed, arrived
    )
    arrived = hop(block, last_section, last_section - 1)

    for step in reversed(range(last_section)):
        onward = step > 0
        if not onward:
            late = lax.cond(
                station == last_section, over_dp, lambda v: nothing(factors_out)[0], late_factors
            )
            late, *arrived = lax.optimization_barrier([late] + list(arrived))

        def work(pack, arrived, kept_here):
            spread = combine(*arrived)
            got = backward(gather_x(spread), kept_here, onward)
            return ([pass_on(spread[0], got[0])] if onward else []) + [got[onward]]

        def rest(pack, arrived, kept_here):
            return ([nothing(block_out)[0]] if onward else []) + [pack]

        got = lax.cond(station == step, work, rest, pack, arrived, kept[step])
        pack = got[-1]
        if onward:
            arrived = hop(got[0], step, step - 1)

    got = over_dp(pack)
    terms = got[:, tokens:, :piece].astype(F32).reshape(DP, 2, DP, piece)
    terms = jnp.sum(terms, (0, 1))
    small = piece // DP
    own = lax.axis_index(("y", "core")) * small
    terms = lax.dynamic_slice_in_dim(terms, own, small, 1).reshape(DP, 1, small)
    gain_grad = jnp.sum(lax.all_to_all(terms, ("x", "zh"), 0, 0), 0)
    grad_query, grad_pair, grad_out_weight = call(
        functools.partial(weights_kernel, last_section),
        [SMEM, HBM, HBM, VMEM],
        [
            (shape((piece, qs), F32), HBM),
            (shape((piece, kvs), F32), HBM),
            (shape((qs, piece), F32), HBM),
        ],
        [
            pltpu.VMEM((DP, tokens, piece + qs), BF16),
            pltpu.VMEM((DP * tokens, piece + qs + kvs), BF16),
            pltpu.VMEM((piece, piece + qs + kvs), F32),
            dma(1),
            dma(3),
        ],
        flops,
        (here, early, late, got),
    )
    return (
        grad_query[None],
        grad_pair.reshape(1, piece, 1, kvs),
        grad_out_weight[None],
        gain_grad[None][:, 0],
    )


def solution(mesh):
    grid = Mesh(mesh.devices.reshape(SECTIONS, XS, HALVES, 4, 2), ("s", "x", "zh", "y", "core"))
    section, tensor, dp = "s", ("x", "zh"), ("y", "core")
    in_specs = (
        P(dp, None, tensor),
        P(dp),
        P(section, tensor),
        P(section, None, tensor),
        P(section, None, tensor, None),
        P(section, tensor, None),
        P(dp, None, tensor),
    )
    out_specs = (
        P(section, dp, tensor),
        P(section, dp, tensor, None),
        P(section, tensor, dp),
        P(section, tensor + dp),
    )
    return jax.shard_map(shards, mesh=grid, in_specs=in_specs, out_specs=out_specs, check_vma=False)
```

time: 443 us -> 392 us (0.88)
  the two profiles are of different devices: /device:TPU:32 before, /device:TPU:1 now
where the time goes in v3:
time: 392 us
  waiting for transfers between devices  274 us (70%)
  starting transfers between devices  71.4 us (18%)
  Pallas kernels  20.7 us (5%)
  blocking collectives  12.2 us (3%)
  local copies, waits for them, and re-layouts  7.81 us (2%)
  other arithmetic  4.53 us (1%)
    ppermute x12, waiting for transfers between devices, hop(): got.append(lax.ppermute(block, ('s', 'x', 'zh'), route))  179 us
    all_to_all x2, waiting for transfers between devices, shards(): over_dp = lambda v: lax.all_to_all(v, ('y', 'core'), 0, 0)  61.9 us
    all_to_all x2, starting transfers between devices, shards(): over_dp = lambda v: lax.all_to_all(v, ('y', 'core'), 0, 0)  35.4 us
    pallas_call x4, Pallas kernels, call(): pl.pallas_call(kernel, out_shape=[out for out, _ in outs], in_specs=ins,...  20.7 us
    all_to_all x1, waiting for transfers between devices, gather_x(): return lax.all_to_all(spread, 'x', 0, 0)  15 us
    ppermute x12, starting transfers between devices, hop(): got.append(lax.ppermute(block, ('s', 'x', 'zh'), route))  14.9 us
    all_to_all x1, blocking collectives, gather_x(): return lax.all_to_all(spread, 'x', 0, 0)  12.2 us
    all_to_all x1, waiting for transfers between devices, scatter_x(): return jnp.sum(lax.all_to_all(parts, 'x', 0, 0).astype(F32), 0)  11.4 us
  transfers between devices with their start and end apart: 18, of which 10 were waited for; matrix products, arithmetic and copies ran while one was open for 1% of the time, Pallas kernels for 1%

profile of v3, /device:TPU:1, one launch (start us, length us, event | category | flops | bytes accessed | tf_op | source)
XLA Modules:
  0.0 391.6 jit_solution(11592480893555022006)
XLA Ops:
  0.6 0.7 reduce.3
  1.3 0.9 broadcast_select_fusion.2
  2.3 7.8 %collective-permute-start = (bf16[144,512]{1,0:T(8,128)(2,1)S(1)}, bf16[144,512]{1,0:T(8,128)(2,1)S(1)}, u32[]{:S(2)}, u32[]{:S(2)}) collective-permute-start(bf16[144,512]{1,0:T(8,128)(2,1)S(1)} %pad_maximum_fusion.1), channel_id=1, source_target_pairs={{0,8},{8,0},{16,24},{24,16},{32,40},{40,32},{48,56},{56,48},{64,72... | collective-permute-start | bytes 442376 | tf_op jit(solution)/shard_map/ppermute | solution.py:313
  10.1 3.0 collective-permute-done
  13.2 0.1 broadcast_select_fusion
  13.2 1.2 broadcast_in_dim.21
  14.4 4.7 %all-to-all-start.14 = ((bf16[4,144,1024]{2,1,0:T(8,128)(2,1)}), bf16[4,144,1024]{2,1,0:T(8,128)(2,1)}, u32[]{:S(2)}, u32[]{:S(2)}) async-start(bf16[4,144,1024]{2,1,0:T(8,128)(2,1)} %broadcast_in_dim.21), calls=%async_computation.14 | async-start | bytes 2359296 | tf_op jit(solution)/shard_map/all_to_all | solution.py:276
  19.2 15.0 %all-to-all-done.14 = bf16[4,144,1024]{2,1,0:T(8,128)(2,1)} async-done(((bf16[4,144,1024]{2,1,0:T(8,128)(2,1)}), bf16[4,144,1024]{2,1,0:T(8,128)(2,1)}, u32[]{:S(2)}, u32[]{:S(2)}) %all-to-all-start.14) | async-done | bytes 1179680 | tf_op jit(solution)/shard_map/all_to_all | solution.py:276
  34.2 0.9 slice.35
  35.0 1.3 slice.34
  36.3 0.0 copy-done.2
  36.3 26.4 %conditional.8 = (bf16[128,1024]{1,0:T(8,128)(2,1)}, bf16[4,128,1024]{2,1,0:T(8,128)(2,1)}, f32[128,1]{1,0:T(8,128)}, bf16[128,512]{1,0:T(8,128)(2,1)S(1)}, bf16...) conditional(s32[]{:T(128)} %convert_element_type.80, () %tuple.73, ...), branch_computations={%region_0.1_spmd, %region_1.3_spmd} | conditional | flops 1343619072 | bytes 20447320 | solution.py:411
  36.4 7.5 %branch_1_fun.15 = (bf16[4,128,1024]{2,1,0:T(8,128)(2,1)}, bf16[8,128,1024]{2,1,0:T(8,128)(2,1)}, f32[128,1]{1,0:T(8,128)}, bf16[128,512]{1,0:T(8,128)(2,1)S(1)}...) custom-call(s32[2]{0:T(128)} %get-tuple-element.155.lens, bf16[4,128,1024]{2,1,0:T(8,128)(2,1)S(1)} %get-tuple-element.357.parts, ...), custom_call_target="tpu_custom_call" | custom-call | flops 1342177280 | bytes 12582912 | tf_op jit(solution)/shard_map/cond/branch_1_fun/pallas_call | solution.py:259
  43.9 4.3 %all-to-all-start.3 = ((bf16[4,128,1024]{2,1,0:T(8,128)(2,1)}), bf16[4,128,1024]{2,1,0:T(8,128)(2,1)}, u32[]{:S(2)}, u32[]{:S(2)}) async-start(bf16[4,128,1024]{2,1,0:T(8,128)(2,1)} %get-tuple-element.161), calls=%async_computation.3 | async-start | bytes 2097152 | tf_op jit(solution)/shard_map/cond/branch_1_fun/all_to_all | solution.py:280
  48.1 1.0 copy.22
  49.1 11.4 %all-to-all-done.3 = bf16[4,128,1024]{2,1,0:T(8,128)(2,1)} async-done(((bf16[4,128,1024]{2,1,0:T(8,128)(2,1)}), bf16[4,128,1024]{2,1,0:T(8,128)(2,1)}, u32[]{:S(2)}, u32[]{:S(2)}) %all-to-all-start.3) | async-done | bytes 1048608 | tf_op jit(solution)/shard_map/cond/branch_1_fun/all_to_all | solution.py:280
  60.5 1.5 convert_reduce_fusion
  61.9 0.8 add_convert_fusion
  62.7 2.0 collective-permute-start.2
  64.7 2.0 collective-permute-start.1
  66.7 0.9 collective-permute-done.2
  67.6 2.0 collective-permute-done.1
  69.6 1.4 collective-permute-start.4
  71.0 1.4 collective-permute-start.3
  72.3 0.0 collective-permute-done.4
  72.3 0.0 collective-permute-done.3
  72.4 1.4 collective-permute-start.6
  73.7 1.3 collective-permute-start.5
  75.1 0.0 collective-permute-done.6
  75.1 0.0 collective-permute-done.5
  75.1 35.6 %conditional.11 = (bf16[128,1024]{1,0:T(8,128)(2,1)S(1)}, bf16[8,144,1280]{2,1,0:T(8,128)(2,1)}, bf16[8,128,1024]{2,1,0:T(8,128)(2,1)}, bf16[8,128,1024]{2,1,0:T(8,128)(2,1)}) conditional(s32[]{:T(128)} %convert_element_type.77, bf16[8,128,1024]{2,1,0:T(8,128)(2,1)} %get-tuple-element.304, (bf16[128,1024]{1,0:T(8,128)(2,1)S(1)}, ...), branch_computations={%region_9.10_spmd, %region_10.12_spmd} | conditional | flops 2686844928 | bytes 79167664 | solution.py:427
  75.1 9.2 %all-to-all-start = ((bf16[8,128,1024]{2,1,0:T(8,128)(2,1)}), bf16[8,128,1024]{2,1,0:T(8,128)(2,1)}, u32[]{:S(2)}, u32[]{:S(2)}) async-start(bf16[8,128,1024]{2,1,0:T(8,128)(2,1)} %param.6), calls=%async_computation | async-start | bytes 4194304 | tf_op jit(solution)/shard_map/cond/branch_0_fun/all_to_all | solution.py:356
  84.3 26.4 %all-to-all-done = bf16[8,128,1024]{2,1,0:T(8,128)(2,1)} async-done(((bf16[8,128,1024]{2,1,0:T(8,128)(2,1)}), bf16[8,128,1024]{2,1,0:T(8,128)(2,1)}, u32[]{:S(2)}, u32[]{:S(2)}) %all-to-all-start) | async-done | bytes 2097184 | tf_op jit(solution)/shard_map/cond/branch_0_fun/all_to_all | solution.py:356
  110.7 0.7 copy-done.26
  111.4 0.7 collective-permute-start.8
  112.1 0.7 collective-permute-start.7
  112.8 0.0 collective-permute-done.8
  112.8 0.0 collective-permute-done.7
  112.8 0.0 copy-start.14
  112.8 0.7 copy-done.12
  113.5 0.1 copy-done.14
  113.6 0.8 collective-permute-start.10
  114.4 0.7 collective-permute-start.9
  115.1 0.0 collective-permute-done.10
  115.1 0.0 collective-permute-done.9
  115.1 0.3 conditional.14
  115.5 1.3 collective-permute-start.12
  116.8 1.3 collective-permute-start.11
  118.1 0.0 copy-start.7
  118.1 175.4 %collective-permute-done.12 = bf16[128,1024]{1,0:T(8,128)(2,1)} collective-permute-done((bf16[128,1024]{1,0:T(8,128)(2,1)}, bf16[128,1024]{1,0:T(8,128)(2,1)}, u32[]{:S(2)}, u32[]{:S(2)}) %collective-permute-start.12) | collective-permute-done | bytes 262176 | tf_op jit(solution)/shard_map/ppermute | solution.py:291
  293.5 0.7 collective-permute-done.11
  294.2 0.0 copy-done.8
  294.2 21.2 %conditional.15 = (bf16[8,144,1280]{2,1,0:T(8,128)(2,1)}) conditional(s32[]{:T(128)} %convert_element_type.80, bf16[8,144,1280]{2,1,0:T(8,128)(2,1)} %get-tuple-element.324, (bf16[128,1024]{1,0:T(8,128)(2,1)}, bf16[128,1024]{1,0:T(8,128)(2,1)}, bf16[4,128,1024]{2,1,0:T(8,128)(2,1)S(1)}, bf16[1,4096]{1,0:T(2,128)(2,1)S(1)}, f32[128,1]{1,0:T(8,128)}, ...), branch_computations={%region_20.21_spmd, %region_21.22_spmd} | conditional | flops 1343225856 | bytes 27527232 | solution.py:448
  294.2 1.1 branch_1_fun.28
  295.4 12.2 %all_to_all.81.grads = bf16[4,128,1024]{2,1,0:T(8,128)(2,1)S(1)} all-to-all(bf16[4,128,1024]{2,1,0:T(8,128)(2,1)S(1)} %branch_1_fun.28), channel_id=1, replica_groups=mesh['s'=4,'x'=4,'zh'=2,'y'=4,'core'=2] {'x'}, dimensions={0} | all-to-all | bytes 2097152 | tf_op jit(solution)/shard_map/cond/branch_1_fun/all_to_all | solution.py:276
  307.6 7.9 %branch_1_fun.29 = bf16[8,144,1280]{2,1,0:T(8,128)(2,1)} custom-call(bf16[4,128,1024]{2,1,0:T(8,128)(2,1)S(1)} %all_to_all.81.grads, bf16[4,128,1024]{2,1,0:T(8,128)(2,1)S(1)} %get-tuple-element.252.parts, bf16[1,4096]{1,0:T(2,128)(2,1)S(1)} %get-tuple-element.253.gain, f32[128,1]{1,0:T(8,128)S(1)} %copy-done.17, ...), custom_call_target="tpu_custom_call" | custom-call | flops 1342177280 | bytes 12582912 | tf_op jit(solution)/shard_map/cond/branch_1_fun/pallas_call | solution.py:259
  315.4 26.2 %all-to-all-start.15 = ((bf16[8,144,1280]{2,1,0:T(8,128)(2,1)}), bf16[8,144,1280]{2,1,0:T(8,128)(2,1)S(1)}, u32[]{:S(2)}, u32[]{:S(2)}) async-start(bf16[8,144,1280]{2,1,0:T(8,128)(2,1)} %get-tuple-element.408), calls=%async_computation.15 | async-start | bytes 5898240 | tf_op jit(solution)/shard_map/all_to_all | solution.py:356
  341.6 35.5 %all-to-all-done.15.got = bf16[8,144,1280]{2,1,0:T(8,128)(2,1)S(1)} async-done(((bf16[8,144,1280]{2,1,0:T(8,128)(2,1)}), bf16[8,144,1280]{2,1,0:T(8,128)(2,1)S(1)}, u32[]{:S(2)}, u32[]{:S(2)}) %all-to-all-start.15) | async-done | bytes 2949152 | tf_op jit(solution)/shard_map/all_to_all | solution.py:356
  377.1 0.7 constant_dynamic-slice_fusion
  377.8 4.3 %all-to-all-start.16 = ((f32[8,1,64]{2,1,0:T(1,128)}), f32[8,1,64]{2,1,0:T(1,128)S(1)}, u32[]{:S(2)}, u32[]{:S(2)}) async-start(f32[8,1,64]{2,1,0:T(1,128)} %bitcast.14), calls=%async_computation.16 | async-start | bytes 8192 | tf_op jit(solution)/shard_map/all_to_all | solution.py:459
  382.1 4.2 %shard_map.102 = (f32[512,512]{1,0:T(8,128)}, f32[512,256]{1,0:T(8,128)S(1)}, f32[512,512]{1,0:T(8,128)}) custom-call(s32[1]{0:T(128)} %bitcast.4.station, bf16[8,128,1024]{2,1,0:T(8,128)(2,1)} %get-tuple-element.306.early, bf16[8,128,1024]{2,1,0:T(8,128)(2,1)} %get-tuple-element.407.late, bf16[8,144,1280]{2,1,0:T(8,128)(2,1)S(1)} %all-to-all-done.15.got), custom_call_target="tpu_custom_call" | custom-call | flops 1342177280 | bytes 12582912 | tf_op jit(solution)/shard_map/pallas_call | solution.py:259
  386.4 1.3 copy.13
  387.7 3.3 all-to-all-done.16
  391.0 0.5 reduce_sum.84
  (29 shorter events, 0.1 us)
Async XLA Ops:
  2.3 10.9 %collective-permute-start = (bf16[144,512]{1,0:T(8,128)(2,1)S(1)}, bf16[144,512]{1,0:T(8,128)(2,1)S(1)}, u32[]{:S(2)}, u32[]{:S(2)}) collective-permute-start(bf16[144,512]{1,0:T(8,128)(2,1)S(1)} %pad_maximum_fusion.1), channel_id=1, source_target_pairs={{0,8},{8,0},{16,24},{24,16},{32,40},{40,32},{48,56},{56,48},{64,72... | collective-permute-start | bytes 442376 | tf_op jit(solution)/shard_map/ppermute | solution.py:313
  14.4 21.9 %copy-start.2 = (bf16[1,4096,1,256]{3,1,2,0:T(8,128)(2,1)S(1)}, bf16[1,4096,1,256]{3,1,2,0:T(8,128)(2,1)}, u32[]{:S(2)}) copy-start(bf16[1,4096,1,256]{3,1,2,0:T(8,128)(2,1)} %param.27) | copy-start | bytes 6291460
  14.4 19.7 %all-to-all-start.14 = ((bf16[4,144,1024]{2,1,0:T(8,128)(2,1)}), bf16[4,144,1024]{2,1,0:T(8,128)(2,1)}, u32[]{:S(2)}, u32[]{:S(2)}) async-start(bf16[4,144,1024]{2,1,0:T(8,128)(2,1)} %broadcast_in_dim.21), calls=%async_computation.14 | async-start | bytes 2359296 | tf_op jit(solution)/shard_map/all_to_all | solution.py:276
  43.9 16.6 %all-to-all-start.3 = ((bf16[4,128,1024]{2,1,0:T(8,128)(2,1)}), bf16[4,128,1024]{2,1,0:T(8,128)(2,1)}, u32[]{:S(2)}, u32[]{:S(2)}) async-start(bf16[4,128,1024]{2,1,0:T(8,128)(2,1)} %get-tuple-element.161), calls=%async_computation.3 | async-start | bytes 2097152 | tf_op jit(solution)/shard_map/cond/branch_1_fun/all_to_all | solution.py:280
  62.7 4.9 %collective-permute-start.2 = (bf16[128,1024]{1,0:T(8,128)(2,1)}, bf16[128,1024]{1,0:T(8,128)(2,1)}, u32[]{:S(2)}, u32[]{:S(2)}) collective-permute-start(bf16[128,1024]{1,0:T(8,128)(2,1)} %get-tuple-element.301), channel_id=1, source_target_pairs={{0,72},{8,64},{16,88},{24,80},{32,104},{40,96},{48,120},{56,112},{... | collective-permute-start | bytes 786440 | tf_op jit(solution)/shard_map/ppermute | solution.py:291
  64.7 4.9 %collective-permute-start.1 = (bf16[128,1024]{1,0:T(8,128)(2,1)}, bf16[128,1024]{1,0:T(8,128)(2,1)}, u32[]{:S(2)}, u32[]{:S(2)}) collective-permute-start(bf16[128,1024]{1,0:T(8,128)(2,1)} %get-tuple-element.301), channel_id=1, source_target_pairs={{0,64},{8,72},{16,80},{24,88},{32,96},{40,104},{48,112},{56,120},{... | collective-permute-start | bytes 786440 | tf_op jit(solution)/shard_map/ppermute | solution.py:291
  69.6 2.7 collective-permute-start.4
  71.0 1.4 collective-permute-start.3
  72.4 2.7 collective-permute-start.6
  73.7 1.4 collective-permute-start.5
  75.1 35.6 %all-to-all-start = ((bf16[8,128,1024]{2,1,0:T(8,128)(2,1)}), bf16[8,128,1024]{2,1,0:T(8,128)(2,1)}, u32[]{:S(2)}, u32[]{:S(2)}) async-start(bf16[8,128,1024]{2,1,0:T(8,128)(2,1)} %param.6), calls=%async_computation | async-start | bytes 4194304 | tf_op jit(solution)/shard_map/cond/branch_0_fun/all_to_all | solution.py:356
  110.7 0.7 copy-start.26
  111.4 1.4 collective-permute-start.8
  112.1 0.7 collective-permute-start.7
  112.8 0.7 copy-start.12
  112.8 0.8 copy-start.14
  113.6 1.5 copy-start.4
  113.6 1.5 copy-start.9
  113.6 1.5 collective-permute-start.10
  114.4 0.7 collective-permute-start.9
  115.5 178.0 %collective-permute-start.12 = (bf16[128,1024]{1,0:T(8,128)(2,1)}, bf16[128,1024]{1,0:T(8,128)(2,1)}, u32[]{:S(2)}, u32[]{:S(2)}) collective-permute-start(bf16[128,1024]{1,0:T(8,128)(2,1)} %get-tuple-element.322), channel_id=1, source_target_pairs={{64,8},{72,0},{80,24},{88,16},{96,40},{104,32},{112,56},{120,48},{... | collective-permute-start | bytes 786440 | tf_op jit(solution)/shard_map/ppermute | solution.py:291
  116.8 177.5 %collective-permute-start.11 = (bf16[128,1024]{1,0:T(8,128)(2,1)}, bf16[128,1024]{1,0:T(8,128)(2,1)}, u32[]{:S(2)}, u32[]{:S(2)}) collective-permute-start(bf16[128,1024]{1,0:T(8,128)(2,1)} %get-tuple-element.322), channel_id=1, source_target_pairs={{64,0},{72,8},{80,16},{88,24},{96,32},{104,40},{112,48},{120,56},{... | collective-permute-start | bytes 786440 | tf_op jit(solution)/shard_map/ppermute | solution.py:291
  118.1 176.2 %copy-start.7 = (bf16[4,128,1024]{2,1,0:T(8,128)(2,1)S(1)}, bf16[4,128,1024]{2,1,0:T(8,128)(2,1)}, u32[]{:S(2)}) copy-start(bf16[4,128,1024]{2,1,0:T(8,128)(2,1)} %get-tuple-element.327) | copy-start | bytes 3145732
  118.1 176.1 %copy-start.8 = (f32[2,256,64]{2,1,0:T(8,128)S(1)}, f32[2,256,64]{2,1,0:T(8,128)}, u32[]{:S(2)}) copy-start(f32[2,256,64]{2,1,0:T(8,128)} %get-tuple-element.331) | copy-start | bytes 393220
  294.2 13.3 %copy-start.17 = (f32[128,1]{1,0:T(8,128)S(1)}, f32[128,1]{1,0:T(8,128)}, u32[]{:S(2)}) copy-start(f32[128,1]{1,0:T(8,128)} %get-tuple-element.254.scale_in) | copy-start | bytes 1540 | tf_op jit(solution)/shard_map/cond
  294.2 13.3 %copy-start.18 = (bf16[128,256]{1,0:T(8,128)(2,1)S(1)}, bf16[128,256]{1,0:T(8,128)(2,1)}, u32[]{:S(2)}) copy-start(bf16[128,256]{1,0:T(8,128)(2,1)} %get-tuple-element.256.kv_in) | copy-start | bytes 196612 | tf_op jit(solution)/shard_map/cond
  315.4 61.7 %all-to-all-start.15 = ((bf16[8,144,1280]{2,1,0:T(8,128)(2,1)}), bf16[8,144,1280]{2,1,0:T(8,128)(2,1)S(1)}, u32[]{:S(2)}, u32[]{:S(2)}) async-start(bf16[8,144,1280]{2,1,0:T(8,128)(2,1)} %get-tuple-element.408), calls=%async_computation.15 | async-start | bytes 5898240 | tf_op jit(solution)/shard_map/all_to_all | solution.py:356
  377.8 13.2 %all-to-all-start.16 = ((f32[8,1,64]{2,1,0:T(1,128)}), f32[8,1,64]{2,1,0:T(1,128)S(1)}, u32[]{:S(2)}, u32[]{:S(2)}) async-start(f32[8,1,64]{2,1,0:T(1,128)} %bitcast.14), calls=%async_computation.16 | async-start | bytes 8192 | tf_op jit(solution)/shard_map/all_to_all | solution.py:459

commit v4 on v3

--- a/solution.py
+++ b/solution.py
@@ -61,9 +61,16 @@
     moves = copies(pairs, sems)
     for move in moves:
         move.start()
-    total = jnp.zeros((parts.shape[1], 1), F32)
-    for j in range(XS):
-        h = parts[j].astype(F32)
+    tokens = q_out.shape[0]
+    outs = []
+    for d in range(DP):
+        outs.append((normed_v.at[:, pl.ds(d * piece, piece)], pack.at[d, :, pl.ds(0, piece)]))
+    for d in range(DP):
+        outs.append((mix_v, pack.at[d, :, pl.ds(piece, mix_v.shape[1])]))
+    outs = copies(outs, out_sems)
+    total = jnp.zeros((tokens, 1), F32)
+    for j in range(XS):
+        h = parts[j, :tokens, :].astype(F32)
         total = total + jnp.sum(h * h, -1, keepdims=True)
     scale = lax.rsqrt(total / width + EPS)
     scale_out[...] = scale
@@ -71,12 +78,14 @@
     kv = jnp.zeros(kv_out.shape, F32)
     for j in range(XS):
         span = slice(j * block, (j + 1) * block)
-        normed = (parts[j].astype(F32) * scale * gain[:, span].astype(F32)).astype(BF16)
+        normed = (parts[j, :tokens, :].astype(F32) * scale * gain[:, span].astype(F32)).astype(BF16)
         normed_v[:, span] = normed
         moves[2 * j].wait()
         q = q + dot(normed, wq_v[span, :])
         moves[2 * j + 1].wait()
         kv = kv + dot(normed, wkv_v[span, :])
+    for move in outs[:DP]:
+        move.start()
     q = q.astype(BF16)
     kv = kv.astype(BF16)
     q_out[...] = q
@@ -96,15 +105,8 @@
         mixes.append(heads_across(dot(attn.astype(BF16), values).astype(BF16), length))
     mix = jnp.concatenate(mixes, axis=0)
     mix_v[...] = mix
-    outs = []
-    for d in range(DP):
-        outs.append((normed_v.at[:, pl.ds(d * piece, piece)], pack.at[d, :, pl.ds(0, piece)]))
-        outs.append((mix_v, pack.at[d, :, pl.ds(piece, mix.shape[1])]))
-    outs = copies(outs, out_sems)
-
-    for move in outs:
+    for move in outs[DP:]:
         move.start()
-
     if project:
         for j in range(XS):
             moves[2 * XS + j].wait()
@@ -121,7 +123,7 @@
     if onward:
         send, rest = rest[0], rest[1:]
     pack, wq_v, wkv_v, wo_v, qg_v, pg_v, gain_v, gain_pair_v, sems, out_sems = rest
-    tokens, block = parts.shape[1:]
+    tokens, block = q_in.shape[0], parts.shape[2]
     width = XS * block
     piece = width // DP
     qs, kvs = qg_v.shape[1], pg_v.shape[1]
@@ -136,26 +138,17 @@
     moves = copies(pairs, sems)
     for move in moves:
         move.start()
-    real = pl.ds(0, tokens)
     outs = []
-    for d in range(DP):
-        outs.append(
-            (grads.at[d // 2, :, pl.ds(d % 2 * piece, piece)], pack.at[d, real, pl.ds(0, piece)])
-        )
-    for d in range(DP):
-        outs.append((qg_v, pack.at[d, real, pl.ds(piece, qs)]))
-        outs.append((pg_v, pack.at[d, real, pl.ds(piece + qs, kvs)]))
-    for d in range(DP):
-        outs.append((gain_pair_v, pack.at[d, pl.ds(tokens, 16), pl.ds(0, piece)]))
+    for d in range(XS):
+        outs.append((qg_v, pack.at[d, pl.ds(0, tokens), pl.ds(0, qs)]))
+        outs.append((pg_v, pack.at[d, pl.ds(0, tokens), pl.ds(qs, kvs)]))
+    for d in range(XS):
+        outs.append((gain_pair_v, pack.at[d, pl.ds(tokens, 2 * DP), pl.ds(0, piece)]))
     outs = copies(outs, out_sems)
-
-    for move in outs[:DP]:
-        move.start()
-
     mix_grad = jnp.zeros(q_in.shape, F32)
     for j in range(XS):
         moves[j].wait()
-        mix_grad = mix_grad + dot(grads[j], wo_v[:, j * block : (j + 1) * block], ((1,), (1,)))
+        mix_grad = mix_grad + dot(grads[j, :tokens, :], wo_v[:, j * block : (j + 1) * block], ((1,), (1,)))
     mix_grad = mix_grad.astype(BF16)
     q = q_in[...]
     kv = kv_in[...]
@@ -177,7 +170,7 @@
     qg_v[...] = query_grad
     pg_v[...] = pair_grad
 
-    for move in outs[DP : 3 * DP]:
+    for move in outs[: 2 * XS]:
         move.start()
 
     scale = scale_in[...]
@@ -192,7 +185,7 @@
         normed_grad = dot(query_grad, wq_v[span, :], ((1,), (1,))) + dot(
             pair_grad, wkv_v[span, :], ((1,), (1,))
         )
-        h = parts[j].astype(F32)
+        h = parts[j, :tokens, :].astype(F32)
         scaled = normed_grad * scale
         part = jnp.sum(scaled * h, 0, keepdims=True)
         gain_v[2 * j : 2 * j + 1, :] = part[:, :piece]
@@ -204,46 +197,65 @@
     low = (terms - high.astype(F32)).astype(BF16)
     gain_pair_v[...] = jnp.concatenate([high, low], axis=0)
 
-    for move in outs[3 * DP :]:
+    for move in outs[2 * XS :]:
         move.start()
     for move in outs:
         move.wait()
 
 
-def weights_kernel(
-    last, station, early, late, got, grad_query, grad_pair, grad_out, factors, wide_v, out_v, sem, sems
-):
+def weights_kernel(last, own, here, early, late, g, grads, *rest):
     tokens = early.shape[1]
-    piece = grad_query.shape[0]
-    qs = grad_query.shape[1]
-    load = copies([(early, factors), (late, factors)], [sem.at[0], sem.at[0]])
-
-    @pl.when(station[0] != last)
+    count, piece = g.shape[0], early.shape[2] // 2
+    qs = early.shape[2] - piece
+    if own:
+        total, factors, wide, sems = rest
+    else:
+        before, grad_query, grad_pair, grad_out, factors, wide, out_v, pair_v, sems, out_sems = rest
+    core = here[1] if own else 1 - here[1]
+    load = [
+        copies([(source.at[2 * i + core], factors.at[i]) for i in range(count)], sems)
+        for source in (early, late)
+    ]
+
+    @pl.when(here[0] != last)
     def _():
-        load[0].start()
-
-    @pl.when(station[0] == last)
+        for move in load[0]:
+            move.start()
+
+    @pl.when(here[0] == last)
     def _():
-        load[1].start()
-
-    for d in range(DP):
-        wide_v[d * tokens : (d + 1) * tokens, :] = got[d, :tokens, :]
-    load[0].wait()
-    flat = factors[...].reshape(DP * tokens, factors.shape[2])
-    wide = wide_v[...]
-    kvs = grad_pair.shape[1]
-    out_v[:, :qs] = dot(flat[:, piece:], wide[:, :piece], ((0,), (0,)))
+        for move in load[1]:
+            move.start()
+
+    for i in range(count):
+        rows = slice(i * tokens, (i + 1) * tokens)
+        part = g[i, :tokens, :]
+        part = jnp.where(here[1] == 0, part[:, :piece], part[:, piece:])
+        wide[rows, :piece] = part
+        wide[rows, piece:] = grads[i, :tokens, :]
+    for move in load[0]:
+        move.wait()
+    flat = factors[...].reshape(count * tokens, factors.shape[2])
+    if own:
+        total[:, :piece] = dot(flat[:, piece:], wide[:, :piece], ((0,), (0,)))
+        total[:, piece:] = dot(flat[:, :piece], wide[:, piece:], ((0,), (0,)))
+        return
     outs = copies(
         [
             (out_v.at[:, pl.ds(0, piece)], grad_out),
             (out_v.at[:, pl.ds(piece, qs)], grad_query),
-            (out_v.at[:, pl.ds(piece + qs, kvs)], grad_pair),
+            (pair_v, grad_pair),
         ],
-        sems,
-    )
+        out_sems,
+    )
+    out_v[:, :piece] = before[:, :piece] + dot(flat[:, piece:], wide[:, :piece], ((0,), (0,)))
     outs[0].start()
-    out_v[:, piece:] = dot(flat[:, :piece], wide[:, piece:], ((0,), (0,)))
+    terms = before[:, piece:] + dot(flat[:, :piece], wide[:, piece:], ((0,), (0,)))
+    out_v[:, piece:] = terms[:, :qs]
     outs[1].start()
+    for i in range(terms.shape[1] // HEAD_DIM - qs // HEAD_DIM):
+        at = qs + i * HEAD_DIM
+        pair_v[pl.ds(i, piece, stride=2), :] = terms[:, at : at + HEAD_DIM]
     outs[2].start()
     for move in outs:
         move.wait()
@@ -276,10 +288,6 @@
     return lax.all_to_all(spread, "x", 0, 0)
 
 
-def scatter_x(parts):
-    return jnp.sum(lax.all_to_all(parts, "x", 0, 0).astype(F32), 0)
-
-
 def hop(block, source, target):
     got = []
     for cross in range(HALVES):
@@ -303,16 +311,42 @@
     )()
 
 
-def pair_up(block, sections):
+def start_kernel(here, hidden, grads, gains, out):
+    rows, length, _ = hidden.shape
+    for row in range(rows):
+        mine = jnp.where(here[0] == 0, hidden[row], grads[row])
+        out[row * length : (row + 1) * length, :] = mine
+    tall = (out.shape[0] - rows * length, out.shape[1])
+    out[rows * length :, :] = jnp.broadcast_to(gains[...].astype(F32), tall).astype(BF16)
+
+
+def pair_kernel(here, mine, other, spread):
+    width = mine.shape[1]
+    first = here[2] == 0
+    left = jnp.where(first, mine[...], other[...])
+    right = jnp.where(first, other[...], mine[...])
+    for j in range(XS):
+        spread[j, :, :width] = left
+        spread[j, :, width:] = right
+
+
+def sum_kernel(tokens, sums, block, out):
+    total = 0.5 * block[0, :tokens, :].astype(F32)
+    for j in range(XS):
+        total = total + sums[j].astype(F32)
+    out[...] = total.astype(BF16)
+
+
+def pair_up(start, here):
     route = [
         (place(s, x, half), place(s, x, 1 - half))
-        for s in sections
+        for s in range(SECTIONS)
         for x in range(XS)
         for half in range(HALVES)
     ]
-    other = lax.ppermute(block, ("s", "x", "zh"), route)
-    first = lax.axis_index("zh") == 0
-    return jnp.concatenate([jnp.where(first, block, other), jnp.where(first, other, block)], -1)
+    other = lax.ppermute(start, ("s", "x", "zh"), route)
+    spread = jax.ShapeDtypeStruct((XS, start.shape[0], 2 * start.shape[1]), BF16)
+    return call(pair_kernel, [SMEM, VMEM, VMEM], [(spread, VMEM)], [], 2**20, (here, start, other))[0]
 
 
 def shards(hidden_in, lengths, gains, w_query, w_keyval, w_out, grad_out):
@@ -328,23 +362,27 @@
     flops = 2 * tokens * width * (2 * qs + kvs)
     tall = qs // HEAD_DIM * length
 
-    start = jnp.where(
-        station == 0, hidden_in.reshape(tokens, shard), grad_out.reshape(tokens, shard)
-    )
-    start = jnp.concatenate([start, jnp.broadcast_to(gains, (16, shard))], 0)
-    start_block = pair_up(start, range(SECTIONS))
-    start_full = gather_x(jnp.broadcast_to(start_block[None], (XS,) + start_block.shape))
+    here = jnp.stack([station, lax.axis_index("core"), lax.axis_index("zh")])
+    start = call(
+        start_kernel,
+        [SMEM] + [VMEM] * 3,
+        [(jax.ShapeDtypeStruct((tokens + 16, shard), BF16), VMEM)],
+        [],
+        2**20,
+        (here, hidden_in, grad_out, gains),
+    )[0]
+    start_spread = pair_up(start, here)
+    start_full = gather_x(start_spread)
+    first_block = start_spread
     gain = start_full[:, tokens, :].reshape(1, width)
-    first = start_full[:, :tokens]
-    first_block = start_block[:tokens]
+    first = start_full
 
     shape = jax.ShapeDtypeStruct
     dma = lambda count: pltpu.SemaphoreType.DMA((count,))
-    here = station.reshape(1)
     piece = width // DP
     sent = (shape((XS, tokens, block_width), BF16), VMEM)
     early_pack = (shape((DP, tokens, piece + qs), BF16), HBM)
-    late_pack = (shape((DP, tokens + 16, piece + qs + kvs), BF16), HBM)
+    late_pack = (shape((XS, tokens + 2 * DP, qs + kvs), BF16), HBM)
     saved = [
         (shape((tokens, 1), F32), VMEM),
         (shape((tokens, qs), BF16), VMEM),
@@ -382,13 +420,20 @@
             + held_out
             + [pltpu.VMEM((tokens, qs), BF16), pltpu.VMEM((tokens, kvs), BF16)]
             + [pltpu.VMEM((DP, piece), F32), pltpu.VMEM((2 * DP, piece), BF16)]
-            + [dma(3 * XS), dma(4 * DP)],
+            + [dma(3 * XS), dma(3 * XS)],
             flops,
             (parts_grad, kept[0], gain) + tuple(kept[1:]) + (wq, wkv, wo),
         )
 
     def pass_on(block, sums):
-        return (0.5 * block.astype(F32) + scatter_x(sums)).astype(BF16)
+        return call(
+            functools.partial(sum_kernel, tokens),
+            [VMEM] * 2,
+            [(block_out[0], VMEM)],
+            [],
+            2**20,
+            (gather_x(sums), block),
+        )[0]
 
     kept = []
     packed = None
@@ -400,16 +445,16 @@
                 parts, block = first, first_block
             else:
                 spread = combine(*arrived)
-                parts, block = gather_x(spread), spread[0]
+                parts, block = gather_x(spread), spread
             got = forward(parts, True)
-            return pass_on(block, got[0]), got[1], [parts] + list(got[2:])
+            return pass_on(block, got[0]), got[1], [parts] * (step > 0) + list(got[2:])
 
         def rest(packed, arrived):
-            empty = nothing(block_out, early_pack, parts_out, *saved)
+            empty = nothing(block_out, early_pack, *[parts_out] * (step > 0), *saved)
             return empty[0], empty[1] if packed is None else packed, list(empty[2:])
 
         block, packed, saved_here = lax.cond(station == step, work, rest, packed, arrived)
-        kept.append(saved_here)
+        kept.append(saved_here if step else [first] + saved_here)
         arrived = hop(block, step, step + 1)
 
     def turn(packed, arrived):
@@ -429,6 +474,9 @@
     )
     arrived = hop(block, last_section, last_section - 1)
 
+    over_y = lambda v: lax.all_to_all(v, "y", 0, 0)
+    swap = lambda v: lax.ppermute(v, "core", [(0, 1), (1, 0)])
+    g_kept = first[:, :tokens]
     for step in reversed(range(last_section)):
         onward = step > 0
         if not onward:
@@ -437,43 +485,63 @@
             )
             late, *arrived = lax.optimization_barrier([late] + list(arrived))
 
-        def work(pack, arrived, kept_here):
+        def work(pack, g_kept, arrived, kept_here):
             spread = combine(*arrived)
-            got = backward(gather_x(spread), kept_here, onward)
-            return ([pass_on(spread[0], got[0])] if onward else []) + [got[onward]]
-
-        def rest(pack, arrived, kept_here):
-            return ([nothing(block_out)[0]] if onward else []) + [pack]
-
-        got = lax.cond(station == step, work, rest, pack, arrived, kept[step])
-        pack = got[-1]
+            g = gather_x(spread)
+            got = backward(g, kept_here, onward)
+            if onward:
+                return got[1], g, pass_on(spread, got[0])
+            return got[0], over_y(g)
+
+        def rest(pack, g_kept, arrived, kept_here):
+            return (pack, g_kept, nothing(block_out)[0]) if onward else (pack, over_y(g_kept))
+
+        got = lax.cond(station == step, work, rest, pack, g_kept, arrived, kept[step])
+        pack, g_kept = got[:2]
         if onward:
-            arrived = hop(got[0], step, step - 1)
-
-    got = over_dp(pack)
-    terms = got[:, tokens:, :piece].astype(F32).reshape(DP, 2, DP, piece)
-    terms = jnp.sum(terms, (0, 1))
+            arrived = hop(got[2], step, step - 1)
+
+    g_own = g_kept
+    g_other = swap(g_own)
+    own = over_y(pack)
+    other = swap(own)
+    terms = 0.0
+    for item in (own, other):
+        item = item[:, tokens:, :piece].astype(F32).reshape(XS, 2, DP, piece)
+        terms = terms + jnp.sum(item, (0, 1))
     small = piece // DP
-    own = lax.axis_index(("y", "core")) * small
-    terms = lax.dynamic_slice_in_dim(terms, own, small, 1).reshape(DP, 1, small)
-    gain_grad = jnp.sum(lax.all_to_all(terms, ("x", "zh"), 0, 0), 0)
+    terms = lax.dynamic_slice_in_dim(terms, lax.axis_index(("y", "core")) * small, small, 1)
+    gain_grad = jnp.sum(lax.all_to_all(terms.reshape(DP, 1, small), ("x", "zh"), 0, 0), 0)
+    everything = piece + qs + kvs
+    scratch = [
+        pltpu.VMEM((XS, tokens, piece + qs), BF16),
+        pltpu.VMEM((XS * tokens, everything), BF16),
+    ]
+    total = call(
+        functools.partial(weights_kernel, last_section, True),
+        [SMEM, HBM, HBM, VMEM, VMEM],
+        [(shape((piece, everything), F32), VMEM)],
+        scratch + [dma(XS)],
+        flops,
+        (here, early, late, g_own, own),
+    )[0]
     grad_query, grad_pair, grad_out_weight = call(
-        functools.partial(weights_kernel, last_section),
-        [SMEM, HBM, HBM, VMEM],
+        functools.partial(weights_kernel, last_section, False),
+        [SMEM, HBM, HBM, VMEM, VMEM, VMEM],
         [
             (shape((piece, qs), F32), HBM),
-            (shape((piece, kvs), F32), HBM),
+            (shape((piece * kvs // HEAD_DIM, HEAD_DIM), F32), HBM),
             (shape((qs, piece), F32), HBM),
         ],
-        [
-            pltpu.VMEM((DP, tokens, piece + qs), BF16),
-            pltpu.VMEM((DP * tokens, piece + qs + kvs), BF16),
-            pltpu.VMEM((piece, piece + qs + kvs), F32),
-            dma(1),
+        scratch
+        + [
+            pltpu.VMEM((piece, piece + qs), F32),
+            pltpu.VMEM((piece * kvs // HEAD_DIM, HEAD_DIM), F32),
+            dma(XS),
             dma(3),
         ],
         flops,
-        (here, early, late, got),
+        (here, early, late, g_other, other, total),
     )
     return (
         grad_query[None],

time: 392 us -> 366 us (0.934)
  waiting for transfers between devices: 274 us -> 222 us
  blocking collectives: 12.2 us -> 40.5 us
  Pallas kernels: 20.7 us -> 28.5 us
  starting transfers between devices: 71.4 us -> 64.9 us
    all_to_all x2 -> x1, waiting for transfers between devices: 61.9 us -> 26.4 us  [shards(): over_dp = lambda v: lax.all_to_all(v, ('y', 'core'), 0, 0)]
    all_to_all x2 -> x1, starting transfers between devices: 35.4 us -> 8.93 us  [shards(): over_dp = lambda v: lax.all_to_all(v, ('y', 'core'), 0, 0)]
    ppermute x1 -> x3, starting transfers between devices: 7.83 us -> 31.2 us  [the longest x2 23.4 us: shards(): swap = lambda v: lax.ppermute(v, 'core', [(0, 1), (1, 0)])]
    all_to_all x1 -> x2, blocking collectives: 12.2 us -> 28.2 us  [gather_x(): return lax.all_to_all(spread, 'x', 0, 0)]
    all_to_all x0 -> x1, blocking collectives: none -> 12.3 us  [shards(): over_y = lambda v: lax.all_to_all(v, 'y', 0, 0)]
    all_to_all x2, waiting for transfers between devices: 14.7 us -> 4.99 us  [the longest x1 4.01 us: shards(): lax.all_to_all(terms.reshape(DP, 1, small), ('x', 'zh'), 0, 0)]
    pallas_call x4 -> x8, Pallas kernels: 20.7 us -> 28.5 us  [call(): pl.pallas_call(kernel, out_shape=[out for out, _ in outs], in_specs=ins,...]
    ppermute x12, waiting for transfers between devices: 179 us -> 172 us  [hop(): got.append(lax.ppermute(block, ('s', 'x', 'zh'), route))]
  transfers between devices with their start and end apart: 18 -> 19, of which waited for: 10 -> 9; matrix products, arithmetic and copies ran while one was open for 1% -> 0% of each run, Pallas kernels for 1% -> 5%
where the time goes in v4:
time: 366 us; the launch traced here: 365 us
  waiting for transfers between devices  222 us (61%)
  starting transfers between devices  64.9 us (18%)
  blocking collectives  40.5 us (11%)
  Pallas kernels  28.5 us (8%)
  local copies, waits for them, and re-layouts  5.73 us (2%)
    ppermute x12, waiting for transfers between devices, hop(): got.append(lax.ppermute(block, ('s', 'x', 'zh'), route))  172 us
    pallas_call x8, Pallas kernels, call(): pl.pallas_call(kernel, out_shape=[out for out, _ in outs], in_specs=ins,...  28.5 us
    all_to_all x2, blocking collectives, gather_x(): return lax.all_to_all(spread, 'x', 0, 0)  28.2 us
    all_to_all x1, waiting for transfers between devices, shards(): over_dp = lambda v: lax.all_to_all(v, ('y', 'core'), 0, 0)  26.4 us
    ppermute x2, starting transfers between devices, shards(): swap = lambda v: lax.ppermute(v, 'core', [(0, 1), (1, 0)])  23.4 us
    all_to_all x1, waiting for transfers between devices, gather_x(): return lax.all_to_all(spread, 'x', 0, 0)  15 us
    all_to_all x1, blocking collectives, shards(): over_y = lambda v: lax.all_to_all(v, 'y', 0, 0)  12.3 us
    ppermute x12, starting transfers between devices, hop(): got.append(lax.ppermute(block, ('s', 'x', 'zh'), route))  10.8 us
  transfers between devices with their start and end apart: 19, of which 9 were waited for; matrix products, arithmetic and copies ran while one was open for 0% of the time, Pallas kernels for 5%

profile of v4, /device:TPU:1, one launch (start us, length us, event | category | flops | bytes accessed | tf_op | source)
XLA Modules:
  0.0 365.0 jit_solution(5714310557312575864)
XLA Ops:
  0.6 0.1 pad_add_fusion.here
  0.7 0.9 copy-done
  1.6 0.9 copy-done.1
  2.5 0.7 copy-done.2
  3.2 0.6 shard_map.102.mine
  3.8 7.8 %collective-permute-start = (bf16[144,512]{1,0:T(8,128)(2,1)S(1)}, bf16[144,512]{1,0:T(8,128)(2,1)S(1)}, u32[]{:S(2)}, u32[]{:S(2)}) collective-permute-start(bf16[144,512]{1,0:T(8,128)(2,1)S(1)} %shard_map.102.mine), channel_id=1, source_target_pairs={{0,8},{8,0},{16,24},{24,16},{32,40},{40,32},{48,56},{56,48},{64,72... | collective-permute-start | bytes 442376 | tf_op jit(solution)/shard_map/ppermute | solution.py:347
  11.6 3.0 collective-permute-done.other
  14.6 1.7 shard_map.103
  16.4 4.6 %all-to-all-start.16 = ((bf16[4,144,1024]{2,1,0:T(8,128)(2,1)}), bf16[4,144,1024]{2,1,0:T(8,128)(2,1)}, u32[]{:S(2)}, u32[]{:S(2)}) async-start(bf16[4,144,1024]{2,1,0:T(8,128)(2,1)} %shard_map.103), calls=%async_computation.16 | async-start | bytes 2359296 | tf_op jit(solution)/shard_map/all_to_all | solution.py:288
  20.9 15.0 %all-to-all-done.16 = bf16[4,144,1024]{2,1,0:T(8,128)(2,1)} async-done(((bf16[4,144,1024]{2,1,0:T(8,128)(2,1)}), bf16[4,144,1024]{2,1,0:T(8,128)(2,1)}, u32[]{:S(2)}, u32[]{:S(2)}) %all-to-all-start.16) | async-done | bytes 1179680 | tf_op jit(solution)/shard_map/all_to_all | solution.py:288
  35.9 0.9 slice.16
  36.8 23.2 %conditional.8 = (bf16[128,1024]{1,0:T(8,128)(2,1)S(1)}, f32[128,1]{1,0:T(8,128)}, bf16[128,512]{1,0:T(8,128)(2,1)}, bf16[128,256]{1,0:T(8,128)(2,1)}, f32[2,256...) conditional(s32[]{:T(128)} %convert_element_type.25, () %tuple.75, (s32[2]{0:T(128)S(1)}, ...), branch_computations={%region_0.0_spmd, %region_1.0_spmd} | conditional | flops 1343225856 | bytes 31981644 | solution.py:456
  36.8 7.8 %branch_1_fun.21 = (bf16[4,128,1024]{2,1,0:T(8,128)(2,1)S(1)}, bf16[8,128,1024]{2,1,0:T(8,128)(2,1)}, f32[128,1]{1,0:T(8,128)}, bf16[128,512]{1,0:T(8,128)(2,1)}...) custom-call(s32[2]{0:T(128)S(1)} %get-tuple-element.159.lens, bf16[4,144,1024]{2,1,0:T(8,128)(2,1)} %get-tuple-element.160.parts, ...), custom_call_target="tpu_custom_call" | custom-call | flops 1342177280 | bytes 12582912 | tf_op jit(solution)/shard_map/cond/branch_1_fun/pallas_call | solution.py:271
  44.6 15.1 %all_to_all.79.sums = bf16[4,128,1024]{2,1,0:T(8,128)(2,1)S(1)} all-to-all(bf16[4,128,1024]{2,1,0:T(8,128)(2,1)S(1)} %get-tuple-element.165), channel_id=1, replica_groups=mesh['s'=4,'x'=4,'zh'=2,'y'=4,'core'=2] {'x'}, dimensions={0} | all-to-all | bytes 2097152 | tf_op jit(solution)/shard_map/cond/branch_1_fun/all_to_all | solution.py:288
  59.8 0.2 branch_1_fun.22
  60.0 1.3 collective-permute-start.2
  61.3 1.3 collective-permute-start.1
  62.6 2.0 collective-permute-done.2
  64.6 1.3 collective-permute-done.1
  65.9 0.7 collective-permute-start.4
  66.6 0.7 collective-permute-start.3
  67.3 0.0 collective-permute-done.4
  67.3 0.0 collective-permute-done.3
  67.3 0.9 collective-permute-start.6
  68.2 0.7 collective-permute-start.5
  68.9 0.0 collective-permute-done.6
  68.9 0.0 collective-permute-done.5
  68.9 35.4 %conditional.11 = (bf16[128,1024]{1,0:T(8,128)(2,1)}, bf16[4,144,768]{2,1,0:T(8,128)(2,1)}, bf16[8,128,1024]{2,1,0:T(8,128)(2,1)}, bf16[8,128,1024]{2,1,0:T(8,128)(2,1)}) conditional(s32[]{:T(128)} %convert_element_type.22, bf16[8,128,1024]{2,1,0:T(8,128)(2,1)} %get-tuple-element.318, (bf16[128,1024]{1,0:T(8,128)(2,1)S(1)}, ...), branch_computations={%region_6.0_spmd, %region_7.0_spmd} | conditional | flops 2686451712 | bytes 89129080 | solution.py:472
  68.9 8.9 %all-to-all-start.5 = ((bf16[8,128,1024]{2,1,0:T(8,128)(2,1)}), bf16[8,128,1024]{2,1,0:T(8,128)(2,1)}, u32[]{:S(2)}, u32[]{:S(2)}) async-start(bf16[8,128,1024]{2,1,0:T(8,128)(2,1)} %param.6), calls=%async_computation.5 | async-start | bytes 4194304 | tf_op jit(solution)/shard_map/cond/branch_0_fun/all_to_all | solution.py:394
  77.8 26.4 %all-to-all-done.5 = bf16[8,128,1024]{2,1,0:T(8,128)(2,1)} async-done(((bf16[8,128,1024]{2,1,0:T(8,128)(2,1)}), bf16[8,128,1024]{2,1,0:T(8,128)(2,1)}, u32[]{:S(2)}, u32[]{:S(2)}) %all-to-all-start.5) | async-done | bytes 2097184 | tf_op jit(solution)/shard_map/cond/branch_0_fun/all_to_all | solution.py:394
  104.3 0.7 collective-permute-start.8
  104.9 0.7 collective-permute-start.7
  105.6 0.0 collective-permute-done.8
  105.6 0.0 collective-permute-done.7
  105.6 2.4 conditional.13
  105.7 2.4 slice.9
  108.0 0.7 collective-permute-start.10
  108.7 0.7 collective-permute-start.9
  109.4 0.0 collective-permute-done.10
  109.4 0.0 collective-permute-done.9
  109.4 0.2 conditional.14
  109.7 1.3 collective-permute-start.12
  111.0 1.3 collective-permute-start.11
  112.3 0.0 copy-start.15
  112.3 168.7 %collective-permute-done.12 = bf16[128,1024]{1,0:T(8,128)(2,1)} collective-permute-done((bf16[128,1024]{1,0:T(8,128)(2,1)}, bf16[128,1024]{1,0:T(8,128)(2,1)}, u32[]{:S(2)}, u32[]{:S(2)}) %collective-permute-start.12) | collective-permute-done | bytes 262176 | tf_op jit(solution)/shard_map/ppermute | solution.py:299
  281.0 0.5 collective-permute-done.11
  281.5 28.8 %conditional.15 = (bf16[4,144,768]{2,1,0:T(8,128)(2,1)}, bf16[4,128,1024]{2,1,0:T(8,128)(2,1)}) conditional(s32[]{:T(128)} %convert_element_type.25, (bf16[4,128,1024]{2,1,0:T(8,128)(2,1)S(1)}, bf16[4,144,768]{2,1,0:T(8,128)(2,1)}) %tuple.129, (bf16[128,1024]{1,0:T(8,128)(2,1)}, bf16[128,1024]{1,0:T(8,128)(2,1)}, bf16[4,144,1024]{2,1,0:T(8,128)(2,1)}, ...), branch_computations={%region_14.0_spmd, %region_15.0_spmd} | conditional | flops 1343225856 | bytes 31195240 | solution.py:499
  281.5 1.1 branch_1_fun.40
  282.6 13.0 %all_to_all.91.grads = bf16[4,128,1024]{2,1,0:T(8,128)(2,1)} all-to-all(bf16[4,128,1024]{2,1,0:T(8,128)(2,1)S(1)} %branch_1_fun.40), channel_id=1, replica_groups=mesh['s'=4,'x'=4,'zh'=2,'y'=4,'core'=2] {'x'}, dimensions={0} | all-to-all | bytes 2097152 | tf_op jit(solution)/shard_map/cond/branch_1_fun/all_to_all | solution.py:288
  295.6 4.8 %all-to-all-start.15 = ((bf16[4,128,1024]{2,1,0:T(8,128)(2,1)}), bf16[4,128,1024]{2,1,0:T(8,128)(2,1)}, u32[]{:S(2)}, u32[]{:S(2)}) async-start(bf16[4,128,1024]{2,1,0:T(8,128)(2,1)} %all_to_all.91.grads), calls=%async_computation.15 | async-start | bytes 2097152 | tf_op jit(solution)/shard_map/cond/branch_1_fun/all_to_all | solution.py:477
  300.5 8.9 %branch_1_fun.41 = bf16[4,144,768]{2,1,0:T(8,128)(2,1)} custom-call(bf16[4,128,1024]{2,1,0:T(8,128)(2,1)} %all_to_all.91.grads, bf16[4,144,1024]{2,1,0:T(8,128)(2,1)} %get-tuple-element.263.parts, bf16[1,4096]{1,0:T(2,128)(2,1)S(1)} %get-tuple-element.264.gain, f32[128,1]{1,0:T(8,128)S(1)} %get-tuple-element.265.scale_in, bf16[128,512]{1,0:T(8,128)(2,1)S(1)} %copy-done.18, ...), custom_call_target="tpu_custom_call" | custom-call | flops 1342177280 | bytes 12582912 | tf_op jit(solution)/shard_map/cond/branch_1_fun/pallas_call | solution.py:271
  309.3 1.0 all-to-all-done.15
  310.3 12.3 %all_to_all.92.grads = bf16[4,144,768]{2,1,0:T(8,128)(2,1)S(1)} all-to-all(bf16[4,144,768]{2,1,0:T(8,128)(2,1)} %get-tuple-element.348), channel_id=1, replica_groups=mesh['s'=4,'x'=4,'zh'=2,'y'=4,'core'=2] {'y'}, dimensions={0} | all-to-all | bytes 1769472 | tf_op jit(solution)/shard_map/all_to_all | solution.py:477
  322.6 23.4 %collective-permute-start.14 = (bf16[4,144,768]{2,1,0:T(8,128)(2,1)S(1)}, bf16[4,144,768]{2,1,0:T(8,128)(2,1)}, u32[]{:S(2)}, u32[]{:S(2)}) collective-permute-start(bf16[4,144,768]{2,1,0:T(8,128)(2,1)S(1)} %all_to_all.92.grads), channel_id=1, source_target_pairs={{0,1},{1,0},{2,3},{3,2},{4,5},{5,4},{6,7},{7,6},{8,9},{9,8},{10,11... | collective-permute-start | bytes 2654216 | tf_op jit(solution)/shard_map/ppermute | solution.py:478
  346.0 0.0 collective-permute-start.13
  346.0 3.4 shard_map.104.rest_0_
  349.4 0.0 collective-permute-done.14.grads
  349.4 0.9 convert_reduce_fusion
  350.3 0.7 dynamic-slice_add_fusion
  351.0 4.6 %all-to-all-start.18 = ((f32[8,1,64]{2,1,0:T(1,128)}), f32[8,1,64]{2,1,0:T(1,128)S(1)}, u32[]{:S(2)}, u32[]{:S(2)}) async-start(f32[8,1,64]{2,1,0:T(1,128)} %bitcast.12), calls=%async_computation.18 | async-start | bytes 8192 | tf_op jit(solution)/shard_map/all_to_all | solution.py:514
  355.6 0.0 collective-permute-done.13.g
  355.6 4.9 %shard_map.105 = (f32[512,512]{1,0:T(8,128)}, f32[1024,128]{1,0:T(8,128)}, f32[512,512]{1,0:T(8,128)}) custom-call(s32[3]{0:T(128)S(1)} %pad_add_fusion.here, bf16[8,128,1024]{2,1,0:T(8,128)(2,1)} %get-tuple-element.320.early, bf16[8,128,1024]{2,1,0:T(8,128)(2,1)} %get-tuple-element.428.late, bf16[4,128,1024]{2,1,0:T(8,128)(2,1)} %collective-permute-done.13.g, ...), custom_call_target="tpu_custom_call" | custom-call | flops 1342177280 | bytes 12582912 | tf_op jit(solution)/shard_map/pallas_call | solution.py:271
  360.5 4.0 %all-to-all-done.18 = f32[8,1,64]{2,1,0:T(1,128)S(1)} async-done(((f32[8,1,64]{2,1,0:T(1,128)}), f32[8,1,64]{2,1,0:T(1,128)S(1)}, u32[]{:S(2)}, u32[]{:S(2)}) %all-to-all-start.18) | async-done | bytes 2080 | tf_op jit(solution)/shard_map/all_to_all | solution.py:514
  364.5 0.5 reduce_sum.49
  (30 shorter events, 0.1 us)
Async XLA Ops:
  0.7 0.9 copy-start
  1.6 0.9 copy-start.1
  2.5 0.7 copy-start.2
  3.2 33.6 %copy-start.5 = (bf16[1,4096,1,256]{3,1,2,0:T(8,128)(2,1)S(1)}, bf16[1,4096,1,256]{3,1,2,0:T(8,128)(2,1)}, u32[]{:S(2)}) copy-start(bf16[1,4096,1,256]{3,1,2,0:T(8,128)(2,1)} %param.27) | copy-start | bytes 6291460
  3.2 33.6 %copy-start.24 = (s32[2]{0:T(128)S(1)}, s32[2]{0:T(128)}, u32[]{:S(2)}) copy-start(s32[2]{0:T(128)} %param.24) | copy-start | bytes 28
  3.8 10.9 %collective-permute-start = (bf16[144,512]{1,0:T(8,128)(2,1)S(1)}, bf16[144,512]{1,0:T(8,128)(2,1)S(1)}, u32[]{:S(2)}, u32[]{:S(2)}) collective-permute-start(bf16[144,512]{1,0:T(8,128)(2,1)S(1)} %shard_map.102.mine), channel_id=1, source_target_pairs={{0,8},{8,0},{16,24},{24,16},{32,40},{40,32},{48,56},{56,48},{64,72... | collective-permute-start | bytes 442376 | tf_op jit(solution)/shard_map/ppermute | solution.py:347
  16.4 19.6 %all-to-all-start.16 = ((bf16[4,144,1024]{2,1,0:T(8,128)(2,1)}), bf16[4,144,1024]{2,1,0:T(8,128)(2,1)}, u32[]{:S(2)}, u32[]{:S(2)}) async-start(bf16[4,144,1024]{2,1,0:T(8,128)(2,1)} %shard_map.103), calls=%async_computation.16 | async-start | bytes 2359296 | tf_op jit(solution)/shard_map/all_to_all | solution.py:288
  44.6 15.2 %copy-start.6 = (bf16[4,144,1024]{2,1,0:T(8,128)(2,1)S(1)}, bf16[4,144,1024]{2,1,0:T(8,128)(2,1)}, u32[]{:S(2)}) copy-start(bf16[4,144,1024]{2,1,0:T(8,128)(2,1)} %get-tuple-element.166.block) | copy-start | bytes 3538948 | tf_op jit(solution)/shard_map/cond
  60.0 4.6 %collective-permute-start.2 = (bf16[128,1024]{1,0:T(8,128)(2,1)S(1)}, bf16[128,1024]{1,0:T(8,128)(2,1)S(1)}, u32[]{:S(2)}, u32[]{:S(2)}) collective-permute-start(bf16[128,1024]{1,0:T(8,128)(2,1)S(1)} %get-tuple-element.315), channel_id=1, source_target_pairs={{0,72},{8,64},{16,88},{24,80},{32,104},{40,96},{48,120},{56,112},{... | collective-permute-start | bytes 786440 | tf_op jit(solution)/shard_map/ppermute | solution.py:299
  61.3 4.6 %collective-permute-start.1 = (bf16[128,1024]{1,0:T(8,128)(2,1)S(1)}, bf16[128,1024]{1,0:T(8,128)(2,1)S(1)}, u32[]{:S(2)}, u32[]{:S(2)}) collective-permute-start(bf16[128,1024]{1,0:T(8,128)(2,1)S(1)} %get-tuple-element.315), channel_id=1, source_target_pairs={{0,64},{8,72},{16,80},{24,88},{32,96},{40,104},{48,112},{56,120},{... | collective-permute-start | bytes 786440 | tf_op jit(solution)/shard_map/ppermute | solution.py:299
  65.9 1.4 collective-permute-start.4
  66.6 0.7 collective-permute-start.3
  67.3 1.6 collective-permute-start.6
  68.2 0.7 collective-permute-start.5
  68.9 35.4 %all-to-all-start.5 = ((bf16[8,128,1024]{2,1,0:T(8,128)(2,1)}), bf16[8,128,1024]{2,1,0:T(8,128)(2,1)}, u32[]{:S(2)}, u32[]{:S(2)}) async-start(bf16[8,128,1024]{2,1,0:T(8,128)(2,1)} %param.6), calls=%async_computation.5 | async-start | bytes 4194304 | tf_op jit(solution)/shard_map/cond/branch_0_fun/all_to_all | solution.py:394
  104.3 1.4 collective-permute-start.8
  104.9 0.7 collective-permute-start.7
  108.0 1.4 collective-permute-start.10
  108.7 0.7 collective-permute-start.9
  109.7 171.3 %collective-permute-start.12 = (bf16[128,1024]{1,0:T(8,128)(2,1)}, bf16[128,1024]{1,0:T(8,128)(2,1)}, u32[]{:S(2)}, u32[]{:S(2)}) collective-permute-start(bf16[128,1024]{1,0:T(8,128)(2,1)} %get-tuple-element.337), channel_id=1, source_target_pairs={{64,8},{72,0},{80,24},{88,16},{96,40},{104,32},{112,56},{120,48},{... | collective-permute-start | bytes 786440 | tf_op jit(solution)/shard_map/ppermute | solution.py:299
  111.0 170.5 %collective-permute-start.11 = (bf16[128,1024]{1,0:T(8,128)(2,1)}, bf16[128,1024]{1,0:T(8,128)(2,1)}, u32[]{:S(2)}, u32[]{:S(2)}) collective-permute-start(bf16[128,1024]{1,0:T(8,128)(2,1)} %get-tuple-element.337), channel_id=1, source_target_pairs={{64,0},{72,8},{80,16},{88,24},{96,32},{104,40},{112,48},{120,56},{... | collective-permute-start | bytes 786440 | tf_op jit(solution)/shard_map/ppermute | solution.py:299
  112.3 169.2 %copy-start.9 = (bf16[4,128,1024]{2,1,0:T(8,128)(2,1)S(1)}, bf16[4,128,1024]{2,1,0:T(8,128)(2,1)}, u32[]{:S(2)}) copy-start(bf16[4,128,1024]{2,1,0:T(8,128)(2,1)} %get-tuple-element.339) | copy-start | bytes 3145732
  112.3 169.2 %copy-start.15 = (f32[2,256,64]{2,1,0:T(8,128)S(1)}, f32[2,256,64]{2,1,0:T(8,128)}, u32[]{:S(2)}) copy-start(f32[2,256,64]{2,1,0:T(8,128)} %get-tuple-element.346) | copy-start | bytes 393220
  112.3 169.2 %copy-start.22 = (f32[128,1]{1,0:T(8,128)S(1)}, f32[128,1]{1,0:T(8,128)}, u32[]{:S(2)}) copy-start(f32[128,1]{1,0:T(8,128)} %get-tuple-element.343) | copy-start | bytes 1540
  282.6 17.9 %copy-start.18 = (bf16[128,512]{1,0:T(8,128)(2,1)S(1)}, bf16[128,512]{1,0:T(8,128)(2,1)}, u32[]{:S(2)}) copy-start(bf16[128,512]{1,0:T(8,128)(2,1)} %get-tuple-element.266.q_in) | copy-start | bytes 393220 | tf_op jit(solution)/shard_map/cond
  282.6 17.9 %copy-start.23 = (bf16[128,256]{1,0:T(8,128)(2,1)S(1)}, bf16[128,256]{1,0:T(8,128)(2,1)}, u32[]{:S(2)}) copy-start(bf16[128,256]{1,0:T(8,128)(2,1)} %get-tuple-element.267.kv_in) | copy-start | bytes 196612 | tf_op jit(solution)/shard_map/cond
  295.6 14.7 %all-to-all-start.15 = ((bf16[4,128,1024]{2,1,0:T(8,128)(2,1)}), bf16[4,128,1024]{2,1,0:T(8,128)(2,1)}, u32[]{:S(2)}, u32[]{:S(2)}) async-start(bf16[4,128,1024]{2,1,0:T(8,128)(2,1)} %all_to_all.91.grads), calls=%async_computation.15 | async-start | bytes 2097152 | tf_op jit(solution)/shard_map/cond/branch_1_fun/all_to_all | solution.py:477
  322.6 26.8 %collective-permute-start.14 = (bf16[4,144,768]{2,1,0:T(8,128)(2,1)S(1)}, bf16[4,144,768]{2,1,0:T(8,128)(2,1)}, u32[]{:S(2)}, u32[]{:S(2)}) collective-permute-start(bf16[4,144,768]{2,1,0:T(8,128)(2,1)S(1)} %all_to_all.92.grads), channel_id=1, source_target_pairs={{0,1},{1,0},{2,3},{3,2},{4,5},{5,4},{6,7},{7,6},{8,9},{9,8},{10,11... | collective-permute-start | bytes 2654216 | tf_op jit(solution)/shard_map/ppermute | solution.py:478
  346.0 9.6 %collective-permute-start.13 = (bf16[4,128,1024]{2,1,0:T(8,128)(2,1)}, bf16[4,128,1024]{2,1,0:T(8,128)(2,1)}, u32[]{:S(2)}, u32[]{:S(2)}) collective-permute-start(bf16[4,128,1024]{2,1,0:T(8,128)(2,1)} %get-tuple-element.347.g), channel_id=1, source_target_pairs={{0,1},{1,0},{2,3},{3,2},{4,5},{5,4},{6,7},{7,6},{8,9},{9,8},{10,11... | collective-permute-start | bytes 3145736 | tf_op jit(solution)/shard_map/ppermute | solution.py:478
  351.0 13.5 %all-to-all-start.18 = ((f32[8,1,64]{2,1,0:T(1,128)}), f32[8,1,64]{2,1,0:T(1,128)S(1)}, u32[]{:S(2)}, u32[]{:S(2)}) async-start(f32[8,1,64]{2,1,0:T(1,128)} %bitcast.12), calls=%async_computation.18 | async-start | bytes 8192 | tf_op jit(solution)/shard_map/all_to_all | solution.py:514

commit v5 on v4

--- a/solution.py
+++ b/solution.py
@@ -44,23 +44,10 @@
     if project:
         send, rest = rest[0], rest[1:]
     pack, scale_out, q_out, kv_out, attn_out = rest[:5]
-    wq_v, wkv_v, normed_v, mix_v, sems, out_sems = rest[5:11]
-    wo_v = rest[11] if project else None
+    normed_v, mix_v, out_sems = rest[5:]
     block = parts.shape[2]
     width = XS * block
     piece = width // DP
-    pairs = []
-    for j in range(XS):
-        span = pl.ds(j * block, block)
-        pairs.append((wq.at[span], wq_v.at[span]))
-        pairs.append((wkv.at[span], wkv_v.at[span]))
-    if project:
-        for j in range(XS):
-            span = pl.ds(j * block, block)
-            pairs.append((wo.at[:, span], wo_v.at[:, span]))
-    moves = copies(pairs, sems)
-    for move in moves:
-        move.start()
     tokens = q_out.shape[0]
     outs = []
     for d in range(DP):
@@ -80,10 +67,8 @@
         span = slice(j * block, (j + 1) * block)
         normed = (parts[j, :tokens, :].astype(F32) * scale * gain[:, span].astype(F32)).astype(BF16)
         normed_v[:, span] = normed
-        moves[2 * j].wait()
-        q = q + dot(normed, wq_v[span, :])
-        moves[2 * j + 1].wait()
-        kv = kv + dot(normed, wkv_v[span, :])
+        q = q + dot(normed, wq[span, :])
+        kv = kv + dot(normed, wkv[span, :])
     for move in outs[:DP]:
         move.start()
     q = q.astype(BF16)
@@ -109,8 +94,7 @@
         move.start()
     if project:
         for j in range(XS):
-            moves[2 * XS + j].wait()
-            send[j] = dot(mix, wo_v[:, j * block : (j + 1) * block]).astype(BF16)
+            send[j] = dot(mix, wo[:, j * block : (j + 1) * block]).astype(BF16)
 
     for move in outs:
         move.wait()
@@ -122,22 +106,11 @@
 ):
     if onward:
         send, rest = rest[0], rest[1:]
-    pack, wq_v, wkv_v, wo_v, qg_v, pg_v, gain_v, gain_pair_v, sems, out_sems = rest
+    pack, qg_v, pg_v, gain_v, gain_pair_v, out_sems = rest
     tokens, block = q_in.shape[0], parts.shape[2]
     width = XS * block
     piece = width // DP
     qs, kvs = qg_v.shape[1], pg_v.shape[1]
-    pairs = []
-    for j in range(XS):
-        span = pl.ds(j * block, block)
-        pairs.append((wo.at[:, span], wo_v.at[:, span]))
-    for j in range(XS):
-        span = pl.ds(j * block, block)
-        pairs.append((wq.at[span], wq_v.at[span]))
-        pairs.append((wkv.at[span], wkv_v.at[span]))
-    moves = copies(pairs, sems)
-    for move in moves:
-        move.start()
     outs = []
     for d in range(XS):
         outs.append((qg_v, pack.at[d, pl.ds(0, tokens), pl.ds(0, qs)]))
@@ -147,8 +120,7 @@
     outs = copies(outs, out_sems)
     mix_grad = jnp.zeros(q_in.shape, F32)
     for j in range(XS):
-        moves[j].wait()
-        mix_grad = mix_grad + dot(grads[j, :tokens, :], wo_v[:, j * block : (j + 1) * block], ((1,), (1,)))
+        mix_grad = mix_grad + dot(grads[j, :tokens, :], wo[:, j * block : (j + 1) * block], ((1,), (1,)))
     mix_grad = mix_grad.astype(BF16)
     q = q_in[...]
     kv = kv_in[...]
@@ -180,10 +152,8 @@
         pull = scale * scale / width * correction
     for j in range(XS):
         span = slice(j * block, (j + 1) * block)
-        moves[XS + 2 * j].wait()
-        moves[XS + 2 * j + 1].wait()
-        normed_grad = dot(query_grad, wq_v[span, :], ((1,), (1,))) + dot(
-            pair_grad, wkv_v[span, :], ((1,), (1,))
+        normed_grad = dot(query_grad, wq[span, :], ((1,), (1,))) + dot(
+            pair_grad, wkv[span, :], ((1,), (1,))
         )
         h = parts[j, :tokens, :].astype(F32)
         scaled = normed_grad * scale
@@ -261,22 +231,21 @@
         move.wait()
 
 
-def combine_kernel(first, second, spread):
+def combine_kernel(first, second, wq, wo, spread):
     total = (first[...].astype(F32) + second[...].astype(F32)).astype(BF16)
     for j in range(XS):
         spread[j] = total
 
 
-def call(kernel, ins, outs, scratch, flops, args, aliases={}):
+def call(kernel, ins, outs, scratch, flops, args, traffic=12 * 2**20):
     return pl.pallas_call(
         kernel,
         out_shape=[out for out, _ in outs],
         in_specs=ins,
         out_specs=[spec for _, spec in outs],
         scratch_shapes=scratch,
-        input_output_aliases=aliases,
-        compiler_params=pltpu.CompilerParams(vmem_limit_bytes=40 * 2**20),
-        cost_estimate=pl.CostEstimate(flops=flops, bytes_accessed=12 * 2**20, transcendentals=2**16),
+        compiler_params=pltpu.CompilerParams(vmem_limit_bytes=24 * 2**20),
+        cost_estimate=pl.CostEstimate(flops=flops, bytes_accessed=traffic, transcendentals=2**16),
     )(*args)
 
 
@@ -300,24 +269,24 @@
     return got
 
 
-def combine(first, second):
+def combine(first, second, wq, wo):
     spread = jax.ShapeDtypeStruct((XS,) + first.shape, BF16)
-    return call(combine_kernel, [VMEM] * 2, [(spread, VMEM)], [], 2**20, (first, second))[0]
+    return call(
+        combine_kernel,
+        [VMEM] * 2 + [pl.BlockSpec(memory_space=pl.ANY)] * 2,
+        [(spread, VMEM)],
+        [],
+        2**20,
+        (first, second, wq, wo),
+        2**27,
+    )[0]
 
 
 def nothing(*outs):
-    return pl.pallas_call(
+    got = pl.pallas_call(
         lambda *refs: None, out_shape=[o for o, _ in outs], out_specs=[HBM for _ in outs]
     )()
-
-
-def start_kernel(here, hidden, grads, gains, out):
-    rows, length, _ = hidden.shape
-    for row in range(rows):
-        mine = jnp.where(here[0] == 0, hidden[row], grads[row])
-        out[row * length : (row + 1) * length, :] = mine
-    tall = (out.shape[0] - rows * length, out.shape[1])
-    out[rows * length :, :] = jnp.broadcast_to(gains[...].astype(F32), tall).astype(BF16)
+    return list(got)
 
 
 def pair_kernel(here, mine, other, spread):
@@ -363,16 +332,12 @@
     tall = qs // HEAD_DIM * length
 
     here = jnp.stack([station, lax.axis_index("core"), lax.axis_index("zh")])
-    start = call(
-        start_kernel,
-        [SMEM] + [VMEM] * 3,
-        [(jax.ShapeDtypeStruct((tokens + 16, shard), BF16), VMEM)],
-        [],
-        2**20,
-        (here, hidden_in, grad_out, gains),
-    )[0]
+    start = jnp.where(
+        station == 0, hidden_in.reshape(tokens, shard), grad_out.reshape(tokens, shard)
+    )
+    start = jnp.concatenate([start, jnp.broadcast_to(gains, (16, shard))], 0)
     start_spread = pair_up(start, here)
-    start_full = gather_x(start_spread)
+    start_full, station = lax.optimization_barrier((gather_x(start_spread), station))
     first_block = start_spread
     gain = start_full[:, tokens, :].reshape(1, width)
     first = start_full
@@ -389,8 +354,6 @@
         (shape((tokens, kvs), BF16), VMEM),
         (shape((rows, tall, length), F32), VMEM),
     ]
-    held = [pltpu.VMEM((width, qs), BF16), pltpu.VMEM((width, kvs), BF16)]
-    held_out = [pltpu.VMEM((qs, width), BF16)]
     over_dp = lambda v: lax.all_to_all(v, ("y", "core"), 0, 0)
 
     last_section = SECTIONS - 1
@@ -401,12 +364,9 @@
     def forward(parts, project):
         return call(
             functools.partial(forward_kernel, rows, length, project),
-            [SMEM, VMEM, VMEM, HBM, HBM, HBM],
+            [SMEM] + [VMEM] * 5,
             [sent] * project + [early_pack] + saved,
-            held
-            + [pltpu.VMEM((tokens, width), BF16), pltpu.VMEM((tokens, qs), BF16)]
-            + [dma(3 * XS), dma(2 * DP)]
-            + held_out * project,
+            [pltpu.VMEM((tokens, width), BF16), pltpu.VMEM((tokens, qs), BF16), dma(2 * DP)],
             flops,
             (lengths, parts, gain, wq, wkv, wo),
         )
@@ -414,13 +374,10 @@
     def backward(parts_grad, kept, onward):
         return call(
             functools.partial(backward_kernel, rows, length, onward),
-            [VMEM] * 7 + [HBM] * 3,
+            [VMEM] * 10,
             [sent] * onward + [late_pack],
-            held
-            + held_out
-            + [pltpu.VMEM((tokens, qs), BF16), pltpu.VMEM((tokens, kvs), BF16)]
-            + [pltpu.VMEM((DP, piece), F32), pltpu.VMEM((2 * DP, piece), BF16)]
-            + [dma(3 * XS), dma(3 * XS)],
+            [pltpu.VMEM((tokens, qs), BF16), pltpu.VMEM((tokens, kvs), BF16)]
+            + [pltpu.VMEM((DP, piece), F32), pltpu.VMEM((2 * DP, piece), BF16), dma(3 * XS)],
             flops,
             (parts_grad, kept[0], gain) + tuple(kept[1:]) + (wq, wkv, wo),
         )
@@ -444,7 +401,7 @@
             if arrived is None:
                 parts, block = first, first_block
             else:
-                spread = combine(*arrived)
+                spread = combine(*arrived, wq, wo)
                 parts, block = gather_x(spread), spread
             got = forward(parts, True)
             return pass_on(block, got[0]), got[1], [parts] * (step > 0) + list(got[2:])
@@ -458,12 +415,12 @@
         arrived = hop(block, step, step + 1)
 
     def turn(packed, arrived):
-        spread = combine(*arrived)
+        empty, *arrived = lax.optimization_barrier(nothing(factors_out) + list(arrived))
+        spread = combine(*arrived, wq, wo)
         parts = gather_x(spread)
         got = forward(parts, False)
         back = backward(first, [parts] + list(got[1:]), True)
-        empty = nothing(factors_out)
-        return pass_on(first_block, back[0]), back[1], got[0], empty[0]
+        return pass_on(first_block, back[0]), back[1], got[0], empty
 
     def exchange(packed, arrived):
         empty = nothing(block_out, late_pack, early_pack)
@@ -486,7 +443,7 @@
             late, *arrived = lax.optimization_barrier([late] + list(arrived))
 
         def work(pack, g_kept, arrived, kept_here):
-            spread = combine(*arrived)
+            spread = combine(*arrived, wq, wo)
             g = gather_x(spread)
             got = backward(g, kept_here, onward)
             if onward:

time: 366 us -> 354 us (0.967)
  waiting for transfers between devices: 222 us -> 215 us
  starting transfers between devices: 64.9 us -> 59.1 us
    ppermute x12, waiting for transfers between devices: 172 us -> 165 us  [hop(): got.append(lax.ppermute(block, ('s', 'x', 'zh'), route))]
    ppermute x2, starting transfers between devices: 23.4 us -> 18.5 us  [shards(): swap = lambda v: lax.ppermute(v, 'core', [(0, 1), (1, 0)])]
    pallas_call x8 -> x7, Pallas kernels: 28.5 us -> 28.4 us  [call(): pl.pallas_call(kernel, out_shape=[out for out, _ in outs], in_specs=ins,...]
  transfers between devices with their start and end apart: 19 -> 19, of which waited for: 9 -> 8; matrix products, arithmetic and copies ran while one was open for 0% -> 0% of each run, Pallas kernels for 5% -> 5%
where the time goes in v5:
time: 354 us
  waiting for transfers between devices  215 us (61%)
  starting transfers between devices  59.1 us (17%)
  blocking collectives  41.9 us (12%)
  Pallas kernels  28.4 us (8%)
  local copies, waits for them, and re-layouts  4.56 us (1%)
  other arithmetic  3.8 us (1%)
    ppermute x12, waiting for transfers between devices, hop(): got.append(lax.ppermute(block, ('s', 'x', 'zh'), route))  165 us
    pallas_call x7, Pallas kernels, call(): pl.pallas_call(kernel, out_shape=[out for out, _ in outs], in_specs=ins,...  28.4 us
    all_to_all x2, blocking collectives, gather_x(): return lax.all_to_all(spread, 'x', 0, 0)  28.1 us
    all_to_all x1, waiting for transfers between devices, shards(): over_dp = lambda v: lax.all_to_all(v, ('y', 'core'), 0, 0)  26.4 us
    ppermute x2, starting transfers between devices, shards(): swap = lambda v: lax.ppermute(v, 'core', [(0, 1), (1, 0)])  18.5 us
    all_to_all x1, waiting for transfers between devices, gather_x(): return lax.all_to_all(spread, 'x', 0, 0)  15 us
    all_to_all x1, blocking collectives, shards(): over_y = lambda v: lax.all_to_all(v, 'y', 0, 0)  13.7 us
    ppermute x12, starting transfers between devices, hop(): got.append(lax.ppermute(block, ('s', 'x', 'zh'), route))  10.6 us
  transfers between devices with their start and end apart: 19, of which 8 were waited for; matrix products, arithmetic and copies ran while one was open for 0% of the time, Pallas kernels for 5%

profile of v5, /device:TPU:1, one launch (start us, length us, event | category | flops | bytes accessed | tf_op | source)
XLA Modules:
  0.0 353.5 jit_solution(16890772458506103958)
XLA Ops:
  0.6 0.7 reduce.5
  1.3 0.9 broadcast_select_fusion
  2.3 0.0 copy-start.10
  2.3 0.0 copy-start.31
  2.3 7.8 %collective-permute-start = (bf16[144,512]{1,0:T(8,128)(2,1)S(1)}, bf16[144,512]{1,0:T(8,128)(2,1)S(1)}, u32[]{:S(2)}, u32[]{:S(2)}) collective-permute-start(bf16[144,512]{1,0:T(8,128)(2,1)S(1)} %pad_maximum_fusion.mine), channel_id=1, source_target_pairs={{0,8},{8,0},{16,24},{24,16},{32,40},{40,32},{48,56},{56,48},{64,72... | collective-permute-start | bytes 442376 | tf_op jit(solution)/shard_map/ppermute | solution.py:316
  10.2 0.1 pad_add_fusion.here
  10.2 3.0 collective-permute-done.other
  13.2 1.7 shard_map.102
  14.9 4.6 %all-to-all-start.16 = ((bf16[4,144,1024]{2,1,0:T(8,128)(2,1)}), bf16[4,144,1024]{2,1,0:T(8,128)(2,1)}, u32[]{:S(2)}, u32[]{:S(2)}) async-start(bf16[4,144,1024]{2,1,0:T(8,128)(2,1)} %shard_map.102), calls=%async_computation.16 | async-start | bytes 2359296 | tf_op jit(solution)/shard_map/all_to_all | solution.py:257
  19.5 15.0 %all-to-all-done.16 = bf16[4,144,1024]{2,1,0:T(8,128)(2,1)} async-done(((bf16[4,144,1024]{2,1,0:T(8,128)(2,1)}), bf16[4,144,1024]{2,1,0:T(8,128)(2,1)}, u32[]{:S(2)}, u32[]{:S(2)}) %all-to-all-start.16) | async-done | bytes 1179680 | tf_op jit(solution)/shard_map/all_to_all | solution.py:257
  34.5 0.9 slice.13
  35.4 23.5 %conditional.8 = (bf16[128,1024]{1,0:T(8,128)(2,1)S(1)}, f32[128,1]{1,0:T(8,128)}, bf16[128,512]{1,0:T(8,128)(2,1)}, bf16[128,256]{1,0:T(8,128)(2,1)}, f32[2,256...) conditional(s32[]{:T(128)} %convert_element_type.25, () %tuple.78, (s32[2]{0:T(128)S(1)}, ...), branch_computations={%region_0.1_spmd, %region_1.2_spmd} | conditional | flops 1343225856 | bytes 31981644 | solution.py:413
  35.4 8.1 %branch_1_fun.21 = (bf16[4,128,1024]{2,1,0:T(8,128)(2,1)S(1)}, bf16[8,128,1024]{2,1,0:T(8,128)(2,1)}, f32[128,1]{1,0:T(8,128)}, bf16[128,512]{1,0:T(8,128)(2,1)}...) custom-call(s32[2]{0:T(128)S(1)} %get-tuple-element.159.lens, bf16[4,144,1024]{2,1,0:T(8,128)(2,1)} %get-tuple-element.160.parts, ...), custom_call_target="tpu_custom_call" | custom-call | flops 1342177280 | bytes 12582912 | tf_op jit(solution)/shard_map/cond/branch_1_fun/pallas_call | solution.py:241
  43.5 15.1 %all_to_all.79.sums = bf16[4,128,1024]{2,1,0:T(8,128)(2,1)S(1)} all-to-all(bf16[4,128,1024]{2,1,0:T(8,128)(2,1)S(1)} %get-tuple-element.165), channel_id=1, replica_groups=mesh['s'=4,'x'=4,'zh'=2,'y'=4,'core'=2] {'x'}, dimensions={0} | all-to-all | bytes 2097152 | tf_op jit(solution)/shard_map/cond/branch_1_fun/all_to_all | solution.py:257
  58.6 0.2 branch_1_fun.22
  58.8 1.3 collective-permute-start.2
  60.1 1.3 collective-permute-start.1
  61.5 2.0 collective-permute-done.2
  63.4 1.3 collective-permute-done.1
  64.7 0.7 collective-permute-start.4
  65.4 0.7 collective-permute-start.3
  66.1 0.0 collective-permute-done.4
  66.1 0.0 collective-permute-done.3
  66.2 0.7 collective-permute-start.6
  66.8 0.7 collective-permute-start.5
  67.6 35.4 %conditional.11 = (bf16[128,1024]{1,0:T(8,128)(2,1)S(1)}, bf16[4,144,768]{2,1,0:T(8,128)(2,1)}, bf16[8,128,1024]{2,1,0:T(8,128)(2,1)}, bf16[8,128,1024]{2,1,0:T(8,128)(2,1)}) conditional(s32[]{:T(128)} %convert_element_type.22, bf16[8,128,1024]{2,1,0:T(8,128)(2,1)} %get-tuple-element.325, (bf16[128,1024]{1,0:T(8,128)(2,1)S(1)}, ...), branch_computations={%region_6.7_spmd, %region_7.8_spmd} | conditional | flops 2686451712 | bytes 214433920 | solution.py:429
  67.6 8.9 %all-to-all-start.5 = ((bf16[8,128,1024]{2,1,0:T(8,128)(2,1)}), bf16[8,128,1024]{2,1,0:T(8,128)(2,1)}, u32[]{:S(2)}, u32[]{:S(2)}) async-start(bf16[8,128,1024]{2,1,0:T(8,128)(2,1)} %param.6), calls=%async_computation.5 | async-start | bytes 4194304 | tf_op jit(solution)/shard_map/cond/branch_0_fun/all_to_all | solution.py:357
  76.5 26.4 %all-to-all-done.5 = bf16[8,128,1024]{2,1,0:T(8,128)(2,1)} async-done(((bf16[8,128,1024]{2,1,0:T(8,128)(2,1)}), bf16[8,128,1024]{2,1,0:T(8,128)(2,1)}, u32[]{:S(2)}, u32[]{:S(2)}) %all-to-all-start.5) | async-done | bytes 2097184 | tf_op jit(solution)/shard_map/cond/branch_0_fun/all_to_all | solution.py:357
  103.0 0.7 collective-permute-start.8
  103.6 0.7 collective-permute-start.7
  104.3 0.0 collective-permute-done.8
  104.3 0.0 collective-permute-done.7
  104.3 2.3 conditional.13
  104.4 2.3 slice.9
  106.6 0.7 copy-done.21
  107.3 0.7 collective-permute-start.10
  108.0 0.7 collective-permute-start.9
  108.7 0.0 collective-permute-done.10
  108.7 0.0 collective-permute-done.9
  108.7 0.0 copy-start.22
  108.7 0.7 copy-done.22
  109.4 1.3 collective-permute-start.12
  110.7 1.3 collective-permute-start.11
  112.0 0.0 copy-start.15
  112.1 162.1 %collective-permute-done.12 = bf16[128,1024]{1,0:T(8,128)(2,1)S(1)} collective-permute-done((bf16[128,1024]{1,0:T(8,128)(2,1)}, bf16[128,1024]{1,0:T(8,128)(2,1)S(1)}, u32[]{:S(2)}, u32[]{:S(2)}) %collective-permute-start.12) | collective-permute-done | bytes 262176 | tf_op jit(solution)/shard_map/ppermute | solution.py:268
  274.2 0.0 collective-permute-done.11
  274.2 28.2 %conditional.15 = (bf16[4,144,768]{2,1,0:T(8,128)(2,1)}, bf16[4,128,1024]{2,1,0:T(8,128)(2,1)}) conditional(s32[]{:T(128)} %convert_element_type.25, (bf16[4,128,1024]{2,1,0:T(8,128)(2,1)S(1)}, bf16[4,144,768]{2,1,0:T(8,128)(2,1)}) %tuple.132, (bf16[128,1024]{1,0:T(8,128)(2,1)}, bf16[128,1024]{1,0:T(8,128)(2,1)S(1)}, bf16[4096,512]{1,0:T(8,128)(2,1)}, ...), branch_computations={%region_14.15_spmd, %region_15.16_spmd} | conditional | flops 1343225856 | bytes 153354384 | solution.py:456
  274.2 1.0 branch_1_fun.40
  275.3 0.0 copy-start.20
  275.3 13.0 %all_to_all.92.grads = bf16[4,128,1024]{2,1,0:T(8,128)(2,1)} all-to-all(bf16[4,128,1024]{2,1,0:T(8,128)(2,1)S(1)} %branch_1_fun.40), channel_id=1, replica_groups=mesh['s'=4,'x'=4,'zh'=2,'y'=4,'core'=2] {'x'}, dimensions={0} | all-to-all | bytes 2097152 | tf_op jit(solution)/shard_map/cond/branch_1_fun/all_to_all | solution.py:257
  288.3 4.2 %all-to-all-start.15 = ((bf16[4,128,1024]{2,1,0:T(8,128)(2,1)}), bf16[4,128,1024]{2,1,0:T(8,128)(2,1)}, u32[]{:S(2)}, u32[]{:S(2)}) async-start(bf16[4,128,1024]{2,1,0:T(8,128)(2,1)} %all_to_all.92.grads), calls=%async_computation.15 | async-start | bytes 2097152 | tf_op jit(solution)/shard_map/cond/branch_1_fun/all_to_all | solution.py:434
  292.6 9.1 %branch_1_fun.41 = bf16[4,144,768]{2,1,0:T(8,128)(2,1)} custom-call(bf16[4,128,1024]{2,1,0:T(8,128)(2,1)} %all_to_all.92.grads, bf16[4,144,1024]{2,1,0:T(8,128)(2,1)} %get-tuple-element.268.parts, bf16[1,4096]{1,0:T(2,128)(2,1)S(1)} %get-tuple-element.269.gain, f32[128,1]{1,0:T(8,128)S(1)} %get-tuple-element.270.scale_in, bf16[128,512]{1,0:T(8,128)(2,1)S(1)} %copy-done.25, ...), custom_call_target="tpu_custom_call" | custom-call | flops 1342177280 | bytes 12582912 | tf_op jit(solution)/shard_map/cond/branch_1_fun/pallas_call | solution.py:241
  301.7 0.7 all-to-all-done.15
  302.4 13.7 %all_to_all.93.grads = bf16[4,144,768]{2,1,0:T(8,128)(2,1)S(1)} all-to-all(bf16[4,144,768]{2,1,0:T(8,128)(2,1)} %get-tuple-element.355), channel_id=1, replica_groups=mesh['s'=4,'x'=4,'zh'=2,'y'=4,'core'=2] {'y'}, dimensions={0} | all-to-all | bytes 1769472 | tf_op jit(solution)/shard_map/all_to_all | solution.py:434
  316.1 18.5 %collective-permute-start.14 = (bf16[4,144,768]{2,1,0:T(8,128)(2,1)S(1)}, bf16[4,144,768]{2,1,0:T(8,128)(2,1)}, u32[]{:S(2)}, u32[]{:S(2)}) collective-permute-start(bf16[4,144,768]{2,1,0:T(8,128)(2,1)S(1)} %all_to_all.93.grads), channel_id=1, source_target_pairs={{0,1},{1,0},{2,3},{3,2},{4,5},{5,4},{6,7},{7,6},{8,9},{9,8},{10,11... | collective-permute-start | bytes 2654216 | tf_op jit(solution)/shard_map/ppermute | solution.py:435
  334.6 0.0 collective-permute-start.13
  334.7 3.4 shard_map.103.rest_0_
  338.1 0.0 collective-permute-done.14.grads
  338.1 0.9 convert_reduce_fusion
  338.9 0.7 dynamic-slice_add_fusion
  339.6 4.4 %all-to-all-start.18 = ((f32[8,1,64]{2,1,0:T(1,128)}), f32[8,1,64]{2,1,0:T(1,128)S(1)}, u32[]{:S(2)}, u32[]{:S(2)}) async-start(f32[8,1,64]{2,1,0:T(1,128)} %bitcast.13), calls=%async_computation.18 | async-start | bytes 8192 | tf_op jit(solution)/shard_map/all_to_all | solution.py:471
  344.1 4.9 %shard_map.104 = (f32[512,512]{1,0:T(8,128)}, f32[1024,128]{1,0:T(8,128)}, f32[512,512]{1,0:T(8,128)}) custom-call(s32[3]{0:T(128)S(1)} %pad_add_fusion.here, bf16[8,128,1024]{2,1,0:T(8,128)(2,1)} %get-tuple-element.327.early, bf16[8,128,1024]{2,1,0:T(8,128)(2,1)} %get-tuple-element.435.late, bf16[4,128,1024]{2,1,0:T(8,128)(2,1)} %collective-permute-done.13.g, ...), custom_call_target="tpu_custom_call" | custom-call | flops 1342177280 | bytes 12582912 | tf_op jit(solution)/shard_map/pallas_call | solution.py:241
  349.0 4.0 %all-to-all-done.18 = f32[8,1,64]{2,1,0:T(1,128)S(1)} async-done(((f32[8,1,64]{2,1,0:T(1,128)}), f32[8,1,64]{2,1,0:T(1,128)S(1)}, u32[]{:S(2)}, u32[]{:S(2)}) %all-to-all-start.18) | async-done | bytes 2080 | tf_op jit(solution)/shard_map/all_to_all | solution.py:471
  353.0 0.5 reduce_sum.49
  (31 shorter events, 0.2 us)
Async XLA Ops:
  2.3 33.1 %copy-start.10 = (bf16[1,4096,1,256]{3,1,2,0:T(8,128)(2,1)S(1)}, bf16[1,4096,1,256]{3,1,2,0:T(8,128)(2,1)}, u32[]{:S(2)}) copy-start(bf16[1,4096,1,256]{3,1,2,0:T(8,128)(2,1)} %param.27) | copy-start | bytes 6291460
  2.3 33.1 %copy-start.31 = (s32[2]{0:T(128)S(1)}, s32[2]{0:T(128)}, u32[]{:S(2)}) copy-start(s32[2]{0:T(128)} %param.24) | copy-start | bytes 28
  2.3 10.9 %collective-permute-start = (bf16[144,512]{1,0:T(8,128)(2,1)S(1)}, bf16[144,512]{1,0:T(8,128)(2,1)S(1)}, u32[]{:S(2)}, u32[]{:S(2)}) collective-permute-start(bf16[144,512]{1,0:T(8,128)(2,1)S(1)} %pad_maximum_fusion.mine), channel_id=1, source_target_pairs={{0,8},{8,0},{16,24},{24,16},{32,40},{40,32},{48,56},{56,48},{64,72... | collective-permute-start | bytes 442376 | tf_op jit(solution)/shard_map/ppermute | solution.py:316
  14.9 19.6 %all-to-all-start.16 = ((bf16[4,144,1024]{2,1,0:T(8,128)(2,1)}), bf16[4,144,1024]{2,1,0:T(8,128)(2,1)}, u32[]{:S(2)}, u32[]{:S(2)}) async-start(bf16[4,144,1024]{2,1,0:T(8,128)(2,1)} %shard_map.102), calls=%async_computation.16 | async-start | bytes 2359296 | tf_op jit(solution)/shard_map/all_to_all | solution.py:257
  43.5 15.2 %copy-start.11 = (bf16[4,144,1024]{2,1,0:T(8,128)(2,1)S(1)}, bf16[4,144,1024]{2,1,0:T(8,128)(2,1)}, u32[]{:S(2)}) copy-start(bf16[4,144,1024]{2,1,0:T(8,128)(2,1)} %get-tuple-element.166.block) | copy-start | bytes 3538948 | tf_op jit(solution)/shard_map/cond
  58.8 4.6 %collective-permute-start.2 = (bf16[128,1024]{1,0:T(8,128)(2,1)S(1)}, bf16[128,1024]{1,0:T(8,128)(2,1)S(1)}, u32[]{:S(2)}, u32[]{:S(2)}) collective-permute-start(bf16[128,1024]{1,0:T(8,128)(2,1)S(1)} %get-tuple-element.322), channel_id=1, source_target_pairs={{0,72},{8,64},{16,88},{24,80},{32,104},{40,96},{48,120},{56,112},{... | collective-permute-start | bytes 786440 | tf_op jit(solution)/shard_map/ppermute | solution.py:268
  60.1 4.6 %collective-permute-start.1 = (bf16[128,1024]{1,0:T(8,128)(2,1)S(1)}, bf16[128,1024]{1,0:T(8,128)(2,1)S(1)}, u32[]{:S(2)}, u32[]{:S(2)}) collective-permute-start(bf16[128,1024]{1,0:T(8,128)(2,1)S(1)} %get-tuple-element.322), channel_id=1, source_target_pairs={{0,64},{8,72},{16,80},{24,88},{32,96},{40,104},{48,112},{56,120},{... | collective-permute-start | bytes 786440 | tf_op jit(solution)/shard_map/ppermute | solution.py:268
  64.7 1.4 collective-permute-start.4
  65.4 0.7 collective-permute-start.3
  66.2 1.4 collective-permute-start.6
  66.8 0.7 collective-permute-start.5
  67.6 35.4 %all-to-all-start.5 = ((bf16[8,128,1024]{2,1,0:T(8,128)(2,1)}), bf16[8,128,1024]{2,1,0:T(8,128)(2,1)}, u32[]{:S(2)}, u32[]{:S(2)}) async-start(bf16[8,128,1024]{2,1,0:T(8,128)(2,1)} %param.6), calls=%async_computation.5 | async-start | bytes 4194304 | tf_op jit(solution)/shard_map/cond/branch_0_fun/all_to_all | solution.py:357
  103.0 1.4 collective-permute-start.8
  103.6 0.7 collective-permute-start.7
  106.6 0.7 copy-start.21
  107.3 1.4 collective-permute-start.10
  108.0 0.7 collective-permute-start.9
  108.7 0.7 copy-start.22
  109.4 164.7 %collective-permute-start.12 = (bf16[128,1024]{1,0:T(8,128)(2,1)}, bf16[128,1024]{1,0:T(8,128)(2,1)S(1)}, u32[]{:S(2)}, u32[]{:S(2)}) collective-permute-start(bf16[128,1024]{1,0:T(8,128)(2,1)} %copy-done.22), channel_id=1, source_target_pairs={{64,8},{72,0},{80,24},{88,16},{96,40},{104,32},{112,56},{120,48},{... | collective-permute-start | bytes 786440 | tf_op jit(solution)/shard_map/ppermute | solution.py:268
  110.7 163.5 %collective-permute-start.11 = (bf16[128,1024]{1,0:T(8,128)(2,1)}, bf16[128,1024]{1,0:T(8,128)(2,1)}, u32[]{:S(2)}, u32[]{:S(2)}) collective-permute-start(bf16[128,1024]{1,0:T(8,128)(2,1)} %copy-done.22), channel_id=1, source_target_pairs={{64,0},{72,8},{80,16},{88,24},{96,32},{104,40},{112,48},{120,56},{... | collective-permute-start | bytes 786440 | tf_op jit(solution)/shard_map/ppermute | solution.py:268
  112.0 162.2 %copy-start.15 = (bf16[4,128,1024]{2,1,0:T(8,128)(2,1)S(1)}, bf16[4,128,1024]{2,1,0:T(8,128)(2,1)}, u32[]{:S(2)}) copy-start(bf16[4,128,1024]{2,1,0:T(8,128)(2,1)} %get-tuple-element.346) | copy-start | bytes 3145732
  112.0 162.2 %copy-start.29 = (f32[128,1]{1,0:T(8,128)S(1)}, f32[128,1]{1,0:T(8,128)}, u32[]{:S(2)}) copy-start(f32[128,1]{1,0:T(8,128)} %get-tuple-element.350) | copy-start | bytes 1540
  275.3 17.3 %copy-start.20 = (f32[2,256,64]{2,1,0:T(8,128)S(1)}, f32[2,256,64]{2,1,0:T(8,128)}, u32[]{:S(2)}) copy-start(f32[2,256,64]{2,1,0:T(8,128)} %get-tuple-element.273.attn_in) | copy-start | bytes 393220 | tf_op jit(solution)/shard_map/cond
  275.3 17.3 %copy-start.25 = (bf16[128,512]{1,0:T(8,128)(2,1)S(1)}, bf16[128,512]{1,0:T(8,128)(2,1)}, u32[]{:S(2)}) copy-start(bf16[128,512]{1,0:T(8,128)(2,1)} %get-tuple-element.271.q_in) | copy-start | bytes 393220 | tf_op jit(solution)/shard_map/cond
  275.3 17.3 %copy-start.30 = (bf16[128,256]{1,0:T(8,128)(2,1)S(1)}, bf16[128,256]{1,0:T(8,128)(2,1)}, u32[]{:S(2)}) copy-start(bf16[128,256]{1,0:T(8,128)(2,1)} %get-tuple-element.272.kv_in) | copy-start | bytes 196612 | tf_op jit(solution)/shard_map/cond
  288.3 14.1 %all-to-all-start.15 = ((bf16[4,128,1024]{2,1,0:T(8,128)(2,1)}), bf16[4,128,1024]{2,1,0:T(8,128)(2,1)}, u32[]{:S(2)}, u32[]{:S(2)}) async-start(bf16[4,128,1024]{2,1,0:T(8,128)(2,1)} %all_to_all.92.grads), calls=%async_computation.15 | async-start | bytes 2097152 | tf_op jit(solution)/shard_map/cond/branch_1_fun/all_to_all | solution.py:434
  316.1 22.0 %collective-permute-start.14 = (bf16[4,144,768]{2,1,0:T(8,128)(2,1)S(1)}, bf16[4,144,768]{2,1,0:T(8,128)(2,1)}, u32[]{:S(2)}, u32[]{:S(2)}) collective-permute-start(bf16[4,144,768]{2,1,0:T(8,128)(2,1)S(1)} %all_to_all.93.grads), channel_id=1, source_target_pairs={{0,1},{1,0},{2,3},{3,2},{4,5},{5,4},{6,7},{7,6},{8,9},{9,8},{10,11... | collective-permute-start | bytes 2654216 | tf_op jit(solution)/shard_map/ppermute | solution.py:435
  334.6 9.4 %collective-permute-start.13 = (bf16[4,128,1024]{2,1,0:T(8,128)(2,1)}, bf16[4,128,1024]{2,1,0:T(8,128)(2,1)}, u32[]{:S(2)}, u32[]{:S(2)}) collective-permute-start(bf16[4,128,1024]{2,1,0:T(8,128)(2,1)} %get-tuple-element.354.g), channel_id=1, source_target_pairs={{0,1},{1,0},{2,3},{3,2},{4,5},{5,4},{6,7},{7,6},{8,9},{9,8},{10,11... | collective-permute-start | bytes 3145736 | tf_op jit(solution)/shard_map/ppermute | solution.py:435
  339.6 13.4 %all-to-all-start.18 = ((f32[8,1,64]{2,1,0:T(1,128)}), f32[8,1,64]{2,1,0:T(1,128)S(1)}, u32[]{:S(2)}, u32[]{:S(2)}) async-start(f32[8,1,64]{2,1,0:T(1,128)} %bitcast.13), calls=%async_computation.18 | async-start | bytes 8192 | tf_op jit(solution)/shard_map/all_to_all | solution.py:471

commit v6 on v5

--- a/solution.py
+++ b/solution.py
@@ -40,7 +40,7 @@
     )
 
 
-def forward_kernel(rows, length, project, lens, parts, gain, wq, wkv, wo, *rest):
+def forward_kernel(rows, length, project, arrive, lens, parts, gain, wq, wkv, wo, *rest):
     if project:
         send, rest = rest[0], rest[1:]
     pack, scale_out, q_out, kv_out, attn_out = rest[:5]
@@ -67,6 +67,7 @@
         span = slice(j * block, (j + 1) * block)
         normed = (parts[j, :tokens, :].astype(F32) * scale * gain[:, span].astype(F32)).astype(BF16)
         normed_v[:, span] = normed
+        arrive(j)
         q = q + dot(normed, wq[span, :])
         kv = kv + dot(normed, wkv[span, :])
     for move in outs[:DP]:
@@ -94,6 +95,7 @@
         move.start()
     if project:
         for j in range(XS):
+            arrive(XS + j)
             send[j] = dot(mix, wo[:, j * block : (j + 1) * block]).astype(BF16)
 
     for move in outs:
@@ -101,7 +103,7 @@
 
 
 def backward_kernel(
-    rows, length, onward, grads, parts, gain, scale_in, q_in, kv_in, attn_in,
+    rows, length, onward, arrive, grads, parts, gain, scale_in, q_in, kv_in, attn_in,
     wq, wkv, wo, *rest
 ):
     if onward:
@@ -120,6 +122,7 @@
     outs = copies(outs, out_sems)
     mix_grad = jnp.zeros(q_in.shape, F32)
     for j in range(XS):
+        arrive(XS + j)
         mix_grad = mix_grad + dot(grads[j, :tokens, :], wo[:, j * block : (j + 1) * block], ((1,), (1,)))
     mix_grad = mix_grad.astype(BF16)
     q = q_in[...]
@@ -152,6 +155,7 @@
         pull = scale * scale / width * correction
     for j in range(XS):
         span = slice(j * block, (j + 1) * block)
+        arrive(j)
         normed_grad = dot(query_grad, wq[span, :], ((1,), (1,))) + dot(
             pair_grad, wkv[span, :], ((1,), (1,))
         )
@@ -171,6 +175,21 @@
         move.start()
     for move in outs:
         move.wait()
+
+
+def streamed(kernel, rows, length, flag, out_first, *refs):
+    *refs, wq_v, wo_v, sems = refs
+    at = 3 if flag and not out_first else 7
+    wq, wo = refs[at], refs[at + 2]
+    block = wq.shape[0] // XS
+    spans = [pl.ds(j * block, block) for j in range(XS)]
+    pairs = [(wq.at[span], wq_v.at[span]) for span in spans]
+    pairs += [(wo.at[:, span], wo_v.at[:, span]) for span in spans]
+    moves = copies(pairs, sems)
+    for move in moves[XS:] + moves[:XS] if out_first else moves:
+        move.start()
+    refs[at], refs[at + 2] = wq_v, wo_v
+    kernel(rows, length, flag, lambda i: moves[i].wait(), *refs)
 
 
 def weights_kernel(last, own, here, early, late, g, grads, *rest):
@@ -361,23 +380,36 @@
     factors_out = (shape((DP, tokens, piece + qs), BF16), HBM)
     parts_out = (shape((XS, tokens, block_width), BF16), HBM)
 
-    def forward(parts, project):
+    ready = lambda i: None
+    stream = [pltpu.VMEM((width, qs), BF16), pltpu.VMEM((qs, width), BF16), dma(2 * XS)]
+
+    def forward(parts, project, own_copies=False):
+        kernel = functools.partial(forward_kernel, rows, length, project, ready)
+        if own_copies:
+            kernel = functools.partial(streamed, forward_kernel, rows, length, project, False)
+        weight = HBM if own_copies else VMEM
         return call(
-            functools.partial(forward_kernel, rows, length, project),
-            [SMEM] + [VMEM] * 5,
+            kernel,
+            [SMEM, VMEM, VMEM, weight, VMEM, weight],
             [sent] * project + [early_pack] + saved,
-            [pltpu.VMEM((tokens, width), BF16), pltpu.VMEM((tokens, qs), BF16), dma(2 * DP)],
+            [pltpu.VMEM((tokens, width), BF16), pltpu.VMEM((tokens, qs), BF16), dma(2 * DP)]
+            + stream * own_copies,
             flops,
             (lengths, parts, gain, wq, wkv, wo),
         )
 
     def backward(parts_grad, kept, onward):
+        kernel = functools.partial(backward_kernel, rows, length, onward, ready)
+        if not onward:
+            kernel = functools.partial(streamed, backward_kernel, rows, length, onward, True)
+        weight = VMEM if onward else HBM
         return call(
-            functools.partial(backward_kernel, rows, length, onward),
-            [VMEM] * 10,
+            kernel,
+            [VMEM] * 7 + [weight, VMEM, weight],
             [sent] * onward + [late_pack],
             [pltpu.VMEM((tokens, qs), BF16), pltpu.VMEM((tokens, kvs), BF16)]
-            + [pltpu.VMEM((DP, piece), F32), pltpu.VMEM((2 * DP, piece), BF16), dma(3 * XS)],
+            + [pltpu.VMEM((DP, piece), F32), pltpu.VMEM((2 * DP, piece), BF16), dma(3 * XS)]
+            + stream * (not onward),
             flops,
             (parts_grad, kept[0], gain) + tuple(kept[1:]) + (wq, wkv, wo),
         )
@@ -403,7 +435,7 @@
             else:
                 spread = combine(*arrived, wq, wo)
                 parts, block = gather_x(spread), spread
-            got = forward(parts, True)
+            got = forward(parts, True, arrived is None)
             return pass_on(block, got[0]), got[1], [parts] * (step > 0) + list(got[2:])
 
         def rest(packed, arrived):

time: 354 us -> 354 us (level)
  no operation moved by 1% of the time
where the time goes in v6:
time: 354 us; the launch traced here: 353 us
  waiting for transfers between devices  215 us (61%)
  starting transfers between devices  59.2 us (17%)
  blocking collectives  41.8 us (12%)
  Pallas kernels  27.6 us (8%)
  local copies, waits for them, and re-layouts  4.56 us (1%)
  other arithmetic  3.8 us (1%)
    ppermute x12, waiting for transfers between devices, hop(): got.append(lax.ppermute(block, ('s', 'x', 'zh'), route))  165 us
    all_to_all x2, blocking collectives, gather_x(): return lax.all_to_all(spread, 'x', 0, 0)  28.1 us
    pallas_call x7, Pallas kernels, call(): pl.pallas_call(kernel, out_shape=[out for out, _ in outs], in_specs=ins,...  27.6 us
    all_to_all x1, waiting for transfers between devices, shards(): over_dp = lambda v: lax.all_to_all(v, ('y', 'core'), 0, 0)  26.4 us
    ppermute x2, starting transfers between devices, shards(): swap = lambda v: lax.ppermute(v, 'core', [(0, 1), (1, 0)])  18.6 us
    all_to_all x1, waiting for transfers between devices, gather_x(): return lax.all_to_all(spread, 'x', 0, 0)  15 us
    all_to_all x1, blocking collectives, shards(): over_y = lambda v: lax.all_to_all(v, 'y', 0, 0)  13.6 us
    ppermute x12, starting transfers between devices, hop(): got.append(lax.ppermute(block, ('s', 'x', 'zh'), route))  10.6 us
  transfers between devices with their start and end apart: 19, of which 8 were waited for; matrix products, arithmetic and copies ran while one was open for 0% of the time, Pallas kernels for 5%

profile of v6, /device:TPU:1, one launch (start us, length us, event | category | flops | bytes accessed | tf_op | source)
XLA Modules:
  0.0 352.9 jit_solution(16949340593057112634)
XLA Ops:
  0.6 0.7 reduce.5
  1.3 0.9 broadcast_select_fusion
  2.3 0.0 copy-start.10
  2.3 0.0 copy-start.31
  2.3 7.8 %collective-permute-start = (bf16[144,512]{1,0:T(8,128)(2,1)S(1)}, bf16[144,512]{1,0:T(8,128)(2,1)S(1)}, u32[]{:S(2)}, u32[]{:S(2)}) collective-permute-start(bf16[144,512]{1,0:T(8,128)(2,1)S(1)} %pad_maximum_fusion.mine), channel_id=1, source_target_pairs={{0,8},{8,0},{16,24},{24,16},{32,40},{40,32},{48,56},{56,48},{64,72... | collective-permute-start | bytes 442376 | tf_op jit(solution)/shard_map/ppermute | solution.py:335
  10.2 0.1 pad_add_fusion.here
  10.2 3.0 collective-permute-done.other
  13.2 1.7 shard_map.102
  14.9 4.6 %all-to-all-start.16 = ((bf16[4,144,1024]{2,1,0:T(8,128)(2,1)}), bf16[4,144,1024]{2,1,0:T(8,128)(2,1)}, u32[]{:S(2)}, u32[]{:S(2)}) async-start(bf16[4,144,1024]{2,1,0:T(8,128)(2,1)} %shard_map.102), calls=%async_computation.16 | async-start | bytes 2359296 | tf_op jit(solution)/shard_map/all_to_all | solution.py:276
  19.5 15.0 %all-to-all-done.16 = bf16[4,144,1024]{2,1,0:T(8,128)(2,1)} async-done(((bf16[4,144,1024]{2,1,0:T(8,128)(2,1)}), bf16[4,144,1024]{2,1,0:T(8,128)(2,1)}, u32[]{:S(2)}, u32[]{:S(2)}) %all-to-all-start.16) | async-done | bytes 1179680 | tf_op jit(solution)/shard_map/all_to_all | solution.py:276
  34.5 0.9 slice.13
  35.4 22.9 %conditional.8 = (bf16[128,1024]{1,0:T(8,128)(2,1)S(1)}, f32[128,1]{1,0:T(8,128)}, bf16[128,512]{1,0:T(8,128)(2,1)}, bf16[128,256]{1,0:T(8,128)(2,1)}, f32[2,256...) conditional(s32[]{:T(128)} %convert_element_type.25, () %tuple.78, (s32[2]{0:T(128)S(1)}, ...), branch_computations={%region_0.1_spmd, %region_1.2_spmd} | conditional | flops 1343225856 | bytes 31981644 | solution.py:445
  35.4 7.5 %branch_1_fun.21 = (bf16[4,128,1024]{2,1,0:T(8,128)(2,1)S(1)}, bf16[8,128,1024]{2,1,0:T(8,128)(2,1)}, f32[128,1]{1,0:T(8,128)}, bf16[128,512]{1,0:T(8,128)(2,1)}...) custom-call(s32[2]{0:T(128)S(1)} %get-tuple-element.159.refs_0_, bf16[4,144,1024]{2,1,0:T(8,128)(2,1)} %get-tuple-element.160.refs_1_, ...), custom_call_target="tpu_custom_call" | custom-call | flops 1342177280 | bytes 12582912 | tf_op jit(solution)/shard_map/cond/branch_1_fun/pallas_call | solution.py:260
  42.9 15.1 %all_to_all.79.sums = bf16[4,128,1024]{2,1,0:T(8,128)(2,1)S(1)} all-to-all(bf16[4,128,1024]{2,1,0:T(8,128)(2,1)S(1)} %get-tuple-element.165), channel_id=1, replica_groups=mesh['s'=4,'x'=4,'zh'=2,'y'=4,'core'=2] {'x'}, dimensions={0} | all-to-all | bytes 2097152 | tf_op jit(solution)/shard_map/cond/branch_1_fun/all_to_all | solution.py:276
  58.1 0.2 branch_1_fun.22
  58.2 1.3 collective-permute-start.2
  59.6 1.3 collective-permute-start.1
  60.9 2.0 collective-permute-done.2
  62.8 1.3 collective-permute-done.1
  64.2 0.7 collective-permute-start.4
  64.8 0.7 collective-permute-start.3
  65.5 0.0 collective-permute-done.4
  65.5 0.0 collective-permute-done.3
  65.6 0.7 collective-permute-start.6
  66.3 0.7 collective-permute-start.5
  67.0 0.0 collective-permute-done.6
  67.0 0.0 collective-permute-done.5
  67.0 35.4 %conditional.11 = (bf16[128,1024]{1,0:T(8,128)(2,1)S(1)}, bf16[4,144,768]{2,1,0:T(8,128)(2,1)}, bf16[8,128,1024]{2,1,0:T(8,128)(2,1)}, bf16[8,128,1024]{2,1,0:T(8,128)(2,1)}) conditional(s32[]{:T(128)} %convert_element_type.22, bf16[8,128,1024]{2,1,0:T(8,128)(2,1)} %get-tuple-element.325, (bf16[128,1024]{1,0:T(8,128)(2,1)S(1)}, ...), branch_computations={%region_6.7_spmd, %region_7.8_spmd} | conditional | flops 2686451712 | bytes 214433920 | solution.py:461
  67.0 8.9 %all-to-all-start.5 = ((bf16[8,128,1024]{2,1,0:T(8,128)(2,1)}), bf16[8,128,1024]{2,1,0:T(8,128)(2,1)}, u32[]{:S(2)}, u32[]{:S(2)}) async-start(bf16[8,128,1024]{2,1,0:T(8,128)(2,1)} %param.6), calls=%async_computation.5 | async-start | bytes 4194304 | tf_op jit(solution)/shard_map/cond/branch_0_fun/all_to_all | solution.py:376
  75.9 26.4 %all-to-all-done.5 = bf16[8,128,1024]{2,1,0:T(8,128)(2,1)} async-done(((bf16[8,128,1024]{2,1,0:T(8,128)(2,1)}), bf16[8,128,1024]{2,1,0:T(8,128)(2,1)}, u32[]{:S(2)}, u32[]{:S(2)}) %all-to-all-start.5) | async-done | bytes 2097184 | tf_op jit(solution)/shard_map/cond/branch_0_fun/all_to_all | solution.py:376
  102.4 0.7 collective-permute-start.8
  103.0 0.7 collective-permute-start.7
  103.7 0.0 collective-permute-done.8
  103.7 0.0 collective-permute-done.7
  103.7 2.3 conditional.13
  103.8 2.3 slice.9
  106.0 0.7 copy-done.21
  106.7 0.7 collective-permute-start.10
  107.4 0.7 collective-permute-start.9
  108.1 0.0 collective-permute-done.10
  108.1 0.0 copy-start.22
  108.2 0.7 copy-done.22
  108.8 1.3 collective-permute-start.12
  110.1 1.3 collective-permute-start.11
  111.4 0.0 copy-start.15
  111.5 162.1 %collective-permute-done.12 = bf16[128,1024]{1,0:T(8,128)(2,1)S(1)} collective-permute-done((bf16[128,1024]{1,0:T(8,128)(2,1)}, bf16[128,1024]{1,0:T(8,128)(2,1)S(1)}, u32[]{:S(2)}, u32[]{:S(2)}) %collective-permute-start.12) | collective-permute-done | bytes 262176 | tf_op jit(solution)/shard_map/ppermute | solution.py:287
  273.6 28.2 %conditional.15 = (bf16[4,144,768]{2,1,0:T(8,128)(2,1)}, bf16[4,128,1024]{2,1,0:T(8,128)(2,1)}) conditional(s32[]{:T(128)} %convert_element_type.25, (bf16[4,128,1024]{2,1,0:T(8,128)(2,1)S(1)}, bf16[4,144,768]{2,1,0:T(8,128)(2,1)}) %tuple.132, (bf16[128,1024]{1,0:T(8,128)(2,1)}, bf16[128,1024]{1,0:T(8,128)(2,1)S(1)}, bf16[4096,512]{1,0:T(8,128)(2,1)}, ...), branch_computations={%region_14.15_spmd, %region_15.16_spmd} | conditional | flops 1343225856 | bytes 153354384 | solution.py:488
  273.6 1.0 branch_1_fun.40
  274.7 0.0 copy-start.20
  274.7 13.0 %all_to_all.92.refs_0_ = bf16[4,128,1024]{2,1,0:T(8,128)(2,1)} all-to-all(bf16[4,128,1024]{2,1,0:T(8,128)(2,1)S(1)} %branch_1_fun.40), channel_id=1, replica_groups=mesh['s'=4,'x'=4,'zh'=2,'y'=4,'core'=2] {'x'}, dimensions={0} | all-to-all | bytes 2097152 | tf_op jit(solution)/shard_map/cond/branch_1_fun/all_to_all | solution.py:276
  287.7 4.2 %all-to-all-start.15 = ((bf16[4,128,1024]{2,1,0:T(8,128)(2,1)}), bf16[4,128,1024]{2,1,0:T(8,128)(2,1)}, u32[]{:S(2)}, u32[]{:S(2)}) async-start(bf16[4,128,1024]{2,1,0:T(8,128)(2,1)} %all_to_all.92.refs_0_), calls=%async_computation.15 | async-start | bytes 2097152 | tf_op jit(solution)/shard_map/cond/branch_1_fun/all_to_all | solution.py:466
  292.0 8.9 %branch_1_fun.41 = bf16[4,144,768]{2,1,0:T(8,128)(2,1)} custom-call(bf16[4,128,1024]{2,1,0:T(8,128)(2,1)} %all_to_all.92.refs_0_, bf16[4,144,1024]{2,1,0:T(8,128)(2,1)} %get-tuple-element.268.refs_1_, bf16[1,4096]{1,0:T(2,128)(2,1)S(1)} %get-tuple-element.269.refs_2_, f32[128,1]{1,0:T(8,128)S(1)} %get-tuple-element.270.refs_3_, ...), custom_call_target="tpu_custom_call" | custom-call | flops 1342177280 | bytes 12582912 | tf_op jit(solution)/shard_map/cond/branch_1_fun/pallas_call | solution.py:260
  300.9 0.9 all-to-all-done.15
  301.8 13.6 %all_to_all.93.grads = bf16[4,144,768]{2,1,0:T(8,128)(2,1)S(1)} all-to-all(bf16[4,144,768]{2,1,0:T(8,128)(2,1)} %get-tuple-element.355), channel_id=1, replica_groups=mesh['s'=4,'x'=4,'zh'=2,'y'=4,'core'=2] {'y'}, dimensions={0} | all-to-all | bytes 1769472 | tf_op jit(solution)/shard_map/all_to_all | solution.py:466
  315.4 18.6 %collective-permute-start.14 = (bf16[4,144,768]{2,1,0:T(8,128)(2,1)S(1)}, bf16[4,144,768]{2,1,0:T(8,128)(2,1)}, u32[]{:S(2)}, u32[]{:S(2)}) collective-permute-start(bf16[4,144,768]{2,1,0:T(8,128)(2,1)S(1)} %all_to_all.93.grads), channel_id=1, source_target_pairs={{0,1},{1,0},{2,3},{3,2},{4,5},{5,4},{6,7},{7,6},{8,9},{9,8},{10,11... | collective-permute-start | bytes 2654216 | tf_op jit(solution)/shard_map/ppermute | solution.py:467
  334.0 0.0 collective-permute-start.13
  334.0 3.4 shard_map.103.rest_0_
  337.4 0.9 convert_reduce_fusion
  338.3 0.7 dynamic-slice_add_fusion
  339.0 4.5 %all-to-all-start.18 = ((f32[8,1,64]{2,1,0:T(1,128)}), f32[8,1,64]{2,1,0:T(1,128)S(1)}, u32[]{:S(2)}, u32[]{:S(2)}) async-start(f32[8,1,64]{2,1,0:T(1,128)} %bitcast.13), calls=%async_computation.18 | async-start | bytes 8192 | tf_op jit(solution)/shard_map/all_to_all | solution.py:503
  343.4 0.0 collective-permute-done.13.g
  343.4 4.9 %shard_map.104 = (f32[512,512]{1,0:T(8,128)}, f32[1024,128]{1,0:T(8,128)}, f32[512,512]{1,0:T(8,128)}) custom-call(s32[3]{0:T(128)S(1)} %pad_add_fusion.here, bf16[8,128,1024]{2,1,0:T(8,128)(2,1)} %get-tuple-element.327.early, bf16[8,128,1024]{2,1,0:T(8,128)(2,1)} %get-tuple-element.435.late, bf16[4,128,1024]{2,1,0:T(8,128)(2,1)} %collective-permute-done.13.g, ...), custom_call_target="tpu_custom_call" | custom-call | flops 1342177280 | bytes 12582912 | tf_op jit(solution)/shard_map/pallas_call | solution.py:260
  348.3 4.0 %all-to-all-done.18 = f32[8,1,64]{2,1,0:T(1,128)S(1)} async-done(((f32[8,1,64]{2,1,0:T(1,128)}), f32[8,1,64]{2,1,0:T(1,128)S(1)}, u32[]{:S(2)}, u32[]{:S(2)}) %all-to-all-start.18) | async-done | bytes 2080 | tf_op jit(solution)/shard_map/all_to_all | solution.py:503
  352.3 0.5 reduce_sum.49
  (31 shorter events, 0.2 us)
Async XLA Ops:
  2.3 33.1 %copy-start.10 = (bf16[1,4096,1,256]{3,1,2,0:T(8,128)(2,1)S(1)}, bf16[1,4096,1,256]{3,1,2,0:T(8,128)(2,1)}, u32[]{:S(2)}) copy-start(bf16[1,4096,1,256]{3,1,2,0:T(8,128)(2,1)} %param.27) | copy-start | bytes 6291460
  2.3 33.1 %copy-start.31 = (s32[2]{0:T(128)S(1)}, s32[2]{0:T(128)}, u32[]{:S(2)}) copy-start(s32[2]{0:T(128)} %param.24) | copy-start | bytes 28
  2.3 10.9 %collective-permute-start = (bf16[144,512]{1,0:T(8,128)(2,1)S(1)}, bf16[144,512]{1,0:T(8,128)(2,1)S(1)}, u32[]{:S(2)}, u32[]{:S(2)}) collective-permute-start(bf16[144,512]{1,0:T(8,128)(2,1)S(1)} %pad_maximum_fusion.mine), channel_id=1, source_target_pairs={{0,8},{8,0},{16,24},{24,16},{32,40},{40,32},{48,56},{56,48},{64,72... | collective-permute-start | bytes 442376 | tf_op jit(solution)/shard_map/ppermute | solution.py:335
  14.9 19.6 %all-to-all-start.16 = ((bf16[4,144,1024]{2,1,0:T(8,128)(2,1)}), bf16[4,144,1024]{2,1,0:T(8,128)(2,1)}, u32[]{:S(2)}, u32[]{:S(2)}) async-start(bf16[4,144,1024]{2,1,0:T(8,128)(2,1)} %shard_map.102), calls=%async_computation.16 | async-start | bytes 2359296 | tf_op jit(solution)/shard_map/all_to_all | solution.py:276
  42.9 15.2 %copy-start.11 = (bf16[4,144,1024]{2,1,0:T(8,128)(2,1)S(1)}, bf16[4,144,1024]{2,1,0:T(8,128)(2,1)}, u32[]{:S(2)}) copy-start(bf16[4,144,1024]{2,1,0:T(8,128)(2,1)} %get-tuple-element.166.block) | copy-start | bytes 3538948 | tf_op jit(solution)/shard_map/cond
  58.2 4.6 %collective-permute-start.2 = (bf16[128,1024]{1,0:T(8,128)(2,1)S(1)}, bf16[128,1024]{1,0:T(8,128)(2,1)S(1)}, u32[]{:S(2)}, u32[]{:S(2)}) collective-permute-start(bf16[128,1024]{1,0:T(8,128)(2,1)S(1)} %get-tuple-element.322), channel_id=1, source_target_pairs={{0,72},{8,64},{16,88},{24,80},{32,104},{40,96},{48,120},{56,112},{... | collective-permute-start | bytes 786440 | tf_op jit(solution)/shard_map/ppermute | solution.py:287
  59.6 4.6 %collective-permute-start.1 = (bf16[128,1024]{1,0:T(8,128)(2,1)S(1)}, bf16[128,1024]{1,0:T(8,128)(2,1)S(1)}, u32[]{:S(2)}, u32[]{:S(2)}) collective-permute-start(bf16[128,1024]{1,0:T(8,128)(2,1)S(1)} %get-tuple-element.322), channel_id=1, source_target_pairs={{0,64},{8,72},{16,80},{24,88},{32,96},{40,104},{48,112},{56,120},{... | collective-permute-start | bytes 786440 | tf_op jit(solution)/shard_map/ppermute | solution.py:287
  64.2 1.4 collective-permute-start.4
  64.8 0.7 collective-permute-start.3
  65.6 1.4 collective-permute-start.6
  66.3 0.7 collective-permute-start.5
  67.0 35.4 %all-to-all-start.5 = ((bf16[8,128,1024]{2,1,0:T(8,128)(2,1)}), bf16[8,128,1024]{2,1,0:T(8,128)(2,1)}, u32[]{:S(2)}, u32[]{:S(2)}) async-start(bf16[8,128,1024]{2,1,0:T(8,128)(2,1)} %param.6), calls=%async_computation.5 | async-start | bytes 4194304 | tf_op jit(solution)/shard_map/cond/branch_0_fun/all_to_all | solution.py:376
  102.4 1.4 collective-permute-start.8
  103.0 0.7 collective-permute-start.7
  106.0 0.7 copy-start.21
  106.7 1.4 collective-permute-start.10
  107.4 0.7 collective-permute-start.9
  108.1 0.7 copy-start.22
  108.8 164.7 %collective-permute-start.12 = (bf16[128,1024]{1,0:T(8,128)(2,1)}, bf16[128,1024]{1,0:T(8,128)(2,1)S(1)}, u32[]{:S(2)}, u32[]{:S(2)}) collective-permute-start(bf16[128,1024]{1,0:T(8,128)(2,1)} %copy-done.22), channel_id=1, source_target_pairs={{64,8},{72,0},{80,24},{88,16},{96,40},{104,32},{112,56},{120,48},{... | collective-permute-start | bytes 786440 | tf_op jit(solution)/shard_map/ppermute | solution.py:287
  110.1 163.4 %collective-permute-start.11 = (bf16[128,1024]{1,0:T(8,128)(2,1)}, bf16[128,1024]{1,0:T(8,128)(2,1)}, u32[]{:S(2)}, u32[]{:S(2)}) collective-permute-start(bf16[128,1024]{1,0:T(8,128)(2,1)} %copy-done.22), channel_id=1, source_target_pairs={{64,0},{72,8},{80,16},{88,24},{96,32},{104,40},{112,48},{120,56},{... | collective-permute-start | bytes 786440 | tf_op jit(solution)/shard_map/ppermute | solution.py:287
  111.4 162.2 %copy-start.15 = (bf16[4,128,1024]{2,1,0:T(8,128)(2,1)S(1)}, bf16[4,128,1024]{2,1,0:T(8,128)(2,1)}, u32[]{:S(2)}) copy-start(bf16[4,128,1024]{2,1,0:T(8,128)(2,1)} %get-tuple-element.346) | copy-start | bytes 3145732
  111.4 162.1 %copy-start.29 = (f32[128,1]{1,0:T(8,128)S(1)}, f32[128,1]{1,0:T(8,128)}, u32[]{:S(2)}) copy-start(f32[128,1]{1,0:T(8,128)} %get-tuple-element.350) | copy-start | bytes 1540
  274.7 17.3 %copy-start.20 = (f32[2,256,64]{2,1,0:T(8,128)S(1)}, f32[2,256,64]{2,1,0:T(8,128)}, u32[]{:S(2)}) copy-start(f32[2,256,64]{2,1,0:T(8,128)} %get-tuple-element.273.refs_6_) | copy-start | bytes 393220 | tf_op jit(solution)/shard_map/cond
  274.7 17.3 %copy-start.25 = (bf16[128,512]{1,0:T(8,128)(2,1)S(1)}, bf16[128,512]{1,0:T(8,128)(2,1)}, u32[]{:S(2)}) copy-start(bf16[128,512]{1,0:T(8,128)(2,1)} %get-tuple-element.271.refs_4_) | copy-start | bytes 393220 | tf_op jit(solution)/shard_map/cond
  274.7 17.3 %copy-start.30 = (bf16[128,256]{1,0:T(8,128)(2,1)S(1)}, bf16[128,256]{1,0:T(8,128)(2,1)}, u32[]{:S(2)}) copy-start(bf16[128,256]{1,0:T(8,128)(2,1)} %get-tuple-element.272.refs_5_) | copy-start | bytes 196612 | tf_op jit(solution)/shard_map/cond
  287.7 14.1 %all-to-all-start.15 = ((bf16[4,128,1024]{2,1,0:T(8,128)(2,1)}), bf16[4,128,1024]{2,1,0:T(8,128)(2,1)}, u32[]{:S(2)}, u32[]{:S(2)}) async-start(bf16[4,128,1024]{2,1,0:T(8,128)(2,1)} %all_to_all.92.refs_0_), calls=%async_computation.15 | async-start | bytes 2097152 | tf_op jit(solution)/shard_map/cond/branch_1_fun/all_to_all | solution.py:466
  315.4 22.0 %collective-permute-start.14 = (bf16[4,144,768]{2,1,0:T(8,128)(2,1)S(1)}, bf16[4,144,768]{2,1,0:T(8,128)(2,1)}, u32[]{:S(2)}, u32[]{:S(2)}) collective-permute-start(bf16[4,144,768]{2,1,0:T(8,128)(2,1)S(1)} %all_to_all.93.grads), channel_id=1, source_target_pairs={{0,1},{1,0},{2,3},{3,2},{4,5},{5,4},{6,7},{7,6},{8,9},{9,8},{10,11... | collective-permute-start | bytes 2654216 | tf_op jit(solution)/shard_map/ppermute | solution.py:467
  334.0 9.4 %collective-permute-start.13 = (bf16[4,128,1024]{2,1,0:T(8,128)(2,1)}, bf16[4,128,1024]{2,1,0:T(8,128)(2,1)}, u32[]{:S(2)}, u32[]{:S(2)}) collective-permute-start(bf16[4,128,1024]{2,1,0:T(8,128)(2,1)} %get-tuple-element.354.g), channel_id=1, source_target_pairs={{0,1},{1,0},{2,3},{3,2},{4,5},{5,4},{6,7},{7,6},{8,9},{9,8},{10,11... | collective-permute-start | bytes 3145736 | tf_op jit(solution)/shard_map/ppermute | solution.py:467
  339.0 13.4 %all-to-all-start.18 = ((f32[8,1,64]{2,1,0:T(1,128)}), f32[8,1,64]{2,1,0:T(1,128)S(1)}, u32[]{:S(2)}, u32[]{:S(2)}) async-start(f32[8,1,64]{2,1,0:T(1,128)} %bitcast.13), calls=%async_computation.18 | async-start | bytes 8192 | tf_op jit(solution)/shard_map/all_to_all | solution.py:503

commit v7 on v6

--- a/solution.py
+++ b/solution.py
@@ -500,6 +500,7 @@
         terms = terms + jnp.sum(item, (0, 1))
     small = piece // DP
     terms = lax.dynamic_slice_in_dim(terms, lax.axis_index(("y", "core")) * small, small, 1)
+    terms, own = lax.optimization_barrier((terms, own))
     gain_grad = jnp.sum(lax.all_to_all(terms.reshape(DP, 1, small), ("x", "zh"), 0, 0), 0)
     everything = piece + qs + kvs
     scratch = [

time: 354 us -> 358 us (1.011)
  starting transfers between devices: 59.2 us -> 65.4 us
    ppermute x12, starting transfers between devices: 10.6 us -> 14.8 us  [hop(): got.append(lax.ppermute(block, ('s', 'x', 'zh'), route))]
  transfers between devices with their start and end apart: 19 -> 19, of which waited for: 8 -> 10; matrix products, arithmetic and copies ran while one was open for 0% -> 0% of each run, Pallas kernels for 5% -> 5%
where the time goes in v7:
time: 358 us
  waiting for transfers between devices  216 us (60%)
  starting transfers between devices  65.4 us (18%)
  blocking collectives  40.4 us (11%)
  Pallas kernels  27.5 us (8%)
  local copies, waits for them, and re-layouts  3.96 us (1%)
    ppermute x12, waiting for transfers between devices, hop(): got.append(lax.ppermute(block, ('s', 'x', 'zh'), route))  166 us
    all_to_all x2, blocking collectives, gather_x(): return lax.all_to_all(spread, 'x', 0, 0)  28 us
    pallas_call x7, Pallas kernels, call(): pl.pallas_call(kernel, out_shape=[out for out, _ in outs], in_specs=ins,...  27.5 us
    all_to_all x1, waiting for transfers between devices, shards(): over_dp = lambda v: lax.all_to_all(v, ('y', 'core'), 0, 0)  26.4 us
    ppermute x2, starting transfers between devices, shards(): swap = lambda v: lax.ppermute(v, 'core', [(0, 1), (1, 0)])  20.4 us
    all_to_all x1, waiting for transfers between devices, gather_x(): return lax.all_to_all(spread, 'x', 0, 0)  15 us
    ppermute x12, starting transfers between devices, hop(): got.append(lax.ppermute(block, ('s', 'x', 'zh'), route))  14.8 us
    all_to_all x1, blocking collectives, shards(): over_y = lambda v: lax.all_to_all(v, 'y', 0, 0)  12.3 us
  transfers between devices with their start and end apart: 19, of which 10 were waited for; matrix products, arithmetic and copies ran while one was open for 0% of the time, Pallas kernels for 5%

profile of v7, /device:TPU:1, one launch (start us, length us, event | category | flops | bytes accessed | tf_op | source)
XLA Modules:
  0.0 357.5 jit_solution(13179605386248756092)
XLA Ops:
  0.6 0.7 reduce.5
  1.3 0.9 broadcast_select_fusion
  2.3 0.0 copy-start.10
  2.3 0.0 copy-start.31
  2.3 7.8 %collective-permute-start = (bf16[144,512]{1,0:T(8,128)(2,1)S(1)}, bf16[144,512]{1,0:T(8,128)(2,1)S(1)}, u32[]{:S(2)}, u32[]{:S(2)}) collective-permute-start(bf16[144,512]{1,0:T(8,128)(2,1)S(1)} %pad_maximum_fusion.mine), channel_id=1, source_target_pairs={{0,8},{8,0},{16,24},{24,16},{32,40},{40,32},{48,56},{56,48},{64,72... | collective-permute-start | bytes 442376 | tf_op jit(solution)/shard_map/ppermute | solution.py:335
  10.2 0.1 pad_add_fusion.here
  10.2 3.0 collective-permute-done.other
  13.2 1.7 shard_map.102
  14.9 4.7 %all-to-all-start.16 = ((bf16[4,144,1024]{2,1,0:T(8,128)(2,1)}), bf16[4,144,1024]{2,1,0:T(8,128)(2,1)}, u32[]{:S(2)}, u32[]{:S(2)}) async-start(bf16[4,144,1024]{2,1,0:T(8,128)(2,1)} %shard_map.102), calls=%async_computation.16 | async-start | bytes 2359296 | tf_op jit(solution)/shard_map/all_to_all | solution.py:276
  19.6 15.0 %all-to-all-done.16 = bf16[4,144,1024]{2,1,0:T(8,128)(2,1)} async-done(((bf16[4,144,1024]{2,1,0:T(8,128)(2,1)}), bf16[4,144,1024]{2,1,0:T(8,128)(2,1)}, u32[]{:S(2)}, u32[]{:S(2)}) %all-to-all-start.16) | async-done | bytes 1179680 | tf_op jit(solution)/shard_map/all_to_all | solution.py:276
  34.6 0.9 slice.13
  35.5 23.5 %conditional.8 = (bf16[128,1024]{1,0:T(8,128)(2,1)}, f32[128,1]{1,0:T(8,128)}, bf16[128,512]{1,0:T(8,128)(2,1)}, bf16[128,256]{1,0:T(8,128)(2,1)}, f32[2,256,64]{2,1,0:T(8,128)}, /*index=5*/bf16[8,128,1024]{2,1,0:T(8,128)(2,1)}) conditional(s32[]{:T(128)} %convert_element_type.25, () %tuple.79, (s32[2]{0:T(128)S(1)}, bf16[4,144,1024]{2,1,0:T(8,128)(2,1)}, ...), branch_computations={%region_0.1_spmd, %region_1.2_spmd} | conditional | flops 1343225856 | bytes 27263024 | solution.py:445
  35.5 7.5 %branch_1_fun.21 = (bf16[4,128,1024]{2,1,0:T(8,128)(2,1)S(1)}, bf16[8,128,1024]{2,1,0:T(8,128)(2,1)}, f32[128,1]{1,0:T(8,128)}, bf16[128,512]{1,0:T(8,128)(2,1)}...) custom-call(s32[2]{0:T(128)S(1)} %get-tuple-element.159.refs_0_, bf16[4,144,1024]{2,1,0:T(8,128)(2,1)} %get-tuple-element.160.refs_1_, ...), custom_call_target="tpu_custom_call" | custom-call | flops 1342177280 | bytes 12582912 | tf_op jit(solution)/shard_map/cond/branch_1_fun/pallas_call | solution.py:260
  43.0 15.0 %all_to_all.79.sums = bf16[4,128,1024]{2,1,0:T(8,128)(2,1)S(1)} all-to-all(bf16[4,128,1024]{2,1,0:T(8,128)(2,1)S(1)} %get-tuple-element.165), channel_id=1, replica_groups=mesh['s'=4,'x'=4,'zh'=2,'y'=4,'core'=2] {'x'}, dimensions={0} | all-to-all | bytes 2097152 | tf_op jit(solution)/shard_map/cond/branch_1_fun/all_to_all | solution.py:276
  58.1 0.9 branch_1_fun.22
  58.9 2.0 collective-permute-start.2
  61.0 2.0 collective-permute-start.1
  62.9 0.9 collective-permute-done.2
  63.8 2.0 collective-permute-done.1
  65.9 1.4 collective-permute-start.4
  67.2 1.3 collective-permute-start.3
  68.6 0.0 collective-permute-done.4
  68.6 0.0 collective-permute-done.3
  68.6 1.4 collective-permute-start.6
  70.0 1.4 collective-permute-start.5
  71.4 0.0 collective-permute-done.6
  71.4 0.0 collective-permute-done.5
  71.4 35.4 %conditional.11 = (bf16[128,1024]{1,0:T(8,128)(2,1)}, bf16[4,144,768]{2,1,0:T(8,128)(2,1)}, bf16[8,128,1024]{2,1,0:T(8,128)(2,1)}, bf16[8,128,1024]{2,1,0:T(8,128)(2,1)}) conditional(s32[]{:T(128)} %convert_element_type.22, bf16[8,128,1024]{2,1,0:T(8,128)(2,1)} %get-tuple-element.327, (bf16[128,1024]{1,0:T(8,128)(2,1)}, bf16[128,1024]{1,0:T(8,128)(2,1)}, ...), branch_computations={%region_6.7_spmd, %region_7.8_spmd} | conditional | flops 2686451712 | bytes 209715296 | solution.py:461
  71.4 8.9 %all-to-all-start.5 = ((bf16[8,128,1024]{2,1,0:T(8,128)(2,1)}), bf16[8,128,1024]{2,1,0:T(8,128)(2,1)}, u32[]{:S(2)}, u32[]{:S(2)}) async-start(bf16[8,128,1024]{2,1,0:T(8,128)(2,1)} %param.6), calls=%async_computation.5 | async-start | bytes 4194304 | tf_op jit(solution)/shard_map/cond/branch_0_fun/all_to_all | solution.py:376
  80.3 26.4 %all-to-all-done.5 = bf16[8,128,1024]{2,1,0:T(8,128)(2,1)} async-done(((bf16[8,128,1024]{2,1,0:T(8,128)(2,1)}), bf16[8,128,1024]{2,1,0:T(8,128)(2,1)}, u32[]{:S(2)}, u32[]{:S(2)}) %all-to-all-start.5) | async-done | bytes 2097184 | tf_op jit(solution)/shard_map/cond/branch_0_fun/all_to_all | solution.py:376
  106.7 0.7 collective-permute-start.8
  107.4 0.7 collective-permute-start.7
  108.1 0.0 collective-permute-done.8
  108.1 0.0 collective-permute-done.7
  108.1 2.4 conditional.13
  108.1 2.4 slice.9
  110.5 0.7 copy-done.23
  111.2 0.7 collective-permute-start.10
  111.9 0.7 collective-permute-start.9
  112.6 0.0 collective-permute-done.10
  112.6 0.0 collective-permute-done.9
  112.6 1.3 collective-permute-start.12
  113.9 1.3 collective-permute-start.11
  115.3 163.0 %collective-permute-done.12 = bf16[128,1024]{1,0:T(8,128)(2,1)} collective-permute-done((bf16[128,1024]{1,0:T(8,128)(2,1)}, bf16[128,1024]{1,0:T(8,128)(2,1)}, u32[]{:S(2)}, u32[]{:S(2)}) %collective-permute-start.12) | collective-permute-done | bytes 262176 | tf_op jit(solution)/shard_map/ppermute | solution.py:287
  278.3 0.3 collective-permute-done.11
  278.6 0.0 copy-done.15
  278.6 0.0 copy-done.29
  278.6 28.7 %conditional.15 = (bf16[4,144,768]{2,1,0:T(8,128)(2,1)}, bf16[4,128,1024]{2,1,0:T(8,128)(2,1)}) conditional(s32[]{:T(128)} %convert_element_type.25, (bf16[4,128,1024]{2,1,0:T(8,128)(2,1)S(1)}, bf16[4,144,768]{2,1,0:T(8,128)(2,1)}) %tuple.136, (bf16[128,1024]{1,0:T(8,128)(2,1)}, bf16[128,1024]{1,0:T(8,128)(2,1)}, bf16[4096,512]{1,0:T(8,128)(2,1)}, ...), branch_computations={%region_14.15_spmd, %region_15.16_spmd} | conditional | flops 1343225856 | bytes 152567888 | solution.py:488
  278.6 1.1 branch_1_fun.40
  279.7 13.0 %all_to_all.92.refs_0_ = bf16[4,128,1024]{2,1,0:T(8,128)(2,1)} all-to-all(bf16[4,128,1024]{2,1,0:T(8,128)(2,1)S(1)} %branch_1_fun.40), channel_id=1, replica_groups=mesh['s'=4,'x'=4,'zh'=2,'y'=4,'core'=2] {'x'}, dimensions={0} | all-to-all | bytes 2097152 | tf_op jit(solution)/shard_map/cond/branch_1_fun/all_to_all | solution.py:276
  292.7 4.7 %all-to-all-start.15 = ((bf16[4,128,1024]{2,1,0:T(8,128)(2,1)}), bf16[4,128,1024]{2,1,0:T(8,128)(2,1)}, u32[]{:S(2)}, u32[]{:S(2)}) async-start(bf16[4,128,1024]{2,1,0:T(8,128)(2,1)} %all_to_all.92.refs_0_), calls=%async_computation.15 | async-start | bytes 2097152 | tf_op jit(solution)/shard_map/cond/branch_1_fun/all_to_all | solution.py:466
  297.4 8.9 %branch_1_fun.41 = bf16[4,144,768]{2,1,0:T(8,128)(2,1)} custom-call(bf16[4,128,1024]{2,1,0:T(8,128)(2,1)} %all_to_all.92.refs_0_, bf16[4,144,1024]{2,1,0:T(8,128)(2,1)} %get-tuple-element.268.refs_1_, bf16[1,4096]{1,0:T(2,128)(2,1)S(1)} %get-tuple-element.269.refs_2_, f32[128,1]{1,0:T(8,128)S(1)} %get-tuple-element.270.refs_3_, ...), custom_call_target="tpu_custom_call" | custom-call | flops 1342177280 | bytes 12582912 | tf_op jit(solution)/shard_map/cond/branch_1_fun/pallas_call | solution.py:260
  306.3 1.0 all-to-all-done.15
  307.3 12.3 %all_to_all.93.grads = bf16[4,144,768]{2,1,0:T(8,128)(2,1)S(1)} all-to-all(bf16[4,144,768]{2,1,0:T(8,128)(2,1)} %get-tuple-element.357), channel_id=1, replica_groups=mesh['s'=4,'x'=4,'zh'=2,'y'=4,'core'=2] {'y'}, dimensions={0} | all-to-all | bytes 1769472 | tf_op jit(solution)/shard_map/all_to_all | solution.py:466
  319.6 20.4 %collective-permute-start.14 = (bf16[4,144,768]{2,1,0:T(8,128)(2,1)S(1)}, bf16[4,144,768]{2,1,0:T(8,128)(2,1)S(1)}, u32[]{:S(2)}, u32[]{:S(2)}) collective-permute-start(bf16[4,144,768]{2,1,0:T(8,128)(2,1)S(1)} %all_to_all.93.grads), channel_id=1, source_target_pairs={{0,1},{1,0},{2,3},{3,2},{4,5},{5,4},{6,7},{7,6},{8,9},{9,8},{10,11... | collective-permute-start | bytes 2654216 | tf_op jit(solution)/shard_map/ppermute | solution.py:467
  340.0 0.0 collective-permute-start.13
  340.1 3.2 collective-permute-done.14.grads
  343.3 0.7 dynamic-slice_add_fusion
  344.0 4.1 %all-to-all-start.18 = ((f32[8,1,64]{2,1,0:T(1,128)}), f32[8,1,64]{2,1,0:T(1,128)S(1)}, u32[]{:S(2)}, u32[]{:S(2)}) async-start(f32[8,1,64]{2,1,0:T(1,128)} %bitcast.14), calls=%async_computation.18 | async-start | bytes 8192 | tf_op jit(solution)/shard_map/all_to_all | solution.py:504
  348.1 3.5 shard_map.103.rest_0_
  351.6 0.0 collective-permute-done.13.g
  351.7 3.9 %shard_map.104 = (f32[512,512]{1,0:T(8,128)}, f32[1024,128]{1,0:T(8,128)}, f32[512,512]{1,0:T(8,128)}) custom-call(s32[3]{0:T(128)S(1)} %pad_add_fusion.here, bf16[8,128,1024]{2,1,0:T(8,128)(2,1)} %get-tuple-element.329.early, bf16[8,128,1024]{2,1,0:T(8,128)(2,1)S(1)} %copy-done.11, bf16[4,128,1024]{2,1,0:T(8,128)(2,1)S(1)} %collective-permute-done.13.g, ...), custom_call_target="tpu_custom_call" | custom-call | flops 1342177280 | bytes 12582912 | tf_op jit(solution)/shard_map/pallas_call | solution.py:260
  355.6 1.4 all-to-all-done.18
  357.0 0.5 reduce_sum.49
  (31 shorter events, 0.1 us)
Async XLA Ops:
  2.3 33.2 %copy-start.10 = (bf16[1,4096,1,256]{3,1,2,0:T(8,128)(2,1)S(1)}, bf16[1,4096,1,256]{3,1,2,0:T(8,128)(2,1)}, u32[]{:S(2)}) copy-start(bf16[1,4096,1,256]{3,1,2,0:T(8,128)(2,1)} %param.27) | copy-start | bytes 6291460
  2.3 33.2 %copy-start.31 = (s32[2]{0:T(128)S(1)}, s32[2]{0:T(128)}, u32[]{:S(2)}) copy-start(s32[2]{0:T(128)} %param.24) | copy-start | bytes 28
  2.3 10.9 %collective-permute-start = (bf16[144,512]{1,0:T(8,128)(2,1)S(1)}, bf16[144,512]{1,0:T(8,128)(2,1)S(1)}, u32[]{:S(2)}, u32[]{:S(2)}) collective-permute-start(bf16[144,512]{1,0:T(8,128)(2,1)S(1)} %pad_maximum_fusion.mine), channel_id=1, source_target_pairs={{0,8},{8,0},{16,24},{24,16},{32,40},{40,32},{48,56},{56,48},{64,72... | collective-permute-start | bytes 442376 | tf_op jit(solution)/shard_map/ppermute | solution.py:335
  14.9 20.6 %copy-start.12 = (bf16[4,144,1024]{2,1,0:T(8,128)(2,1)S(1)}, bf16[4,144,1024]{2,1,0:T(8,128)(2,1)}, u32[]{:S(2)}) copy-start(bf16[4,144,1024]{2,1,0:T(8,128)(2,1)} %shard_map.102) | copy-start | bytes 3538948
  14.9 19.7 %all-to-all-start.16 = ((bf16[4,144,1024]{2,1,0:T(8,128)(2,1)}), bf16[4,144,1024]{2,1,0:T(8,128)(2,1)}, u32[]{:S(2)}, u32[]{:S(2)}) async-start(bf16[4,144,1024]{2,1,0:T(8,128)(2,1)} %shard_map.102), calls=%async_computation.16 | async-start | bytes 2359296 | tf_op jit(solution)/shard_map/all_to_all | solution.py:276
  58.9 4.9 %collective-permute-start.2 = (bf16[128,1024]{1,0:T(8,128)(2,1)}, bf16[128,1024]{1,0:T(8,128)(2,1)}, u32[]{:S(2)}, u32[]{:S(2)}) collective-permute-start(bf16[128,1024]{1,0:T(8,128)(2,1)} %get-tuple-element.324), channel_id=1, source_target_pairs={{0,72},{8,64},{16,88},{24,80},{32,104},{40,96},{48,120},{56,112},{... | collective-permute-start | bytes 786440 | tf_op jit(solution)/shard_map/ppermute | solution.py:287
  61.0 4.9 %collective-permute-start.1 = (bf16[128,1024]{1,0:T(8,128)(2,1)}, bf16[128,1024]{1,0:T(8,128)(2,1)}, u32[]{:S(2)}, u32[]{:S(2)}) collective-permute-start(bf16[128,1024]{1,0:T(8,128)(2,1)} %get-tuple-element.324), channel_id=1, source_target_pairs={{0,64},{8,72},{16,80},{24,88},{32,96},{40,104},{48,112},{56,120},{... | collective-permute-start | bytes 786440 | tf_op jit(solution)/shard_map/ppermute | solution.py:287
  65.9 2.7 collective-permute-start.4
  67.2 1.4 collective-permute-start.3
  68.6 2.8 collective-permute-start.6
  70.0 1.4 collective-permute-start.5
  71.4 35.4 %all-to-all-start.5 = ((bf16[8,128,1024]{2,1,0:T(8,128)(2,1)}), bf16[8,128,1024]{2,1,0:T(8,128)(2,1)}, u32[]{:S(2)}, u32[]{:S(2)}) async-start(bf16[8,128,1024]{2,1,0:T(8,128)(2,1)} %param.6), calls=%async_computation.5 | async-start | bytes 4194304 | tf_op jit(solution)/shard_map/cond/branch_0_fun/all_to_all | solution.py:376
  106.7 1.4 collective-permute-start.8
  107.4 0.7 collective-permute-start.7
  110.5 0.7 copy-start.23
  111.2 1.4 collective-permute-start.10
  111.9 0.7 collective-permute-start.9
  112.6 165.7 %collective-permute-start.12 = (bf16[128,1024]{1,0:T(8,128)(2,1)}, bf16[128,1024]{1,0:T(8,128)(2,1)}, u32[]{:S(2)}, u32[]{:S(2)}) collective-permute-start(bf16[128,1024]{1,0:T(8,128)(2,1)} %get-tuple-element.346), channel_id=1, source_target_pairs={{64,8},{72,0},{80,24},{88,16},{96,40},{104,32},{112,56},{120,48},{... | collective-permute-start | bytes 786440 | tf_op jit(solution)/shard_map/ppermute | solution.py:287
  113.9 164.7 %collective-permute-start.11 = (bf16[128,1024]{1,0:T(8,128)(2,1)}, bf16[128,1024]{1,0:T(8,128)(2,1)}, u32[]{:S(2)}, u32[]{:S(2)}) collective-permute-start(bf16[128,1024]{1,0:T(8,128)(2,1)} %get-tuple-element.346), channel_id=1, source_target_pairs={{64,0},{72,8},{80,16},{88,24},{96,32},{104,40},{112,48},{120,56},{... | collective-permute-start | bytes 786440 | tf_op jit(solution)/shard_map/ppermute | solution.py:287
  115.2 163.4 %copy-start.15 = (bf16[4,128,1024]{2,1,0:T(8,128)(2,1)S(1)}, bf16[4,128,1024]{2,1,0:T(8,128)(2,1)}, u32[]{:S(2)}) copy-start(bf16[4,128,1024]{2,1,0:T(8,128)(2,1)} %get-tuple-element.348) | copy-start | bytes 3145732
  115.2 163.3 %copy-start.25 = (bf16[128,512]{1,0:T(8,128)(2,1)S(1)}, bf16[128,512]{1,0:T(8,128)(2,1)}, u32[]{:S(2)}) copy-start(bf16[128,512]{1,0:T(8,128)(2,1)} %get-tuple-element.353) | copy-start | bytes 393220
  115.2 163.3 %copy-start.29 = (f32[128,1]{1,0:T(8,128)S(1)}, f32[128,1]{1,0:T(8,128)}, u32[]{:S(2)}) copy-start(f32[128,1]{1,0:T(8,128)} %get-tuple-element.352) | copy-start | bytes 1540
  115.3 163.3 %copy-start.30 = (bf16[128,256]{1,0:T(8,128)(2,1)S(1)}, bf16[128,256]{1,0:T(8,128)(2,1)}, u32[]{:S(2)}) copy-start(bf16[128,256]{1,0:T(8,128)(2,1)} %get-tuple-element.354) | copy-start | bytes 196612
  279.7 17.7 %copy-start.22 = (f32[2,256,64]{2,1,0:T(8,128)S(1)}, f32[2,256,64]{2,1,0:T(8,128)}, u32[]{:S(2)}) copy-start(f32[2,256,64]{2,1,0:T(8,128)} %get-tuple-element.273.refs_6_) | copy-start | bytes 393220 | tf_op jit(solution)/shard_map/cond
  292.7 14.5 %all-to-all-start.15 = ((bf16[4,128,1024]{2,1,0:T(8,128)(2,1)}), bf16[4,128,1024]{2,1,0:T(8,128)(2,1)}, u32[]{:S(2)}, u32[]{:S(2)}) async-start(bf16[4,128,1024]{2,1,0:T(8,128)(2,1)} %all_to_all.92.refs_0_), calls=%async_computation.15 | async-start | bytes 2097152 | tf_op jit(solution)/shard_map/cond/branch_1_fun/all_to_all | solution.py:466
  319.6 23.7 %collective-permute-start.14 = (bf16[4,144,768]{2,1,0:T(8,128)(2,1)S(1)}, bf16[4,144,768]{2,1,0:T(8,128)(2,1)S(1)}, u32[]{:S(2)}, u32[]{:S(2)}) collective-permute-start(bf16[4,144,768]{2,1,0:T(8,128)(2,1)S(1)} %all_to_all.93.grads), channel_id=1, source_target_pairs={{0,1},{1,0},{2,3},{3,2},{4,5},{5,4},{6,7},{7,6},{8,9},{9,8},{10,11... | collective-permute-start | bytes 2654216 | tf_op jit(solution)/shard_map/ppermute | solution.py:467
  340.0 11.6 %collective-permute-start.13 = (bf16[4,128,1024]{2,1,0:T(8,128)(2,1)}, bf16[4,128,1024]{2,1,0:T(8,128)(2,1)S(1)}, u32[]{:S(2)}, u32[]{:S(2)}) collective-permute-start(bf16[4,128,1024]{2,1,0:T(8,128)(2,1)} %get-tuple-element.356.g), channel_id=1, source_target_pairs={{0,1},{1,0},{2,3},{3,2},{4,5},{5,4},{6,7},{7,6},{8,9},{9,8},{10,11... | collective-permute-start | bytes 3145736 | tf_op jit(solution)/shard_map/ppermute | solution.py:467
  344.0 13.0 %all-to-all-start.18 = ((f32[8,1,64]{2,1,0:T(1,128)}), f32[8,1,64]{2,1,0:T(1,128)S(1)}, u32[]{:S(2)}, u32[]{:S(2)}) async-start(f32[8,1,64]{2,1,0:T(1,128)} %bitcast.14), calls=%async_computation.18 | async-start | bytes 8192 | tf_op jit(solution)/shard_map/all_to_all | solution.py:504
  348.1 3.6 copy-start.11
